TPU v7x, 32 devices: a whole 2x2x4 slice. The times are simulated.
32 devices in a mesh: probe: 2 (over x), space: 16 (over z, y, core).
Axes of the slice: x: 2, y: 2, z: 4, core: 2. Of those that a mesh axis runs over, the one named last changes fastest.
Arguments:
- field_before: float32 [2, 64, 256, 256], P('probe', 'space'), may hold values from -6 to 6
- field_now: float32 [2, 64, 256, 256], P('probe', 'space'), may hold values from -6 to 6
- stiffness: float32 [64, 256, 256], P('space'), may hold values from 0.04 to 0.1
- buoyancy: float32 [64, 256, 256], P('space'), may hold values from 0.6 to 1.4
- perturbation: float32 [2, 64, 256, 256], P('probe', 'space'), may hold values from -0.25 to 0.25
Outputs:
- field_after: float32 [2, 64, 256, 256], P('probe', 'space')
All inputs are finite; a program needn't handle non-finite values.
Results may differ from a plain program's by a relative error of at most 0.00002.
Values sent between devices are 32-bit elements; how exact they have to be, the bound alone decides.
No kernel may reach another device: no remote copies, remote signals or barrier semaphores. Data moves between devices by JAX's collectives and lax.ppermute only.
A program may use at most 128 MiB of HBM per device.

v0:
```python
import jax
import jax.numpy as jnp
from jax import lax
from jax.sharding import PartitionSpec as P

STEPS = 2


second_coeffs = (8.0 / 5.0, -1.0 / 5.0, 8.0 / 315.0, -1.0 / 560.0)
first_coeffs = (4.0 / 5.0, -1.0 / 5.0, 4.0 / 105.0, -1.0 / 280.0)
centre_coeff = -205.0 / 72.0


def with_halo(block, sides, width):
    for axis, dim in sides:
        count = lax.axis_size(axis)
        forward = [(i, i + 1) for i in range(count - 1)]
        backward = [(target, source) for source, target in forward]
        low = lax.ppermute(
            lax.slice_in_dim(block, block.shape[dim] - width, None, axis=dim), axis, forward
        )
        high = lax.ppermute(lax.slice_in_dim(block, 0, width, axis=dim), axis, backward)
        block = jnp.concatenate([low, block, high], axis=dim)
    return block


def spread(block, axis, owner):
    block = jnp.where(lax.axis_index(axis) == owner, block, jnp.zeros_like(block))
    return lax.psum(block, axis)


def shifted(padded, direction, offset):
    window = [
        slice(4, padded.shape[0] - 4),
        slice(4, padded.shape[1] - 4),
        slice(4, padded.shape[2] - 4),
    ]
    window[direction] = slice(4 + offset, padded.shape[direction] - 4 + offset)
    return padded[tuple(window)]


def second_sum(padded):
    total = 3.0 * centre_coeff * shifted(padded, 0, 0)
    for direction in range(3):
        for reach in range(1, 5):
            total = total + second_coeffs[reach - 1] * (
                shifted(padded, direction, reach) + shifted(padded, direction, -reach)
            )
    return total


def first_parts(padded):
    parts = []
    for direction in range(3):
        total = jnp.zeros_like(shifted(padded, 0, 0))
        for reach in range(1, 5):
            total = total + first_coeffs[reach - 1] * (
                shifted(padded, direction, reach) - shifted(padded, direction, -reach)
            )
        parts.append(total)
    return parts


def pad_sides(extended):
    return jnp.pad(extended, ((0, 0), (4, 4), (4, 4)))


def divergence(padded, buoyancy, slope):
    grads = first_parts(padded)
    return (
        buoyancy * second_sum(padded)
        + slope[0] * grads[0]
        + slope[1] * grads[1]
        + slope[2] * grads[2]
    )


def on_device(field_before, field_now, stiffness, buoyancy, perturbation):
    rim = with_halo(buoyancy - 1.0, (("space", 0),), 4)
    slope = first_parts(pad_sides(rim))
    born_flag = (lax.axis_index("probe") > 0).astype(jnp.float32)
    source_scale = born_flag * perturbation[0]

    def operate(extended):
        return divergence(pad_sides(extended), buoyancy, slope)

    before = field_before[0]
    now = field_now[0]
    for step in range(STEPS):
        base = spread(now, "probe", 0)
        both = with_halo(jnp.stack([base, now]), (("space", 1),), 4)
        base_term = operate(both[0])
        own_term = operate(both[1])
        following = 2.0 * now - before + stiffness * own_term + source_scale * base_term
        before, now = (now, following)
    return now[None]


def solution(mesh):
    placed = (
        P("probe", "space", None, None),
        P("probe", "space", None, None),
        P("space", None, None),
        P("space", None, None),
        P("probe", "space", None, None),
    )
    return jax.shard_map(
        on_device,
        mesh=mesh,
        in_specs=placed,
        out_specs=P("probe", "space", None, None),
        check_vma=False,
    )
```

profile of v0, /device:TPU:4, one launch (start us, length us, event | category | flops | bytes accessed | tf_op | source)
XLA Modules:
  0.0 316.2 jit_solution(4905952962133589606)
XLA Ops:
  6.5 0.0 copy-start.4
  6.5 0.0 all-reduce.8.cloned.1.call-start
  6.5 2.4 bitcast_select_fusion
  8.9 0.0 all-reduce.8.cloned.1.call-update
  8.9 0.0 all-reduce.10.cloned.1.call-start
  9.0 41.9 %all-reduce.8.cloned.1.call-done = f32[4,256,256]{2,1,0:T(8,128)} async-done(((f32[4,256,256]{2,1,0:T(8,128)}), f32[4,256,256]{2,1,0:T(8,128)}) %all-reduce.8.cloned.1.call-update) | async-done | bytes 1048592 | tf_op jit(solution)/shard_map/psum | solution.py:29
  50.9 3.0 pad_maximum_fusion.4
  54.0 1.9 collective-permute-start.1
  55.9 3.6 %collective-permute-start = (f32[2,4,256,256]{3,2,1,0:T(8,128)}, f32[2,4,256,256]{3,2,1,0:T(8,128)}, u32[]{:S(2)}, u32[]{:S(2)}) collective-permute-start(f32[2,4,256,256]{3,2,1,0:T(8,128)} %pad_maximum_fusion.4), channel_id=1, source_target_pairs={{1,0},{2,1},{3,2},{4,3},{5,4},{6,5},{7,6},{8,7},{9,8},{10,9},{11,1... | collective-permute-start | bytes 6291464 | tf_op jit(solution)/shard_map/ppermute | solution.py:22
  59.5 0.0 copy-done.4
  59.5 1.1 broadcast_add_fusion
  60.6 0.0 copy-start
  60.6 2.0 collective-permute-start.3
  62.6 3.6 %collective-permute-start.2 = (f32[4,256,256]{2,1,0:T(8,128)}, f32[4,256,256]{2,1,0:T(8,128)}, u32[]{:S(2)}, u32[]{:S(2)}) collective-permute-start(f32[4,256,256]{2,1,0:T(8,128)} %broadcast_add_fusion), channel_id=1, source_target_pairs={{1,0},{2,1},{3,2},{4,3},{5,4},{6,5},{7,6},{8,7},{9,8},{10,9},{11,1... | collective-permute-start | bytes 3145736 | tf_op jit(solution)/shard_map/ppermute | solution.py:22
  66.3 0.0 copy-start.2
  66.3 60.2 %collective-permute-done.3 = f32[4,256,256]{2,1,0:T(8,128)} collective-permute-done((f32[4,256,256]{2,1,0:T(8,128)}, f32[4,256,256]{2,1,0:T(8,128)}, u32[]{:S(2)}, u32[]{:S(2)}) %collective-permute-start.3) | collective-permute-done | bytes 1048608 | tf_op jit(solution)/shard_map/ppermute | solution.py:19
  126.6 0.0 collective-permute-done.2
  126.6 5.4 %select_maximum_fusion = f32[12,264,264]{2,1,0:T(8,128)} fusion(f32[4,256,256]{2,1,0:T(8,128)} %collective-permute-done.2, f32[4,256,256]{2,1,0:T(8,128)} %broadcast_add_fusion, f32[4,256,256]{2,1,0:T(8,128)} %collective-permute-done.3), kind=kLoop, calls=%fused_computation.70 | loop fusion | flops 12545280 | bytes 6491136 | tf_op jit(solution)/shard_map/concatenate | solution.py:23
  131.9 0.0 collective-permute-done.1
  131.9 0.0 copy-start.1
  131.9 0.0 collective-permute-done
  131.9 0.0 copy-done
  131.9 0.0 copy-done.2
  131.9 2.7 pad_maximum_fusion
  134.7 3.2 %slice_bitcast_fusion.3 = (f32[12,256,256]{2,1,0:T(8,128)}, f32[12,256,256]{2,1,0:T(8,128)}) fusion(f32[2,12,256,256]{3,2,1,0:T(8,128)S(1)} %pad_maximum_fusion), kind=kLoop, calls=%fused_computation.82 | loop fusion | bytes 12582912 | tf_op jit(solution)/shard_map/squeeze | solution.py:93
  137.9 0.0 copy-done.1
  137.9 5.0 %pad_maximum_fusion.2 = (f32[2,8,256,256]{3,2,1,0:T(8,128)}, f32[2,8,256,256]{3,2,1,0:T(8,128)}) fusion(f32[2,4,256,256]{3,2,1,0:T(8,128)} %collective-permute-done, f32[1,4,256,256]{3,2,1,0:T(8,128)S(1)} %copy-done, f32[1,4,256,256]{3,2,1,0:T(8,128)S(1)} %bitcast.239, f32[2,4,256,256]{3,2,1,0:T(8,128)S(1)} %collective-permute-done.1), kind=kLoop, calls=%fused_computation.75 | loop fusion | flops 4194304 | bytes 14680064 | tf_op jit(solution)/shard_map/concatenate | solution.py:23
  142.9 45.2 %broadcast_select_fusion = (f32[4,256,256]{2,1,0:T(8,128)}, f32[4,256,256]{2,1,0:T(8,128)S(1)}, f32[4,256,256]{2,1,0:T(8,128)}, f32[4,256,256]{2,1,0:T(8,128)}, f32[4,256,256]{2,1,0:T(8,128)}) fusion(pred[]{:T(512)S(6)} %eq.4, f32[4,256,256]{2,1,0:T(8,128)} %param.8, f32[12,256,256]{2,1,0:T(8,128)} %get-tuple-element.13, f32[2,4,256,256]{3,2,1,0:T(8,128)} %copy-done.1, ...), kind=kLoop, calls=%fused_computation.213 | loop fusion | flops 52690944 | bytes 54525956 | tf_op jit(solution)/shard_map/jit(_where)/select_n | solution.py:28
  188.1 0.0 all-reduce.10.cloned.1.call-update
  188.2 39.6 %all-reduce.10.cloned.1.call-done = f32[4,256,256]{2,1,0:T(8,128)} async-done(((f32[4,256,256]{2,1,0:T(8,128)}), f32[4,256,256]{2,1,0:T(8,128)}) %all-reduce.10.cloned.1.call-update) | async-done | bytes 1048592 | tf_op jit(solution)/shard_map/psum | solution.py:29
  227.8 0.0 copy-start.3
  227.8 1.4 pad_maximum_fusion.5
  229.3 1.9 collective-permute-start.5
  231.2 3.8 %collective-permute-start.4 = (f32[2,4,256,256]{3,2,1,0:T(8,128)S(1)}, f32[2,4,256,256]{3,2,1,0:T(8,128)S(1)}, u32[]{:S(2)}, u32[]{:S(2)}) collective-permute-start(f32[2,4,256,256]{3,2,1,0:T(8,128)S(1)} %pad_maximum_fusion.5), channel_id=1, source_target_pairs={{1,0},{2,1},{3,2},{4,3},{5,4},{6,5},{7,6},{8,7},{9,8},{10,9},{11,1... | collective-permute-start | bytes 6291464 | tf_op jit(solution)/shard_map/ppermute | solution.py:22
  235.0 44.1 %collective-permute-done.5 = f32[2,4,256,256]{3,2,1,0:T(8,128)S(1)} collective-permute-done((f32[2,4,256,256]{3,2,1,0:T(8,128)S(1)}, f32[2,4,256,256]{3,2,1,0:T(8,128)S(1)}, u32[]{:S(2)}, u32[]{:S(2)}) %collective-permute-start.5) | collective-permute-done | bytes 2097184 | tf_op jit(solution)/shard_map/ppermute | solution.py:19
  279.1 0.0 collective-permute-done.4
  279.1 0.0 copy-done.3
  279.1 0.5 pad_maximum_fusion.1
  279.6 3.3 %slice_bitcast_fusion.1 = (f32[12,256,256]{2,1,0:T(8,128)}, f32[12,256,256]{2,1,0:T(8,128)}) fusion(f32[2,12,256,256]{3,2,1,0:T(8,128)S(1)} %pad_maximum_fusion.1), kind=kLoop, calls=%fused_computation.80 | loop fusion | bytes 12582912 | tf_op jit(solution)/shard_map/squeeze | solution.py:93
  282.9 0.0 copy-start.5
  282.9 0.9 pad_maximum_fusion.3
  283.7 0.3 copy-done.5
  284.1 25.3 %fusion.35 = f32[1,4,256,256]{3,2,1,0:T(8,128)} fusion(f32[4,256,256]{2,1,0:T(8,128)} %get-tuple-element.9, f32[4,256,256]{2,1,0:T(8,128)S(1)} %copy-done.5, f32[4,256,256]{2,1,0:T(8,128)} %param.7, f32[1,4,256,256]{3,2,1,0:T(8,128)S(1)} %copy-done, f32[4,256,256]{2,1,0:T(8,128)} %get-tuple-element.8, f32[4,256,256]{2,1,0:T(8,128)} %get-tuple-element.7, ...), kind=kLoop, calls=%fused_computation.136 | loop fusion | flops 42205184 | bytes 33554436 | tf_op jit(solution)/shard_map/broadcast_in_dim | solution.py:96
Async XLA Ops:
  6.5 53.0 %copy-start.4 = (f32[4,256,256]{2,1,0:T(8,128)S(1)}, f32[4,256,256]{2,1,0:T(8,128)}, u32[]{:S(2)}) copy-start(f32[4,256,256]{2,1,0:T(8,128)} %param.8) | copy-start | bytes 3145732
  6.5 44.4 %all-reduce.8.cloned.1.call-start = ((), (), s32[]{:S(2)}) async-start(), calls=%async_computation | async-start | bytes 2097152 | tf_op jit(solution)/shard_map/psum | solution.py:29
  8.9 218.9 %all-reduce.10.cloned.1.call-start = ((), (), s32[]{:S(2)}) async-start(), calls=%async_computation.1 | async-start | bytes 2097152 | tf_op jit(solution)/shard_map/psum | solution.py:29
  54.0 78.0 %collective-permute-start.1 = (f32[2,4,256,256]{3,2,1,0:T(8,128)}, f32[2,4,256,256]{3,2,1,0:T(8,128)S(1)}, u32[]{:S(2)}, u32[]{:S(2)}) collective-permute-start(f32[2,4,256,256]{3,2,1,0:T(8,128)} %pad_maximum_fusion.4), channel_id=1, source_target_pairs={{0,1},{1,2},{2,3},{3,4},{4,5},{5,6},{6,7},{7,8},{8,9},{9,10},{10,1... | collective-permute-start | bytes 6291464 | tf_op jit(solution)/shard_map/ppermute | solution.py:19
  55.9 76.0 %collective-permute-start = (f32[2,4,256,256]{3,2,1,0:T(8,128)}, f32[2,4,256,256]{3,2,1,0:T(8,128)}, u32[]{:S(2)}, u32[]{:S(2)}) collective-permute-start(f32[2,4,256,256]{3,2,1,0:T(8,128)} %pad_maximum_fusion.4), channel_id=1, source_target_pairs={{1,0},{2,1},{3,2},{4,3},{5,4},{6,5},{7,6},{8,7},{9,8},{10,9},{11,1... | collective-permute-start | bytes 6291464 | tf_op jit(solution)/shard_map/ppermute | solution.py:22
  60.6 71.3 %copy-start = (f32[1,4,256,256]{3,2,1,0:T(8,128)S(1)}, f32[1,4,256,256]{3,2,1,0:T(8,128)}, u32[]{:S(2)}) copy-start(f32[1,4,256,256]{3,2,1,0:T(8,128)} %param.6) | copy-start | bytes 3145732
  60.6 66.0 %collective-permute-start.3 = (f32[4,256,256]{2,1,0:T(8,128)}, f32[4,256,256]{2,1,0:T(8,128)}, u32[]{:S(2)}, u32[]{:S(2)}) collective-permute-start(f32[4,256,256]{2,1,0:T(8,128)} %broadcast_add_fusion), channel_id=1, source_target_pairs={{0,1},{1,2},{2,3},{3,4},{4,5},{5,6},{6,7},{7,8},{8,9},{9,10},{10,1... | collective-permute-start | bytes 3145736 | tf_op jit(solution)/shard_map/ppermute | solution.py:19
  62.6 63.9 %collective-permute-start.2 = (f32[4,256,256]{2,1,0:T(8,128)}, f32[4,256,256]{2,1,0:T(8,128)}, u32[]{:S(2)}, u32[]{:S(2)}) collective-permute-start(f32[4,256,256]{2,1,0:T(8,128)} %broadcast_add_fusion), channel_id=1, source_target_pairs={{1,0},{2,1},{3,2},{4,3},{5,4},{6,5},{7,6},{8,7},{9,8},{10,9},{11,1... | collective-permute-start | bytes 3145736 | tf_op jit(solution)/shard_map/ppermute | solution.py:22
  66.3 65.6 %copy-start.2 = (f32[4,256,256]{2,1,0:T(8,128)S(1)}, f32[4,256,256]{2,1,0:T(8,128)}, u32[]{:S(2)}) copy-start(f32[4,256,256]{2,1,0:T(8,128)} %all-reduce.8.cloned.1.call-done) | copy-start | bytes 3145732
  131.9 6.0 %copy-start.1 = (f32[2,4,256,256]{3,2,1,0:T(8,128)}, f32[2,4,256,256]{3,2,1,0:T(8,128)S(1)}, u32[]{:S(2)}) copy-start(f32[2,4,256,256]{3,2,1,0:T(8,128)S(1)} %collective-permute-done.1) | copy-start | bytes 6291460
  227.8 51.3 %copy-start.3 = (f32[4,256,256]{2,1,0:T(8,128)S(1)}, f32[4,256,256]{2,1,0:T(8,128)}, u32[]{:S(2)}) copy-start(f32[4,256,256]{2,1,0:T(8,128)} %all-reduce.10.cloned.1.call-done) | copy-start | bytes 3145732
  229.3 49.8 %collective-permute-start.5 = (f32[2,4,256,256]{3,2,1,0:T(8,128)S(1)}, f32[2,4,256,256]{3,2,1,0:T(8,128)S(1)}, u32[]{:S(2)}, u32[]{:S(2)}) collective-permute-start(f32[2,4,256,256]{3,2,1,0:T(8,128)S(1)} %pad_maximum_fusion.5), channel_id=1, source_target_pairs={{0,1},{1,2},{2,3},{3,4},{4,5},{5,6},{6,7},{7,8},{8,9},{9,10},{10,1... | collective-permute-start | bytes 6291464 | tf_op jit(solution)/shard_map/ppermute | solution.py:19
  231.2 47.9 %collective-permute-start.4 = (f32[2,4,256,256]{3,2,1,0:T(8,128)S(1)}, f32[2,4,256,256]{3,2,1,0:T(8,128)S(1)}, u32[]{:S(2)}, u32[]{:S(2)}) collective-permute-start(f32[2,4,256,256]{3,2,1,0:T(8,128)S(1)} %pad_maximum_fusion.5), channel_id=1, source_target_pairs={{1,0},{2,1},{3,2},{4,3},{5,4},{6,5},{7,6},{8,7},{9,8},{10,9},{11,1... | collective-permute-start | bytes 6291464 | tf_op jit(solution)/shard_map/ppermute | solution.py:22
  282.9 1.2 copy-start.5
Sparse Core Ops, SparseCore 0:
  9.6 41.2 all-reduce.7
  188.3 39.4 all-reduce.9
where the time goes:
time: 317 us; the launch traced here: 316 us
  waiting for transfers between devices  186 us (59%)
  other arithmetic  92.8 us (29%)
  starting transfers between devices  17 us (5%)
  between operations  13.5 us (4%)
  local copies, waits for them, and re-layouts  6.93 us (2%)
    ppermute x3, waiting for transfers between devices, with_halo(): lax.ppermute(lax.slice_in_dim(block, block.shape[dim] - width, None, axis...  104 us
    psum x2, waiting for transfers between devices, spread(): return lax.psum(block, axis)  81.6 us
    select_n x2, other arithmetic, spread(): jnp.where(lax.axis_index(axis) == owner, block, jnp.zeros_like(block))  47.6 us
    broadcast_in_dim x1, other arithmetic, on_device(): return now[None]  25.3 us
    concatenate x5, other arithmetic, with_halo(): block = jnp.concatenate([low, block, high], axis=dim)  14.4 us
    ppermute x3, starting transfers between devices, with_halo(): lax.ppermute(lax.slice_in_dim(block, 0, width, axis=dim), axis, backward)  11.1 us
    squeeze x2, local copies, waits for them, and re-layouts, on_device(): own_term = operate(both[1])  6.56 us
  transfers between devices with their start and end apart: 8, of which 4 were waited for; matrix products, arithmetic and copies ran while one was open for 2% of the time, Pallas kernels for 0%

commit v1 on v0

v1 whole, which is shorter than its diff:
```python
import functools

import jax
import jax.numpy as jnp
from jax import lax
from jax.experimental import pallas as pl
from jax.experimental.pallas import tpu as pltpu
from jax.sharding import PartitionSpec as P

STEPS = 2
REACH = 4
SUB = 8
LANES = 128

second_coeffs = (8.0 / 5.0, -1.0 / 5.0, 8.0 / 315.0, -1.0 / 560.0)
first_coeffs = (4.0 / 5.0, -1.0 / 5.0, 4.0 / 105.0, -1.0 / 280.0)
centre_coeff = -205.0 / 72.0


def pad_copy(scratch, pieces, width):
    for scr, load in pieces:
        planes, halves = scr.shape[0], scr.shape[1]
        zero = jnp.zeros((planes, SUB, LANES), jnp.float32)
        for h in range(halves):
            scr[:, h, pl.ds(0, SUB), :] = zero
            scr[:, h, pl.ds(width + SUB, SUB), :] = zero

    def body(i, _):
        for scr, load in pieces:
            value = load(i)
            for h in range(scr.shape[1]):
                scr[:, h, pl.ds(pl.multiple_of(SUB * (i + 1), SUB), SUB), :] = value[:, :, h * LANES:(h + 1) * LANES]
        return 0

    lax.fori_loop(0, width // SUB, body, 0)


def taps(scr, row, low, high, h, lane):
    halves = scr.shape[1]
    here = [scr[:, j, pl.ds(pl.multiple_of(row, SUB), SUB), :] for j in range(halves)]
    centre = here[h]
    slab = centre.shape[0]
    full = jnp.concatenate([low, centre, high], axis=0)
    out = []
    for k in range(1, REACH + 1):
        first = (full[REACH + k:REACH + k + slab], full[REACH - k:REACH - k + slab])
        second = (scr[:, h, pl.ds(row + k, SUB), :], scr[:, h, pl.ds(row - k, SUB), :])
        up = pltpu.roll(centre, LANES - k, 2)
        down = pltpu.roll(centre, k, 2)
        above = pltpu.roll(here[h + 1], LANES - k, 2) if h + 1 < halves else 0.0
        below = pltpu.roll(here[h - 1], k, 2) if h > 0 else 0.0
        third = (jnp.where(lane < LANES - k, up, above), jnp.where(lane >= k, down, below))
        out.append((first, second, third))
    return centre, out


def firsts(near):
    totals = []
    for d in range(3):
        total = None
        for k in range(REACH):
            term = first_coeffs[k] * (near[k][d][0] - near[k][d][1])
            total = term if total is None else total + term
        totals.append(total)
    return totals


def seconds(centre, near):
    total = (3.0 * centre_coeff) * centre
    for k in range(REACH):
        (a, b), (c, d), (e, f) = near[k]
        total = total + second_coeffs[k] * (((a + b) + (c + d)) + (e + f))
    return total


def sides(even, inner, outer):
    return jnp.where(even, outer, inner), jnp.where(even, inner, outer)


def lane_index(slab):
    return lax.broadcasted_iota(jnp.int32, (slab, SUB, LANES), 2)


def slope_kernel(width, info, buoy, inner, outer, s1, s2, s3, scr):
    start, even = info[0], info[1] == 1
    slab, halves = scr.shape[0], scr.shape[1]

    def load(i):
        return buoy[:, pl.ds(pl.multiple_of(start + SUB * i, SUB), SUB), :] - 1.0

    pad_copy(None, [(scr, load)], width)
    lane = lane_index(slab)

    def body(i, _):
        rows = pl.ds(pl.multiple_of(SUB * i, SUB), SUB)
        for h in range(halves):
            cols = slice(h * LANES, (h + 1) * LANES)
            low, high = sides(even, inner[0, :, rows, cols], outer[0, :, rows, cols])
            _, near = taps(scr, SUB * (i + 1), low, high, h, lane)
            for ref, value in zip((s1, s2, s3), firsts(near)):
                ref[:, rows, cols] = value
        return 0

    lax.fori_loop(0, width // SUB, body, 0)


def operator(scr, row, low, high, h, lane, buoyancy, slopes):
    centre, near = taps(scr, row, low, high, h, lane)
    grads = firsts(near)
    value = buoyancy * seconds(centre, near)
    for slope, grad in zip(slopes, grads):
        value = value + slope * grad
    return centre, value


def first_kernel(parts, width, rows_core, info, now_own, now_far, in_own, out_own, in_far, out_far, before_own, far,
                 pert_own, stiff, buoy, s1, s2, s3, following, faces, *scrs):
    start, even, base, offset = info[0], info[1] == 1, info[2], info[3]
    slab, halves = scrs[0].shape[0], scrs[0].shape[1]

    def whole(i):
        return pl.ds(pl.multiple_of(start + SUB * i, SUB), SUB)

    loads = [lambda i: now_own[:, whole(i), :]]
    for s in range(1, parts):
        loads.append(lambda i, s=s: now_far[s - 1, :, pl.ds(pl.multiple_of(SUB * i, SUB), SUB), :])
    pad_copy(None, list(zip(scrs, loads)), width)
    lane = lane_index(slab)

    def body(i, _):
        rows = pl.ds(pl.multiple_of(SUB * i, SUB), SUB)
        for h in range(halves):
            cols = slice(h * LANES, (h + 1) * LANES)
            slopes = [ref[:, rows, cols] for ref in (s1, s2, s3)]
            b = buoy[:, whole(i), cols]
            k = stiff[:, whole(i), cols]
            centres, images = [], []
            for s in range(parts):
                if s == 0:
                    low, high = sides(even, in_own[1, :, rows, cols], out_own[1, :, rows, cols])
                else:
                    low, high = sides(even, in_far[s - 1, :, rows, cols], out_far[s - 1, :, rows, cols])
                centre, image = operator(scrs[s], SUB * (i + 1), low, high, h, lane, b, slopes)
                centres.append(centre)
                images.append(image)
            source = images[0]
            for s in range(1, parts):
                source = jnp.where(base == s, images[s], source)
            for s in range(parts):
                if s == 0:
                    before = before_own[:, whole(i), cols]
                    scale = pert_own[:, whole(i), cols]
                else:
                    before = far[s - 1, 0, :, rows, cols]
                    scale = far[s - 1, 1, :, rows, cols]
                scale = jnp.where(base == s, 0.0, scale)
                value = 2.0 * centres[s] - before + k * images[s] + scale * source
                following[s, :, rows, cols] = value
        return 0

    lax.fori_loop(0, width // SUB, body, 0)

    def core(i, _):
        src = pl.ds(pl.multiple_of(offset + SUB * i, SUB), SUB)
        dst = pl.ds(pl.multiple_of(SUB * i, SUB), SUB)
        faces[:, :, dst, :] = following[:, :, src, :]
        return 0

    lax.fori_loop(0, rows_core // SUB, core, 0)


def second_kernel(parts, width, rows_core, info, now, inner, outer, before_own, before_far, far, pert_own, stiff, buoy,
                  s1, s2, s3, own, others, *scrs):
    start, even, base, offset = info[0], info[1] == 1, info[2], info[3]
    slab, halves = scrs[0].shape[0], scrs[0].shape[1]
    loads = []
    for s in range(parts):
        loads.append(lambda i, s=s: now[s, :, pl.ds(pl.multiple_of(SUB * i, SUB), SUB), :])
    pad_copy(None, list(zip(scrs, loads)), width)
    lane = lane_index(slab)

    def body(i, _):
        rows = pl.ds(pl.multiple_of(SUB * i, SUB), SUB)
        win = pl.ds(pl.multiple_of(offset + SUB * i, SUB), SUB)
        whole = pl.ds(pl.multiple_of(start + offset + SUB * i, SUB), SUB)
        for h in range(halves):
            cols = slice(h * LANES, (h + 1) * LANES)
            slopes = [ref[:, win, cols] for ref in (s1, s2, s3)]
            b = buoy[:, whole, cols]
            k = stiff[:, whole, cols]
            centres, images = [], []
            for s in range(parts):
                low, high = sides(even, inner[s, :, rows, cols], outer[s, :, rows, cols])
                centre, image = operator(scrs[s], offset + SUB * (i + 1), low, high, h, lane, b, slopes)
                centres.append(centre)
                images.append(image)
            source = images[0]
            for s in range(1, parts):
                source = jnp.where(base == s, images[s], source)
            for s in range(parts):
                if s == 0:
                    before = before_own[:, whole, cols]
                    scale = pert_own[:, whole, cols]
                else:
                    before = before_far[s - 1, :, win, cols]
                    scale = far[s - 1, 1, :, win, cols]
                scale = jnp.where(base == s, 0.0, scale)
                value = 2.0 * centres[s] - before + k * images[s] + scale * source
                if s == 0:
                    own[:, whole, cols] = value
                else:
                    others[s - 1, :, rows, cols] = value
        return 0

    lax.fori_loop(0, rows_core // SUB, body, 0)


def call(kernel, info, args, outs, scratch, flops):
    vmem = pl.BlockSpec(memory_space=pltpu.VMEM)
    size = sum(4 * a.size for a in args) + sum(4 * o.size for o in outs)
    return pl.pallas_call(
        kernel,
        out_shape=outs,
        in_specs=[pl.BlockSpec(memory_space=pltpu.SMEM)] + [vmem] * len(args),
        out_specs=[vmem] * len(outs),
        scratch_shapes=scratch,
        compiler_params=pltpu.CompilerParams(vmem_limit_bytes=24 << 20),
        cost_estimate=pl.CostEstimate(flops=flops, bytes_accessed=size, transcendentals=0),
    )(info, *args)


def on_device(field_before, field_now, stiffness, buoyancy, perturbation):
    parts, count = lax.axis_size("probe"), lax.axis_size("space")
    part, place = lax.axis_index("probe"), lax.axis_index("space")
    before, now, pert = field_before[0], field_now[0], perturbation[0]
    slab, height, depth = now.shape
    core = height // parts
    width = min(height, core + (2 if parts > 2 else 1) * 2 * REACH)

    def window(p):
        return jnp.clip(core * p - 2 * REACH, 0, height - width)

    start = window(part)
    offset = core * part - start
    even = place % 2 == 0
    info = jnp.stack([start, even.astype(jnp.int32), part, offset]).astype(jnp.int32)

    def rows(field, p):
        return lax.dynamic_slice_in_dim(field, window(p), width, axis=field.ndim - 2)

    inner_pairs = [(i, i ^ 1) for i in range(count)]
    outer_pairs = [(i, ((i + 1) ^ 1) - 1) for i in range(1, count - 1)]

    def exchange(stack):
        results = []
        for pairs, from_end in ((inner_pairs, even), (outer_pairs, jnp.logical_not(even))):
            face = stack
            if slab > REACH:
                face = lax.dynamic_slice_in_dim(stack, jnp.where(from_end, slab - REACH, 0), REACH, axis=1)
            results.append(lax.ppermute(face, "space", pairs))
        return results

    def turn(field, s):
        return lax.ppermute(field, "probe", [(i, (i + s) % parts) for i in range(parts)])

    in_own, out_own = exchange(jnp.stack([rows(buoyancy, part) - 1.0, rows(now, part)]))
    now_far = jnp.stack([turn(rows(now, (part + s) % parts), s) for s in range(1, parts)])
    in_far, out_far = exchange(now_far)
    pair = lax.optimization_barrier((before, pert, now_far))
    far = jnp.stack(
        [turn(rows(jnp.stack([pair[0], pair[1]]), (part + s) % parts), s) for s in range(1, parts)]
    )

    f32 = jnp.float32
    field = jax.ShapeDtypeStruct((slab, width, depth), f32)
    scr = pltpu.VMEM((slab, depth // LANES, width + 2 * SUB, LANES), f32)
    cells = slab * width * depth
    s1, s2, s3 = call(
        functools.partial(slope_kernel, width), info, (buoyancy, in_own, out_own), [field] * 3, [scr], 33 * cells
    )
    following, faces = call(
        functools.partial(first_kernel, parts, width, core),
        info,
        (now, now_far, in_own, out_own, in_far, out_far, before, far, pert, stiffness, buoyancy, s1, s2, s3),
        [
            jax.ShapeDtypeStruct((parts, slab, width, depth), f32),
            jax.ShapeDtypeStruct((parts, slab, core, depth), f32),
        ],
        [scr] * parts,
        80 * parts * cells,
    )
    inner, outer = exchange(faces)
    own, others = call(
        functools.partial(second_kernel, parts, width, core),
        info,
        (following, inner, outer, now, now_far, far, pert, stiffness, buoyancy, s1, s2, s3),
        [
            jax.ShapeDtypeStruct((slab, height, depth), f32),
            jax.ShapeDtypeStruct((parts - 1, slab, core, depth), f32),
        ],
        [scr] * parts,
        80 * parts * cells,
    )
    for s in range(1, parts):
        back = turn(others[s - 1], parts - s)
        own = lax.dynamic_update_slice_in_dim(own, back, core * ((part + s) % parts), axis=1)
    return own[None]


def solution(mesh):
    placed = (
        P("probe", "space", None, None),
        P("probe", "space", None, None),
        P("space", None, None),
        P("space", None, None),
        P("probe", "space", None, None),
    )
    return jax.shard_map(
        on_device,
        mesh=mesh,
        in_specs=placed,
        out_specs=P("probe", "space", None, None),
        check_vma=False,
    )
```

time: 317 us -> 95.6 us (0.30)
  waiting for transfers between devices: 186 us -> 57.5 us
  other arithmetic: 92.8 us -> 2.33 us
  Pallas kernels: 0 us -> 19.3 us
  between operations: 13.5 us -> 0.11 us
  local copies, waits for them, and re-layouts: 6.93 us -> 2.29 us
  starting transfers between devices: 17 us -> 13.7 us
    psum x2 -> x0, waiting for transfers between devices: 81.6 us -> none  [spread(): return lax.psum(block, axis)]
    select_n x2 -> x0, other arithmetic: 47.6 us -> none  [spread(): jnp.where(lax.axis_index(axis) == owner, block, jnp.zeros_like(block))]
    ppermute x6 -> x9, waiting for transfers between devices: 104 us -> 57.5 us  [the longest x6 41.7 us: exchange(): results.append(lax.ppermute(face, 'space', pairs))]
    broadcast_in_dim x1 -> x0, other arithmetic: 25.3 us -> none  [on_device(): return now[None]]
    pallas_call x0 -> x3, Pallas kernels: none -> 19.3 us  [call(): pl.pallas_call(kernel, out_shape=outs, in_specs=[pl.BlockSpec(memory_spac...]
    concatenate x5 -> x0, other arithmetic: 14.4 us -> none  [with_halo(): block = jnp.concatenate([low, block, high], axis=dim)]
    squeeze x2 -> x0, local copies, waits for them, and re-layouts: 6.56 us -> none  [on_device(): own_term = operate(both[1])]
    ppermute x6 -> x9, starting transfers between devices: 17 us -> 13.7 us  [the longest x6 9.18 us: exchange(): results.append(lax.ppermute(face, 'space', pairs))]
  transfers between devices with their start and end apart: 8 -> 9, of which waited for: 4 -> 5; matrix products, arithmetic and copies ran while one was open for 2% -> 2% of each run, Pallas kernels for 0% -> 5%
where the time goes in v1:
time: 95.6 us; the launch traced here: 95.3 us
  waiting for transfers between devices  57.5 us (60%)
  Pallas kernels  19.3 us (20%)
  starting transfers between devices  13.7 us (14%)
  other arithmetic  2.33 us (2%)
  local copies, waits for them, and re-layouts  2.29 us (2%)
    ppermute x6, waiting for transfers between devices, exchange(): results.append(lax.ppermute(face, 'space', pairs))  41.7 us
    pallas_call x3, Pallas kernels, call(): pl.pallas_call(kernel, out_shape=outs, in_specs=[pl.BlockSpec(memory_spac...  19.3 us
    ppermute x3, waiting for transfers between devices, turn(): lax.ppermute(field, 'probe', [(i, (i + s) % parts) for i in range(parts)])  15.9 us
    ppermute x6, starting transfers between devices, exchange(): results.append(lax.ppermute(face, 'space', pairs))  9.18 us
    ppermute x3, starting transfers between devices, turn(): lax.ppermute(field, 'probe', [(i, (i + s) % parts) for i in range(parts)])  4.56 us
  transfers between devices with their start and end apart: 9, of which 5 were waited for; matrix products, arithmetic and copies ran while one was open for 2% of the time, Pallas kernels for 5%

profile of v1, /device:TPU:4, one launch (start us, length us, event | category | flops | bytes accessed | tf_op | source)
XLA Modules:
  0.0 95.3 jit_solution(17219138064869911369)
XLA Ops:
  0.0 0.0 copy-start
  0.0 1.4 %constant_dynamic-slice_fusion = (f32[1,4,136,256]{3,2,1,0:T(8,128)S(1)}, f32[4,136,256]{2,1,0:T(8,128)S(1)}) fusion(f32[1,4,256,256]{3,2,1,0:T(8,128)} %param.6, s32[]{:T(128)} %min.10, s32[]{:T(128)S(6)} %min.11), kind=kLoop, calls=%fused_computation.7 | loop fusion | bytes 2228232 | tf_op jit(solution)/shard_map/dynamic_slice | solution.py:249
  1.4 1.6 %collective-permute-start = (f32[4,136,256]{2,1,0:T(8,128)S(1)}, f32[4,136,256]{2,1,0:T(8,128)}, u32[]{:S(2)}, u32[]{:S(2)}) collective-permute-start(f32[4,136,256]{2,1,0:T(8,128)S(1)} %get-tuple-element.24), channel_id=1, source_target_pairs={{0,16},{16,0},{1,17},{17,1},{2,18},{18,2},{3,19},{19,3},{4,20},{20... | collective-permute-start | bytes 1671176 | tf_op jit(solution)/shard_map/ppermute | solution.py:264
  3.0 0.0 copy-done
  3.0 0.1 add_bitcast_fusion
  3.1 0.0 copy-start.2
  3.1 0.0 copy-start.3
  3.1 1.1 %pad_maximum_fusion = f32[2,4,136,256]{3,2,1,0:T(8,128)} fusion(f32[1,4,136,256]{3,2,1,0:T(8,128)S(1)} %get-tuple-element.23, f32[1,4,136,256]{3,2,1,0:T(8,128)S(1)} %add_bitcast_fusion), kind=kLoop, calls=%fused_computation.3 | loop fusion | flops 278528 | bytes 2228224 | tf_op jit(solution)/shard_map/stack | solution.py:266
  4.2 1.9 %collective-permute-start.2 = (f32[2,4,136,256]{3,2,1,0:T(8,128)}, f32[2,4,136,256]{3,2,1,0:T(8,128)S(1)}, u32[]{:S(2)}, u32[]{:S(2)}) collective-permute-start(f32[2,4,136,256]{3,2,1,0:T(8,128)} %pad_maximum_fusion), channel_id=1, source_target_pairs={{1,2},{2,1},{3,4},{4,3},{5,6},{6,5},{7,8},{8,7},{9,10},{10,9},{11,... | collective-permute-start | bytes 3342344 | tf_op jit(solution)/shard_map/ppermute | solution.py:260
  6.1 1.7 %collective-permute-start.1 = (f32[2,4,136,256]{3,2,1,0:T(8,128)}, f32[2,4,136,256]{3,2,1,0:T(8,128)}, u32[]{:S(2)}, u32[]{:S(2)}) collective-permute-start(f32[2,4,136,256]{3,2,1,0:T(8,128)} %pad_maximum_fusion), channel_id=1, source_target_pairs={{0,1},{1,0},{2,3},{3,2},{4,5},{5,4},{6,7},{7,6},{8,9},{9,8},{10,11... | collective-permute-start | bytes 3342344 | tf_op jit(solution)/shard_map/ppermute | solution.py:260
  7.8 8.2 %collective-permute-done = f32[4,136,256]{2,1,0:T(8,128)} collective-permute-done((f32[4,136,256]{2,1,0:T(8,128)S(1)}, f32[4,136,256]{2,1,0:T(8,128)}, u32[]{:S(2)}, u32[]{:S(2)}) %collective-permute-start) | collective-permute-done | bytes 557088 | tf_op jit(solution)/shard_map/ppermute | solution.py:264
  16.0 0.0 copy-done.2
  16.0 0.0 copy-done.3
  16.0 1.1 %fusion = f32[2,4,136,256]{3,2,1,0:T(8,128)} fusion(s32[]{:T(128)S(6)} %min.11, f32[1,4,256,256]{3,2,1,0:T(8,128)S(1)} %copy-done.3, f32[1,4,256,256]{3,2,1,0:T(8,128)S(1)} %copy-done.2), kind=kLoop, calls=%fused_computation.2 | loop fusion | flops 278528 | bytes 3211268 | tf_op jit(solution)/shard_map/stack | solution.py:271
  17.1 1.5 %collective-permute-start.5 = (f32[2,4,136,256]{3,2,1,0:T(8,128)}, f32[2,4,136,256]{3,2,1,0:T(8,128)}, u32[]{:S(2)}, u32[]{:S(2)}) collective-permute-start(f32[2,4,136,256]{3,2,1,0:T(8,128)} %fusion), channel_id=1, source_target_pairs={{0,16},{16,0},{1,17},{17,1},{2,18},{18,2},{3,19},{19,3},{4,20},{20... | collective-permute-start | bytes 3342344 | tf_op jit(solution)/shard_map/ppermute | solution.py:264
  18.6 1.9 %collective-permute-start.4 = (f32[1,4,136,256]{3,2,1,0:T(8,128)}, f32[1,4,136,256]{3,2,1,0:T(8,128)}, u32[]{:S(2)}, u32[]{:S(2)}) collective-permute-start(f32[1,4,136,256]{3,2,1,0:T(8,128)} %bitcast.6.now_far.before_far), channel_id=1, source_target_pairs={{1,2},{2,1},{3,4},{4,3},{5,6},{6,5},{7,8},{8,7},{9,10},{10,9},{11,... | collective-permute-start | bytes 1671176 | tf_op jit(solution)/shard_map/ppermute | solution.py:260
  20.5 1.7 %collective-permute-start.3 = (f32[1,4,136,256]{3,2,1,0:T(8,128)}, f32[1,4,136,256]{3,2,1,0:T(8,128)}, u32[]{:S(2)}, u32[]{:S(2)}) collective-permute-start(f32[1,4,136,256]{3,2,1,0:T(8,128)} %bitcast.6.now_far.before_far), channel_id=1, source_target_pairs={{0,1},{1,0},{2,3},{3,2},{4,5},{5,4},{6,7},{7,6},{8,9},{9,8},{10,11... | collective-permute-start | bytes 1671176 | tf_op jit(solution)/shard_map/ppermute | solution.py:260
  22.2 0.1 pad_add_fusion.info
  22.3 0.0 copy-start.1
  22.3 0.0 copy-start.4
  22.3 0.0 copy-start.5
  22.3 16.8 %collective-permute-done.2.outer.out_own = f32[2,4,136,256]{3,2,1,0:T(8,128)S(1)} collective-permute-done((f32[2,4,136,256]{3,2,1,0:T(8,128)}, f32[2,4,136,256]{3,2,1,0:T(8,128)S(1)}, u32[]{:S(2)}, u32[]{:S(2)}) %collective-permute-start.2) | collective-permute-done | bytes 1114144 | tf_op jit(solution)/shard_map/ppermute | solution.py:260
  39.1 0.0 collective-permute-done.1.inner.in_own
  39.1 4.3 %shard_map.55 = (f32[4,136,256]{2,1,0:T(8,128)S(1)}, f32[4,136,256]{2,1,0:T(8,128)S(1)}, f32[4,136,256]{2,1,0:T(8,128)S(1)}) custom-call(s32[4]{0:T(128)S(1)} %pad_add_fusion.info, f32[4,256,256]{2,1,0:T(8,128)S(1)} %copy-done, f32[2,4,136,256]{3,2,1,0:T(8,128)} %collective-permute-done.1.inner.in_own, ...), custom_call_target="tpu_custom_call" | custom-call | flops 4595712 | bytes 4947968 | tf_op jit(solution)/shard_map/pallas_call | solution.py:221
  43.4 1.8 %collective-permute-done.4.out_far = f32[1,4,136,256]{3,2,1,0:T(8,128)} collective-permute-done((f32[1,4,136,256]{3,2,1,0:T(8,128)}, f32[1,4,136,256]{3,2,1,0:T(8,128)}, u32[]{:S(2)}, u32[]{:S(2)}) %collective-permute-start.4) | collective-permute-done | bytes 557088 | tf_op jit(solution)/shard_map/ppermute | solution.py:260
  45.2 0.0 collective-permute-done.3.in_far
  45.2 0.0 collective-permute-done.5
  45.2 0.0 copy-done.1
  45.2 0.0 copy-done.4
  45.2 0.0 copy-done.5
  45.2 7.5 %shard_map.56 = (f32[2,4,136,256]{3,2,1,0:T(8,128)S(1)}, f32[2,4,128,256]{3,2,1,0:T(8,128)S(1)}) custom-call(s32[4]{0:T(128)S(1)} %pad_add_fusion.info, f32[4,256,256]{2,1,0:T(8,128)S(1)} %bitcast.19, f32[1,4,136,256]{3,2,1,0:T(8,128)} %bitcast.6.now_far.before_far, f32[2,4,136,256]{3,2,1,0:T(8,128)} %collective-permute-done.1.inner.in_own, ...), custom_call_target="tpu_custom_call" | custom-call | flops 22282240 | bytes 14090240 | tf_op jit(solution)/shard_map/pallas_call | solution.py:221
  52.7 1.9 %collective-permute-start.7 = (f32[2,4,128,256]{3,2,1,0:T(8,128)S(1)}, f32[2,4,128,256]{3,2,1,0:T(8,128)S(1)}, u32[]{:S(2)}, u32[]{:S(2)}) collective-permute-start(f32[2,4,128,256]{3,2,1,0:T(8,128)S(1)} %get-tuple-element.20), channel_id=1, source_target_pairs={{1,2},{2,1},{3,4},{4,3},{5,6},{6,5},{7,8},{8,7},{9,10},{10,9},{11,... | collective-permute-start | bytes 3145736 | tf_op jit(solution)/shard_map/ppermute | solution.py:260
  54.7 0.1 collective-permute-start.6
  54.7 23.1 %collective-permute-done.7.outer = f32[2,4,128,256]{3,2,1,0:T(8,128)S(1)} collective-permute-done((f32[2,4,128,256]{3,2,1,0:T(8,128)S(1)}, f32[2,4,128,256]{3,2,1,0:T(8,128)S(1)}, u32[]{:S(2)}, u32[]{:S(2)}) %collective-permute-start.7) | collective-permute-done | bytes 1048608 | tf_op jit(solution)/shard_map/ppermute | solution.py:260
  77.8 0.0 collective-permute-done.6.inner
  77.8 7.5 %shard_map.57 = (f32[4,256,256]{2,1,0:T(8,128)}, f32[1,4,128,256]{3,2,1,0:T(8,128)S(1)}) custom-call(s32[4]{0:T(128)S(1)} %pad_add_fusion.info, f32[2,4,136,256]{3,2,1,0:T(8,128)S(1)} %get-tuple-element.19.now, f32[2,4,128,256]{3,2,1,0:T(8,128)S(1)} %collective-permute-done.6.inner, f32[2,4,128,256]{3,2,1,0:T(8,128)S(1)} %collective-permute-done.7.outer, ...), custom_call_target="tpu_custom_call" | custom-call | flops 22282240 | bytes 12320768 | tf_op jit(solution)/shard_map/pallas_call | solution.py:221
  85.3 1.5 %collective-permute-start.8 = (f32[4,128,256]{2,1,0:T(8,128)S(1)}, f32[4,128,256]{2,1,0:T(8,128)S(1)}, u32[]{:S(2)}, u32[]{:S(2)}) collective-permute-start(f32[4,128,256]{2,1,0:T(8,128)S(1)} %bitcast.24), channel_id=1, source_target_pairs={{0,16},{16,0},{1,17},{17,1},{2,18},{18,2},{3,19},{19,3},{4,20},{20... | collective-permute-start | bytes 1572872 | tf_op jit(solution)/shard_map/ppermute | solution.py:264
  86.8 7.7 %collective-permute-done.8 = f32[4,128,256]{2,1,0:T(8,128)S(1)} collective-permute-done((f32[4,128,256]{2,1,0:T(8,128)S(1)}, f32[4,128,256]{2,1,0:T(8,128)S(1)}, u32[]{:S(2)}, u32[]{:S(2)}) %collective-permute-start.8) | collective-permute-done | bytes 524320 | tf_op jit(solution)/shard_map/ppermute | solution.py:264
  94.5 0.8 bitcast_dynamic-update-slice_fusion
Async XLA Ops:
  0.0 3.0 %copy-start = (f32[4,256,256]{2,1,0:T(8,128)S(1)}, f32[4,256,256]{2,1,0:T(8,128)}, u32[]{:S(2)}) copy-start(f32[4,256,256]{2,1,0:T(8,128)} %buoy.5) | copy-start | bytes 3145732
  1.4 14.5 %collective-permute-start = (f32[4,136,256]{2,1,0:T(8,128)S(1)}, f32[4,136,256]{2,1,0:T(8,128)}, u32[]{:S(2)}, u32[]{:S(2)}) collective-permute-start(f32[4,136,256]{2,1,0:T(8,128)S(1)} %get-tuple-element.24), channel_id=1, source_target_pairs={{0,16},{16,0},{1,17},{17,1},{2,18},{18,2},{3,19},{19,3},{4,20},{20... | collective-permute-start | bytes 1671176 | tf_op jit(solution)/shard_map/ppermute | solution.py:264
  3.1 12.9 %copy-start.2 = (f32[1,4,256,256]{3,2,1,0:T(8,128)S(1)}, f32[1,4,256,256]{3,2,1,0:T(8,128)}, u32[]{:S(2)}) copy-start(f32[1,4,256,256]{3,2,1,0:T(8,128)} %param.9) | copy-start | bytes 3145732
  3.1 12.9 %copy-start.3 = (f32[1,4,256,256]{3,2,1,0:T(8,128)S(1)}, f32[1,4,256,256]{3,2,1,0:T(8,128)}, u32[]{:S(2)}) copy-start(f32[1,4,256,256]{3,2,1,0:T(8,128)} %param.5) | copy-start | bytes 3145732
  4.2 34.9 %collective-permute-start.2 = (f32[2,4,136,256]{3,2,1,0:T(8,128)}, f32[2,4,136,256]{3,2,1,0:T(8,128)S(1)}, u32[]{:S(2)}, u32[]{:S(2)}) collective-permute-start(f32[2,4,136,256]{3,2,1,0:T(8,128)} %pad_maximum_fusion), channel_id=1, source_target_pairs={{1,2},{2,1},{3,4},{4,3},{5,6},{6,5},{7,8},{8,7},{9,10},{10,9},{11,... | collective-permute-start | bytes 3342344 | tf_op jit(solution)/shard_map/ppermute | solution.py:260
  6.1 33.0 %collective-permute-start.1 = (f32[2,4,136,256]{3,2,1,0:T(8,128)}, f32[2,4,136,256]{3,2,1,0:T(8,128)}, u32[]{:S(2)}, u32[]{:S(2)}) collective-permute-start(f32[2,4,136,256]{3,2,1,0:T(8,128)} %pad_maximum_fusion), channel_id=1, source_target_pairs={{0,1},{1,0},{2,3},{3,2},{4,5},{5,4},{6,7},{7,6},{8,9},{9,8},{10,11... | collective-permute-start | bytes 3342344 | tf_op jit(solution)/shard_map/ppermute | solution.py:260
  17.1 28.1 %collective-permute-start.5 = (f32[2,4,136,256]{3,2,1,0:T(8,128)}, f32[2,4,136,256]{3,2,1,0:T(8,128)}, u32[]{:S(2)}, u32[]{:S(2)}) collective-permute-start(f32[2,4,136,256]{3,2,1,0:T(8,128)} %fusion), channel_id=1, source_target_pairs={{0,16},{16,0},{1,17},{17,1},{2,18},{18,2},{3,19},{19,3},{4,20},{20... | collective-permute-start | bytes 3342344 | tf_op jit(solution)/shard_map/ppermute | solution.py:264
  18.6 26.6 %collective-permute-start.4 = (f32[1,4,136,256]{3,2,1,0:T(8,128)}, f32[1,4,136,256]{3,2,1,0:T(8,128)}, u32[]{:S(2)}, u32[]{:S(2)}) collective-permute-start(f32[1,4,136,256]{3,2,1,0:T(8,128)} %bitcast.6.now_far.before_far), channel_id=1, source_target_pairs={{1,2},{2,1},{3,4},{4,3},{5,6},{6,5},{7,8},{8,7},{9,10},{10,9},{11,... | collective-permute-start | bytes 1671176 | tf_op jit(solution)/shard_map/ppermute | solution.py:260
  20.5 24.7 %collective-permute-start.3 = (f32[1,4,136,256]{3,2,1,0:T(8,128)}, f32[1,4,136,256]{3,2,1,0:T(8,128)}, u32[]{:S(2)}, u32[]{:S(2)}) collective-permute-start(f32[1,4,136,256]{3,2,1,0:T(8,128)} %bitcast.6.now_far.before_far), channel_id=1, source_target_pairs={{0,1},{1,0},{2,3},{3,2},{4,5},{5,4},{6,7},{7,6},{8,9},{9,8},{10,11... | collective-permute-start | bytes 1671176 | tf_op jit(solution)/shard_map/ppermute | solution.py:260
  22.3 22.9 %copy-start.1 = (f32[1,4,256,256]{3,2,1,0:T(8,128)S(1)}, f32[1,4,256,256]{3,2,1,0:T(8,128)}, u32[]{:S(2)}) copy-start(f32[1,4,256,256]{3,2,1,0:T(8,128)} %param.6) | copy-start | bytes 3145732
  22.3 22.9 %copy-start.4 = (f32[1,4,256,256]{3,2,1,0:T(8,128)S(1)}, f32[1,4,256,256]{3,2,1,0:T(8,128)}, u32[]{:S(2)}) copy-start(f32[1,4,256,256]{3,2,1,0:T(8,128)} %param.5) | copy-start | bytes 3145732
  22.3 22.9 %copy-start.5 = (f32[4,256,256]{2,1,0:T(8,128)S(1)}, f32[4,256,256]{2,1,0:T(8,128)}, u32[]{:S(2)}) copy-start(f32[4,256,256]{2,1,0:T(8,128)} %stiff.3) | copy-start | bytes 3145732
  52.7 25.1 %collective-permute-start.7 = (f32[2,4,128,256]{3,2,1,0:T(8,128)S(1)}, f32[2,4,128,256]{3,2,1,0:T(8,128)S(1)}, u32[]{:S(2)}, u32[]{:S(2)}) collective-permute-start(f32[2,4,128,256]{3,2,1,0:T(8,128)S(1)} %get-tuple-element.20), channel_id=1, source_target_pairs={{1,2},{2,1},{3,4},{4,3},{5,6},{6,5},{7,8},{8,7},{9,10},{10,9},{11,... | collective-permute-start | bytes 3145736 | tf_op jit(solution)/shard_map/ppermute | solution.py:260
  54.7 23.2 %collective-permute-start.6 = (f32[2,4,128,256]{3,2,1,0:T(8,128)S(1)}, f32[2,4,128,256]{3,2,1,0:T(8,128)S(1)}, u32[]{:S(2)}, u32[]{:S(2)}) collective-permute-start(f32[2,4,128,256]{3,2,1,0:T(8,128)S(1)} %get-tuple-element.20), channel_id=1, source_target_pairs={{0,1},{1,0},{2,3},{3,2},{4,5},{5,4},{6,7},{7,6},{8,9},{9,8},{10,11... | collective-permute-start | bytes 3145736 | tf_op jit(solution)/shard_map/ppermute | solution.py:260
  85.3 9.2 %collective-permute-start.8 = (f32[4,128,256]{2,1,0:T(8,128)S(1)}, f32[4,128,256]{2,1,0:T(8,128)S(1)}, u32[]{:S(2)}, u32[]{:S(2)}) collective-permute-start(f32[4,128,256]{2,1,0:T(8,128)S(1)} %bitcast.24), channel_id=1, source_target_pairs={{0,16},{16,0},{1,17},{17,1},{2,18},{18,2},{3,19},{19,3},{4,20},{20... | collective-permute-start | bytes 1572872 | tf_op jit(solution)/shard_map/ppermute | solution.py:264

commit v2 on v0

v2 whole, which is shorter than its diff:
```python
import functools

import jax
import jax.numpy as jnp
from jax import lax
from jax.experimental import pallas as pl
from jax.experimental.pallas import tpu as pltpu
from jax.sharding import PartitionSpec as P

STEPS = 2
REACH = 4
SUB = 8
LANES = 128
HALF = (1, 2)
TINY = True

second_coeffs = (8.0 / 5.0, -1.0 / 5.0, 8.0 / 315.0, -1.0 / 560.0)
first_coeffs = (4.0 / 5.0, -1.0 / 5.0, 4.0 / 105.0, -1.0 / 280.0)
centre_coeff = -205.0 / 72.0


def aligned(row):
    return pl.ds(pl.multiple_of(row, SUB), SUB)


def total_of(terms):
    total = None
    for term in terms:
        total = term if total is None else total + term
    return total


def pad_rows(scr, load, width):
    planes, halves = scr.shape[0], scr.shape[1]
    zero = jnp.zeros((planes, SUB, LANES), jnp.float32)
    for h in range(halves):
        scr[:, h, pl.ds(0, SUB), :] = zero
        scr[:, h, pl.ds(width + SUB, SUB), :] = zero

    def body(i, _):
        value = load(SUB * i)
        for h in range(halves):
            scr[:, h, aligned(SUB * (i + 1)), :] = value[:, :, h * LANES:(h + 1) * LANES]
        return 0

    lax.fori_loop(0, width // SUB, body, 0)


def local_terms(scr, row, h, lane, with_second=True):
    halves = scr.shape[1]
    here = [scr[:, j, aligned(row + SUB), :] for j in range(halves)]
    centre = here[h]
    slab = centre.shape[0]
    grads = ([], [])
    laps = []
    for k in range(1, REACH + 1):
        up = pltpu.roll(centre, LANES - k, 2)
        down = pltpu.roll(centre, k, 2)
        above = pltpu.roll(here[h + 1], LANES - k, 2) if h + 1 < halves else 0.0
        below = pltpu.roll(here[h - 1], k, 2) if h > 0 else 0.0
        up = jnp.where(lane < LANES - k, up, above)
        down = jnp.where(lane >= k, down, below)
        right = scr[:, h, pl.ds(row + SUB + k, SUB), :]
        left = scr[:, h, pl.ds(row + SUB - k, SUB), :]
        grads[0].append(first_coeffs[k - 1] * (right - left))
        grads[1].append(first_coeffs[k - 1] * (up - down))
        if with_second:
            laps.append(second_coeffs[k - 1] * ((right + left) + (up + down)))
    planes = []
    plane_laps = []
    for p in range(slab):
        first, second = [], []
        for k in range(1, REACH + 1):
            high = centre[p + k] if p + k < slab else None
            low = centre[p - k] if p >= k else None
            if high is not None and low is not None:
                first.append(first_coeffs[k - 1] * (high - low))
                second.append(second_coeffs[k - 1] * (high + low))
            elif high is not None:
                first.append(first_coeffs[k - 1] * high)
                second.append(second_coeffs[k - 1] * high)
            elif low is not None:
                first.append(-first_coeffs[k - 1] * low)
                second.append(second_coeffs[k - 1] * low)
        planes.append(total_of(first))
        plane_laps.append(total_of(second))
    along = jnp.stack(planes)
    lap = None
    if with_second:
        lap = total_of(laps + [(3.0 * centre_coeff) * centre, jnp.stack(plane_laps)])
    return centre, lap, along, total_of(grads[0]), total_of(grads[1])


def face_terms(low, high, slab, with_second=True):
    laps, grads = [], []
    for p in range(slab):
        first, second = [], []
        for k in range(1, REACH + 1):
            if p + k >= slab:
                plane = high[p + k - slab]
                first.append(first_coeffs[k - 1] * plane)
                second.append(second_coeffs[k - 1] * plane)
            if p - k < 0:
                plane = low[REACH + p - k]
                first.append(-first_coeffs[k - 1] * plane)
                second.append(second_coeffs[k - 1] * plane)
        zero = jnp.zeros_like(low[0])
        grads.append(total_of(first) if first else zero)
        laps.append(total_of(second) if second else zero)
    return (jnp.stack(laps) if with_second else None), jnp.stack(grads)


def lane_index(slab):
    return lax.broadcasted_iota(jnp.int32, (slab, SUB, LANES), 2)


def columns(depth):
    return [slice(h * LANES, (h + 1) * LANES) for h in range(depth // LANES)]


START, EVEN, FIRST, LAST, PART, OFFSET, OTHERS = range(7)


def pack_kernel(copies, count, info, *refs):
    sources, outs, sems = refs[:count], refs[count:-1], refs[-1]
    started = []
    for number, (source, who, row, out, at) in enumerate(copies):
        begin = info[START] if who == 0 else info[OTHERS + who - 1]
        target = outs[out].at[at]
        rows = pl.ds(pl.multiple_of(begin + row, SUB), target.shape[1])
        copy = pltpu.make_async_copy(sources[source].at[:, rows, :], target, sems.at[number])
        copy.start()
        started.append(copy)
    for copy in started:
        copy.wait()


def slope_kernel(width, info, buoy, s1, s2, s3, scr):
    slab = scr.shape[0]
    pad_rows(scr, lambda row: buoy[:, aligned(info[START] + row), :] - 1.0, width)
    lane = lane_index(slab)

    def body(i, _):
        for h, cols in enumerate(columns(buoy.shape[2])):
            _, _, one, two, three = local_terms(scr, SUB * i, h, lane, False)
            s1[:, aligned(SUB * i), cols] = one
            s2[:, aligned(SUB * i), cols] = two
            s3[:, aligned(SUB * i), cols] = three
        return 0

    lax.fori_loop(0, width // SUB, body, 0)


def local_loop(width, start, depth, buoy, s2, s3, image, along, scr):
    lane = lane_index(scr.shape[0])

    def body(i, _):
        rows = aligned(SUB * i)
        for h, cols in enumerate(columns(depth)):
            _, lap, one, two, three = local_terms(scr, SUB * i, h, lane)
            b = buoy[:, aligned(start + SUB * i), cols]
            image[:, rows, cols] = b * lap + s2[:, rows, cols] * two + s3[:, rows, cols] * three
            along[:, rows, cols] = one
        return 0

    lax.fori_loop(0, width // SUB, body, 0)


def own_kernel(width, info, now, buoy, s2, s3, image, along, scr):
    pad_rows(scr, lambda row: now[:, aligned(info[START] + row), :], width)
    local_loop(width, info[START], now.shape[2], buoy, s2, s3, image, along, scr)


def far_kernel(width, split, info, now_a, now_b, buoy, s2, s3, image, along, whole, scr):
    halves = scr.shape[1]
    zero = jnp.zeros((scr.shape[0], SUB, LANES), jnp.float32)
    for h in range(halves):
        scr[:, h, pl.ds(0, SUB), :] = zero
        scr[:, h, pl.ds(width + SUB, SUB), :] = zero
    for ref, first in ((now_a, 0), (now_b, split)):

        def body(i, _):
            value = ref[0, :, aligned(SUB * i), :]
            whole[:, aligned(first + SUB * i), :] = value
            for h in range(halves):
                scr[:, h, aligned(first + SUB * (i + 1)), :] = value[:, :, h * LANES:(h + 1) * LANES]
            return 0

        lax.fori_loop(0, ref.shape[2] // SUB, body, 0)
    local_loop(width, info[START], buoy.shape[2], buoy, s2, s3, image, along, scr)


def planes_of(ref, index, rows, cols):
    return [ref[index, q, rows, cols] for q in range(REACH)]


def finish_kernel(parts, first_row, count, face_row, again, info, *refs):
    refs = list(refs)

    def take(n):
        got = refs[:n]
        del refs[:n]
        return got

    far = parts - 1
    in_own, out_own = take(2)
    ins, outs = take(far), take(far)
    now_own, before_own, pert_own, stiff, buoy, s1 = take(6)
    nows, pairs = take(far), take(far)
    images, alongs = take(parts), take(parts)
    earlier = take(2 + far) if again else ()
    following, slope, *scales, faces = refs
    start, base, offset = info[START], info[PART], info[OFFSET]
    first, last = info[FIRST] == 1, info[LAST] == 1
    slab, depth = s1.shape[0], s1.shape[2]

    def loop(even):
        def sides(index, inner, inner_rows, outer, outer_rows, cols):
            inside = planes_of(inner, index, inner_rows, cols)
            outside = planes_of(outer, index, outer_rows, cols)
            return (outside, inside) if even else (inside, outside)

        def body(i, _):
            part = aligned(SUB * i)
            rows = aligned(first_row + SUB * i)
            whole = aligned(start + first_row + SUB * i)
            for cols in columns(depth):
                low, high = sides(0, in_own, rows, out_own, part, cols)
                low = [jnp.where(first, 0.0, plane - 1.0) for plane in low]
                high = [jnp.where(last, 0.0, plane - 1.0) for plane in high]
                one = s1[:, rows, cols] + face_terms(low, high, slab, False)[1]
                slope[:, rows, cols] = one
                b, k = buoy[:, whole, cols], stiff[:, whole, cols]
                values = []
                for s in range(parts):
                    if s == 0:
                        low, high = sides(1, in_own, rows, out_own, part, cols)
                    else:
                        low, high = sides(0, ins[s - 1], part, outs[s - 1], part, cols)
                    lap, grad = face_terms(low, high, slab)
                    values.append(images[s][:, rows, cols] + b * lap + one * (alongs[s][:, rows, cols] + grad))
                source = values[0]
                for s in range(1, parts):
                    source = jnp.where(base == s, values[s], source)
                for s in range(parts):
                    if s == 0:
                        now, before = now_own[:, whole, cols], before_own[:, whole, cols]
                        scale = jnp.where(base == 0, 0.0, pert_own[:, whole, cols])
                    else:
                        now, before = nows[s - 1][:, rows, cols], pairs[s - 1][0, :, part, cols]
                        scale = jnp.where(base == s, 0.0, pairs[s - 1][1, :, part, cols])
                        scales[s - 1][:, rows, cols] = scale
                    following[s, :, rows, cols] = 2.0 * now - before + k * values[s] + scale * source
            return 0

        lax.fori_loop(0, count // SUB, body, 0)

    pl.when(info[EVEN] == 1)(lambda: loop(True))
    pl.when(info[EVEN] == 0)(lambda: loop(False))

    def keep(i, _):
        for source, target in zip(earlier, (following, slope, *scales)):
            rows = aligned(SUB * i)
            if len(source.shape) == 4:
                target[:, :, rows, :] = source[:, :, rows, :]
            else:
                target[:, rows, :] = source[:, rows, :]
        return 0

    if again:
        lax.fori_loop(0, first_row // SUB, keep, 0)

    def send(i, _):
        faces[:, :, aligned(SUB * i), :] = following[:, :, aligned(offset + face_row + SUB * i), :]
        return 0

    lax.fori_loop(0, faces.shape[2] // SUB, send, 0)


def start_kernel(parts, width, core, info, *refs):
    field, now_own, pert_own, stiff, buoy, s1, s2, s3 = refs[:8]
    nows, scales = refs[8:8 + parts - 1], refs[8 + parts - 1:8 + 2 * (parts - 1)]
    partial, scrs = refs[8 + 2 * (parts - 1)], refs[9 + 2 * (parts - 1):]
    start, base, offset = info[START], info[PART], info[OFFSET]
    for s in range(parts):
        pad_rows(scrs[s], lambda row, s=s: field[s, :, aligned(row), :], width)
    lane = lane_index(s1.shape[0])

    def body(i, _):
        out = aligned(SUB * i)
        rows = aligned(offset + SUB * i)
        whole = aligned(start + offset + SUB * i)
        for h, cols in enumerate(columns(s1.shape[2])):
            slopes = [ref[:, rows, cols] for ref in (s1, s2, s3)]
            b, k = buoy[:, whole, cols], stiff[:, whole, cols]
            centres, values = [], []
            for s in range(parts):
                centre, lap, one, two, three = local_terms(scrs[s], offset + SUB * i, h, lane)
                centres.append(centre)
                values.append(b * lap + slopes[0] * one + slopes[1] * two + slopes[2] * three)
            source = values[0]
            for s in range(1, parts):
                source = jnp.where(base == s, values[s], source)
            for s in range(parts):
                if s == 0:
                    now = now_own[:, whole, cols]
                    scale = jnp.where(base == 0, 0.0, pert_own[:, whole, cols])
                else:
                    now, scale = nows[s - 1][:, rows, cols], scales[s - 1][:, rows, cols]
                partial[s, :, out, cols] = 2.0 * centres[s] - now + k * values[s] + scale * source
        return 0

    lax.fori_loop(0, core // SUB, body, 0)


def end_kernel(parts, first_row, info, *refs):
    inner, outer, partial, pert_own, stiff, buoy, s1 = refs[:7]
    scales = refs[7:7 + parts - 1]
    own, others = refs[-2:]
    start, base, offset = info[START], info[PART], info[OFFSET]
    slab, depth, count = s1.shape[0], s1.shape[2], inner.shape[2]

    def loop(even):
        low_ref, high_ref = (outer, inner) if even else (inner, outer)

        def body(i, _):
            part = aligned(SUB * i)
            mine = aligned(first_row + SUB * i)
            rows = aligned(offset + first_row + SUB * i)
            whole = aligned(start + offset + first_row + SUB * i)
            for cols in columns(depth):
                b, k, one = buoy[:, whole, cols], stiff[:, whole, cols], s1[:, rows, cols]
                values = []
                for s in range(parts):
                    lap, grad = face_terms(
                        planes_of(low_ref, s, part, cols), planes_of(high_ref, s, part, cols), slab
                    )
                    values.append(b * lap + one * grad)
                source = values[0]
                for s in range(1, parts):
                    source = jnp.where(base == s, values[s], source)
                for s in range(parts):
                    if s == 0:
                        scale = jnp.where(base == 0, 0.0, pert_own[:, whole, cols])
                    else:
                        scale = scales[s - 1][:, rows, cols]
                    value = partial[s, :, mine, cols] + k * values[s] + scale * source
                    if s == 0:
                        own[:, part, cols] = value
                    else:
                        others[s - 1, :, part, cols] = value
            return 0

        lax.fori_loop(0, count // SUB, body, 0)

    pl.when(info[EVEN] == 1)(lambda: loop(True))
    pl.when(info[EVEN] == 0)(lambda: loop(False))


def call(kernel, info, args, outs, scratch=(), flops=0, space=None):
    vmem = pl.BlockSpec(memory_space=pltpu.VMEM)
    source = pl.BlockSpec(memory_space=space or pltpu.VMEM)
    outs = [jax.ShapeDtypeStruct(o, jnp.float32) for o in outs]
    size = flops = 1024 if TINY else sum(4 * a.size for a in args) + sum(4 * o.size for o in outs)
    return pl.pallas_call(
        kernel,
        name=kernel.func.__name__,
        out_shape=outs,
        in_specs=[pl.BlockSpec(memory_space=pltpu.SMEM)] + [source] * len(args),
        out_specs=[vmem] * len(outs),
        scratch_shapes=list(scratch),
        compiler_params=pltpu.CompilerParams(vmem_limit_bytes=12 << 20),
        cost_estimate=pl.CostEstimate(flops=flops, bytes_accessed=size, transcendentals=0),
    )(info, *args)


def lay_kernel(count, rows, *refs):
    pieces, result, sems = refs[:count], refs[-2], refs[-1]
    copies = []
    for number, piece in enumerate(pieces):
        target = result.at[:, pl.ds(pl.multiple_of(rows[number], SUB), piece.shape[1]), :]
        copy = pltpu.make_async_copy(piece, target, sems.at[number])
        copy.start()
        copies.append(copy)
    for copy in copies:
        copy.wait()


def lay(pieces, result, shape):
    rows = jnp.stack([row for row, _ in pieces]).astype(jnp.int32)
    pieces = [piece for _, piece in pieces]
    hbm = pl.BlockSpec(memory_space=pltpu.HBM)
    given = [] if result is None else [result]
    return pl.pallas_call(
        functools.partial(lay_kernel, len(pieces)),
        name="lay_kernel",
        out_shape=jax.ShapeDtypeStruct(shape, jnp.float32),
        in_specs=[pl.BlockSpec(memory_space=pltpu.SMEM)]
        + [pl.BlockSpec(memory_space=pltpu.VMEM)] * len(pieces)
        + [hbm] * len(given),
        out_specs=hbm,
        scratch_shapes=[pltpu.SemaphoreType.DMA((len(pieces),))],
        input_output_aliases={1 + len(pieces): 0} if given else {},
        compiler_params=pltpu.CompilerParams(vmem_limit_bytes=12 << 20),
    )(rows, *pieces, *given)


def after(value, *others):
    return lax.optimization_barrier((value, *others))[0]


def on_device(field_before, field_now, stiffness, buoyancy, perturbation):
    parts, count = lax.axis_size("probe"), lax.axis_size("space")
    part, place = lax.axis_index("probe"), lax.axis_index("space")
    before, now, pert = field_before[0], field_now[0], perturbation[0]
    slab, height, depth = now.shape
    far = parts - 1
    core = height // parts
    rim = 2 * REACH
    width = min(height, core + (2 if parts > 2 else 1) * rim)
    half = SUB * (core // SUB * HALF[0] // HALF[1])
    halves = (half, core - half)
    split = half + width - core
    chunks = (split, width - split)

    def window(p):
        return jnp.clip(core * p - rim, 0, height - width)

    even = place % 2 == 0
    info = jnp.stack(
        [window(part), even, place == 0, place == count - 1, part, core * part - window(part)]
        + [window((part + s) % parts) for s in range(1, parts)]
    ).astype(jnp.int32)

    inner_pairs = [(i, i ^ 1) for i in range(count)]
    outer_pairs = [(i, ((i + 1) ^ 1) - 1) for i in range(1, count - 1)]

    def swap(stack, pairs, from_end):
        if slab > REACH:
            stack = lax.dynamic_slice_in_dim(stack, jnp.where(from_end, slab - REACH, 0), REACH, axis=1)
        return lax.ppermute(stack, "space", pairs)

    def inside(stack):
        return swap(stack, inner_pairs, even)

    def outside(stack):
        return swap(stack, outer_pairs, jnp.logical_not(even))

    def turn(field, s):
        return lax.ppermute(field, "probe", [(i, (i + s) % parts) for i in range(parts)])

    def run_pack(args, copies, outs):
        return call(
            functools.partial(pack_kernel, tuple(copies), len(args)),
            info,
            args,
            outs,
            [pltpu.SemaphoreType.DMA((len(copies),))],
            space=pltpu.HBM,
        )

    spans = ((0, split), (split, width - split))
    copies, outs = [], []
    for span in ((0, width),) + spans:
        for f in range(2):
            copies.append((f, 0, span[0], len(outs), f))
        outs.append((2, slab, span[1], depth))
    for s in range(1, parts):
        for span in spans:
            copies.append((1, s, span[0], len(outs), 0))
            outs.append((1, slab, span[1], depth))
    face, face_a, face_b, *turning = run_pack(
        [pltpu.with_memory_space_constraint(field, pltpu.HBM) for field in (buoyancy, now)], copies, outs
    )

    out_own = [outside(face_a)]
    in_own = inside(face)
    nows = [[turn(turning[2 * (s - 1) + c], s) for s in range(1, parts)] for c in range(2)]
    out_own.append(outside(after(face_b, *nows[0])))

    scr = pltpu.VMEM((slab, depth // LANES, width + 2 * SUB, LANES), jnp.float32)
    wide = (slab, width, depth)
    cells = slab * width * depth
    s1, s2, s3 = call(functools.partial(slope_kernel, width), info, (after(buoyancy, in_own),), [wide] * 3, [scr], 33 * cells)

    copies, outs = [], []
    for s in range(1, parts):
        for span in spans:
            for f in range(2):
                copies.append((f, s, span[0], len(outs), f))
            outs.append((2, slab, span[1], depth))
    packed = run_pack((after(before, *nows[0]), pert), copies, outs)
    pairs = [[turn(packed[2 * (s - 1)], s) for s in range(1, parts)]]

    image, along = call(
        functools.partial(own_kernel, width), info, (now, buoyancy, s2, s3), [wide] * 2, [scr], 60 * cells
    )
    images, alongs = [image], [along]

    sent = nows[0]
    out_far = [[outside(field) for field in sent]]
    in_far = [[inside(field) for field in sent]]
    wholes = []
    for s in range(1, parts):
        image, along, whole = call(
            functools.partial(far_kernel, width, split),
            info,
            (nows[0][s - 1], nows[1][s - 1], buoyancy, s2, s3),
            [wide] * 3,
            [scr],
            60 * cells,
        )
        images.append(image)
        alongs.append(along)
        wholes.append(whole)
    sent = [after(field, images[-1]) for field in nows[1]]
    out_far.append([outside(field) for field in sent])
    in_far.append([inside(field) for field in sent])
    pairs.append([turn(after(packed[2 * (s - 1) + 1], images[-1]), s) for s in range(1, parts)])

    carried = ()
    faces = []
    for c in range(2):
        args = (
            [in_own, out_own[c]] + in_far[c] + out_far[c] + [now, before, pert, stiffness, buoyancy, s1]
            + wholes + pairs[c] + images + alongs
        )
        outs = [(parts, slab, width, depth), wide] + [wide] * far
        *carried, face = call(
            functools.partial(finish_kernel, parts, spans[c][0], spans[c][1], c * half, c == 1),
            info,
            (*args, *carried),
            outs + [(parts, slab, halves[c], depth)],
            (),
            45 * parts * spans[c][1] * slab * depth,
        )
        faces.append(face)
    following, slope, *scales = carried

    out_ends = [outside(face) for face in faces]
    in_ends = [inside(face) for face in faces]
    (partial,) = call(
        functools.partial(start_kernel, parts, width, core),
        info,
        (following, now, pert, stiffness, buoyancy, slope, s2, s3, *wholes, *scales),
        [(parts, slab, core, depth)],
        [scr] * parts,
        70 * parts * cells,
    )
    pieces = []
    for c in range(2):
        own, others = call(
            functools.partial(end_kernel, parts, c * half),
            info,
            (in_ends[c], out_ends[c], partial, pert, stiffness, buoyancy, slope, *scales),
            [(slab, halves[c], depth), (far, slab, halves[c], depth)],
            (),
            25 * parts * slab * halves[c] * depth,
        )
        pieces.append((core * part + c * half, own))
        for s in range(1, parts):
            row = core * ((part + s) % parts) + c * half
            pieces.append((row, turn(others[s - 1], parts - s)))
    result = lay(pieces[:-far], None, now.shape)
    result = lay(pieces[-far:], result, now.shape)
    return result[None]


def solution(mesh):
    placed = (
        P("probe", "space", None, None),
        P("probe", "space", None, None),
        P("space", None, None),
        P("space", None, None),
        P("probe", "space", None, None),
    )
    return jax.shard_map(
        on_device,
        mesh=mesh,
        in_specs=placed,
        out_specs=P("probe", "space", None, None),
        check_vma=False,
    )
```

time: 317 us -> 77.5 us (0.24)
  waiting for transfers between devices: 186 us -> 21.6 us
  other arithmetic: 92.8 us -> 0.08 us
  Pallas kernels: 0 us -> 27.1 us
  between operations: 13.5 us -> 0.22 us
  starting transfers between devices: 17 us -> 27.7 us
  local copies, waits for them, and re-layouts: 6.93 us -> 0.11 us
    ppermute x6 -> x17, waiting for transfers between devices: 104 us -> 21.6 us  [the longest x6 12.6 us: turn(): lax.ppermute(field, 'probe', [(i, (i + s) % parts) for i in range(parts)])]
    psum x2 -> x0, waiting for transfers between devices: 81.6 us -> none  [spread(): return lax.psum(block, axis)]
    select_n x2 -> x0, other arithmetic: 47.6 us -> none  [spread(): jnp.where(lax.axis_index(axis) == owner, block, jnp.zeros_like(block))]
    pallas_call x0 -> x12, Pallas kernels: none -> 27.1 us  [the longest x10 24.9 us: call(): pl.pallas_call(kernel, name=kernel.func.__name__, out_shape=outs, in_spec...]
    broadcast_in_dim x1 -> x0, other arithmetic: 25.3 us -> none  [on_device(): return now[None]]
    concatenate x5 -> x0, other arithmetic: 14.4 us -> none  [with_halo(): block = jnp.concatenate([low, block, high], axis=dim)]
    ppermute x6 -> x17, starting transfers between devices: 17 us -> 27.7 us  [the longest x11 21.2 us: swap(): return lax.ppermute(stack, 'space', pairs)]
    squeeze x2 -> x0, local copies, waits for them, and re-layouts: 6.56 us -> none  [on_device(): own_term = operate(both[1])]
  transfers between devices with their start and end apart: 8 -> 17, of which waited for: 4 -> 8; matrix products, arithmetic and copies ran while one was open for 2% -> 0% of each run, Pallas kernels for 0% -> 31%
where the time goes in v2:
time: 77.5 us; the launch traced here: 76.8 us
  starting transfers between devices  27.7 us (36%)
  Pallas kernels  27.1 us (35%)
  waiting for transfers between devices  21.6 us (28%)
    pallas_call x10, Pallas kernels, call(): pl.pallas_call(kernel, name=kernel.func.__name__, out_shape=outs, in_spec...  24.9 us
    ppermute x11, starting transfers between devices, swap(): return lax.ppermute(stack, 'space', pairs)  21.2 us
    ppermute x6, waiting for transfers between devices, turn(): lax.ppermute(field, 'probe', [(i, (i + s) % parts) for i in range(parts)])  12.6 us
    ppermute x11, waiting for transfers between devices, swap(): return lax.ppermute(stack, 'space', pairs)  9.08 us
    ppermute x6, starting transfers between devices, turn(): lax.ppermute(field, 'probe', [(i, (i + s) % parts) for i in range(parts)])  6.48 us
    pallas_call x2, Pallas kernels, lay(): pl.pallas_call(functools.partial(lay_kernel, len(pieces)), name='lay_kern...  2.15 us
  transfers between devices with their start and end apart: 17, of which 8 were waited for; matrix products, arithmetic and copies ran while one was open for 0% of the time, Pallas kernels for 31%

profile of v2, /device:TPU:4, one launch (start us, length us, event | category | flops | bytes accessed | tf_op | source)
XLA Modules:
  0.0 76.8 jit_solution(10789471583517731272)
XLA Ops:
  0.0 0.1 stack.59.info
  0.1 2.4 %pack_kernel.2 = (f32[2,4,136,256]{3,2,1,0:T(8,128)S(1)}, f32[2,4,72,256]{3,2,1,0:T(8,128)S(1)}, f32[2,4,64,256]{3,2,1,0:T(8,128)S(1)}, f32[1,4,72,256]{3,2,1,0:T(8,128)S(1)}, f32[1,4,64,256]{3,2,1,0:T(8,128)S(1)}) custom-call(s32[7]{0:T(128)S(1)} %stack.59.info, f32[4,256,256]{2,1,0:T(8,128)} %refs_5_.3, f32[4,256,256]{2,1,0:T(8,128)} %bitcast.23), custom_call_target="tpu_custom_call" | custom-call | flops 1024 | bytes 1024 | tf_op jit(solution)/shard_map/pack_kernel/pallas_call | solution.py:365
  2.5 0.0 copy-start
  2.5 0.1 collective-permute-start
  2.6 1.7 %collective-permute-start.1 = (f32[1,4,72,256]{3,2,1,0:T(8,128)S(1)}, f32[1,4,72,256]{3,2,1,0:T(8,128)S(1)}, u32[]{:S(2)}, u32[]{:S(2)}) collective-permute-start(f32[1,4,72,256]{3,2,1,0:T(8,128)S(1)} %get-tuple-element.39), channel_id=1, source_target_pairs={{0,16},{16,0},{1,17},{17,1},{2,18},{18,2},{3,19},{19,3},{4,20},{20... | collective-permute-start | bytes 884744 | tf_op jit(solution)/shard_map/ppermute | solution.py:450
  4.3 2.2 %collective-permute-start.7 = (f32[2,4,72,256]{3,2,1,0:T(8,128)S(1)}, f32[2,4,72,256]{3,2,1,0:T(8,128)S(1)}, u32[]{:S(2)}, u32[]{:S(2)}) collective-permute-start(f32[2,4,72,256]{3,2,1,0:T(8,128)S(1)} %get-tuple-element.55), channel_id=1, source_target_pairs={{1,2},{2,1},{3,4},{4,3},{5,6},{6,5},{7,8},{8,7},{9,10},{10,9},{11,... | collective-permute-start | bytes 1769480 | tf_op jit(solution)/shard_map/ppermute | solution.py:441
  6.4 5.6 %collective-permute-done.1.now_a = f32[1,4,72,256]{3,2,1,0:T(8,128)S(1)} collective-permute-done((f32[1,4,72,256]{3,2,1,0:T(8,128)S(1)}, f32[1,4,72,256]{3,2,1,0:T(8,128)S(1)}, u32[]{:S(2)}, u32[]{:S(2)}) %collective-permute-start.1) | collective-permute-done | bytes 294944 | tf_op jit(solution)/shard_map/ppermute | solution.py:450
  12.0 1.9 %collective-permute-start.9 = (f32[1,4,72,256]{3,2,1,0:T(8,128)S(1)}, f32[1,4,72,256]{3,2,1,0:T(8,128)S(1)}, u32[]{:S(2)}, u32[]{:S(2)}) collective-permute-start(f32[1,4,72,256]{3,2,1,0:T(8,128)S(1)} %collective-permute-done.1.now_a), channel_id=1, source_target_pairs={{1,2},{2,1},{3,4},{4,3},{5,6},{6,5},{7,8},{8,7},{9,10},{10,9},{11,... | collective-permute-start | bytes 884744 | tf_op jit(solution)/shard_map/ppermute | solution.py:441
  13.9 1.7 %collective-permute-start.3 = (f32[1,4,64,256]{3,2,1,0:T(8,128)S(1)}, f32[1,4,64,256]{3,2,1,0:T(8,128)S(1)}, u32[]{:S(2)}, u32[]{:S(2)}) collective-permute-start(f32[1,4,64,256]{3,2,1,0:T(8,128)S(1)} %get-tuple-element.41), channel_id=1, source_target_pairs={{0,16},{16,0},{1,17},{17,1},{2,18},{18,2},{3,19},{19,3},{4,20},{20... | collective-permute-start | bytes 786440 | tf_op jit(solution)/shard_map/ppermute | solution.py:450
  15.6 0.7 pack_kernel.3
  16.3 0.5 collective-permute-start.10
  16.8 0.0 collective-permute-done.refs_0_
  16.8 1.1 %collective-permute-start.8 = (f32[1,4,72,256]{3,2,1,0:T(8,128)S(1)}, f32[1,4,72,256]{3,2,1,0:T(8,128)S(1)}, u32[]{:S(2)}, u32[]{:S(2)}) collective-permute-start(f32[1,4,72,256]{3,2,1,0:T(8,128)S(1)} %collective-permute-done.1.now_a), channel_id=1, source_target_pairs={{0,1},{1,0},{2,3},{3,2},{4,5},{5,4},{6,7},{7,6},{8,9},{9,8},{10,11... | collective-permute-start | bytes 884744 | tf_op jit(solution)/shard_map/ppermute | solution.py:441
  17.9 3.6 %slope_kernel.1 = (f32[4,136,256]{2,1,0:T(8,128)S(1)}, f32[4,136,256]{2,1,0:T(8,128)S(1)}, f32[4,136,256]{2,1,0:T(8,128)S(1)}) custom-call(s32[7]{0:T(128)S(1)} %stack.59.info, f32[4,256,256]{2,1,0:T(8,128)S(1)} %copy-done), custom_call_target="tpu_custom_call" | custom-call | flops 1024 | bytes 1024 | tf_op jit(solution)/shard_map/slope_kernel/pallas_call | solution.py:365
  21.5 1.1 %collective-permute-done.3.now_b = f32[1,4,64,256]{3,2,1,0:T(8,128)S(1)} collective-permute-done((f32[1,4,64,256]{3,2,1,0:T(8,128)S(1)}, f32[1,4,64,256]{3,2,1,0:T(8,128)S(1)}, u32[]{:S(2)}, u32[]{:S(2)}) %collective-permute-start.3) | collective-permute-done | bytes 262176 | tf_op jit(solution)/shard_map/ppermute | solution.py:450
  22.6 3.4 %collective-permute-start.2 = (f32[2,4,64,256]{3,2,1,0:T(8,128)S(1)}, f32[2,4,64,256]{3,2,1,0:T(8,128)S(1)}, u32[]{:S(2)}, u32[]{:S(2)}) collective-permute-start(f32[2,4,64,256]{3,2,1,0:T(8,128)S(1)} %get-tuple-element.40), channel_id=1, source_target_pairs={{1,2},{2,1},{3,4},{4,3},{5,6},{6,5},{7,8},{8,7},{9,10},{10,9},{11,... | collective-permute-start | bytes 1572872 | tf_op jit(solution)/shard_map/ppermute | solution.py:441
  26.0 0.0 copy-start.3
  26.0 3.8 %far_kernel.1 = (f32[4,136,256]{2,1,0:T(8,128)S(1)}, f32[4,136,256]{2,1,0:T(8,128)S(1)}, f32[4,136,256]{2,1,0:T(8,128)S(1)}) custom-call(s32[7]{0:T(128)S(1)} %stack.59.info, f32[1,4,72,256]{3,2,1,0:T(8,128)S(1)} %collective-permute-done.1.now_a, f32[1,4,64,256]{3,2,1,0:T(8,128)S(1)} %collective-permute-done.3.now_b, f32[4,256,256]{2,1,0:T(8,128)S(1)} %copy-done, ...), custom_call_target="tpu_custom_call" | custom-call | flops 1024 | bytes 1024 | tf_op jit(solution)/shard_map/far_kernel/pallas_call | solution.py:365
  29.8 0.0 copy-start.2
  29.8 0.0 collective-permute-done.9.refs_3_
  29.8 1.7 %collective-permute-start.6 = (f32[2,4,64,256]{3,2,1,0:T(8,128)S(1)}, f32[2,4,64,256]{3,2,1,0:T(8,128)S(1)}, u32[]{:S(2)}, u32[]{:S(2)}) collective-permute-start(f32[2,4,64,256]{3,2,1,0:T(8,128)S(1)} %get-tuple-element.51), channel_id=1, source_target_pairs={{0,16},{16,0},{1,17},{17,1},{2,18},{18,2},{3,19},{19,3},{4,20},{20... | collective-permute-start | bytes 1572872 | tf_op jit(solution)/shard_map/ppermute | solution.py:450
  31.5 0.0 collective-permute-done.8.refs_2_
  31.5 1.9 %collective-permute-start.5 = (f32[1,4,64,256]{3,2,1,0:T(8,128)S(1)}, f32[1,4,64,256]{3,2,1,0:T(8,128)S(1)}, u32[]{:S(2)}, u32[]{:S(2)}) collective-permute-start(f32[1,4,64,256]{3,2,1,0:T(8,128)S(1)} %collective-permute-done.3.now_b), channel_id=1, source_target_pairs={{1,2},{2,1},{3,4},{4,3},{5,6},{6,5},{7,8},{8,7},{9,10},{10,9},{11,... | collective-permute-start | bytes 786440 | tf_op jit(solution)/shard_map/ppermute | solution.py:441
  33.4 2.5 %collective-permute-start.4 = (f32[1,4,64,256]{3,2,1,0:T(8,128)S(1)}, f32[1,4,64,256]{3,2,1,0:T(8,128)S(1)}, u32[]{:S(2)}, u32[]{:S(2)}) collective-permute-start(f32[1,4,64,256]{3,2,1,0:T(8,128)S(1)} %collective-permute-done.3.now_b), channel_id=1, source_target_pairs={{0,1},{1,0},{2,3},{3,2},{4,5},{5,4},{6,7},{7,6},{8,9},{9,8},{10,11... | collective-permute-start | bytes 786440 | tf_op jit(solution)/shard_map/ppermute | solution.py:441
  35.9 3.8 %own_kernel.1 = (f32[4,136,256]{2,1,0:T(8,128)S(1)}, f32[4,136,256]{2,1,0:T(8,128)S(1)}) custom-call(s32[7]{0:T(128)S(1)} %stack.59.info, f32[4,256,256]{2,1,0:T(8,128)S(1)} %bitcast.24, f32[4,256,256]{2,1,0:T(8,128)S(1)} %copy-done, f32[4,136,256]{2,1,0:T(8,128)S(1)} %get-tuple-element.43.s2.refs_6_, f32[4,136,256]{2,1,0:T(8,128)S(1)} %get-tuple-element.44.s3.refs_7_), custom_call_target="tpu_custom_call" | custom-call | flops 1024 | bytes 1024 | tf_op jit(solution)/shard_map/own_kernel/pallas_call | solution.py:365
  39.7 0.0 collective-permute-done.10.refs_11_
  39.7 1.5 %finish_kernel.2 = (f32[2,4,136,256]{3,2,1,0:T(8,128)S(1)}, f32[4,136,256]{2,1,0:T(8,128)S(1)}, f32[4,136,256]{2,1,0:T(8,128)S(1)}, f32[2,4,64,256]{3,2,1,0:T(8,128)S(1)}) custom-call(s32[7]{0:T(128)S(1)} %stack.59.info, f32[2,4,136,256]{3,2,1,0:T(8,128)S(1)} %collective-permute-done.refs_0_, f32[2,4,72,256]{3,2,1,0:T(8,128)S(1)} %collective-permute-done.7.refs_1_, ...), custom_call_target="tpu_custom_call" | custom-call | flops 1024 | bytes 1024 | tf_op jit(solution)/shard_map/finish_kernel/pallas_call | solution.py:365
  41.2 1.9 %collective-permute-start.15 = (f32[2,4,64,256]{3,2,1,0:T(8,128)S(1)}, f32[2,4,64,256]{3,2,1,0:T(8,128)S(1)}, u32[]{:S(2)}, u32[]{:S(2)}) collective-permute-start(f32[2,4,64,256]{3,2,1,0:T(8,128)S(1)} %get-tuple-element.65), channel_id=1, source_target_pairs={{1,2},{2,1},{3,4},{4,3},{5,6},{6,5},{7,8},{8,7},{9,10},{10,9},{11,... | collective-permute-start | bytes 1572872 | tf_op jit(solution)/shard_map/ppermute | solution.py:441
  43.1 1.4 %collective-permute-start.14 = (f32[2,4,64,256]{3,2,1,0:T(8,128)S(1)}, f32[2,4,64,256]{3,2,1,0:T(8,128)S(1)}, u32[]{:S(2)}, u32[]{:S(2)}) collective-permute-start(f32[2,4,64,256]{3,2,1,0:T(8,128)S(1)} %get-tuple-element.65), channel_id=1, source_target_pairs={{0,1},{1,0},{2,3},{3,2},{4,5},{5,4},{6,7},{7,6},{8,9},{9,8},{10,11... | collective-permute-start | bytes 1572872 | tf_op jit(solution)/shard_map/ppermute | solution.py:441
  44.5 0.4 collective-permute-done.5.refs_3_
  44.9 0.0 collective-permute-done.4.refs_2_
  45.0 1.5 %collective-permute-done.6.refs_11_ = f32[2,4,64,256]{3,2,1,0:T(8,128)S(1)} collective-permute-done((f32[2,4,64,256]{3,2,1,0:T(8,128)S(1)}, f32[2,4,64,256]{3,2,1,0:T(8,128)S(1)}, u32[]{:S(2)}, u32[]{:S(2)}) %collective-permute-start.6) | collective-permute-done | bytes 524320 | tf_op jit(solution)/shard_map/ppermute | solution.py:450
  46.4 1.5 %finish_kernel.3 = (f32[2,4,136,256]{3,2,1,0:T(8,128)S(1)}, f32[4,136,256]{2,1,0:T(8,128)S(1)}, f32[4,136,256]{2,1,0:T(8,128)S(1)}, f32[2,4,64,256]{3,2,1,0:T(8,128)S(1)}) custom-call(s32[7]{0:T(128)S(1)} %stack.59.info, f32[2,4,136,256]{3,2,1,0:T(8,128)S(1)} %collective-permute-done.refs_0_, f32[2,4,64,256]{3,2,1,0:T(8,128)S(1)} %collective-permute-done.2.refs_1_, ...), custom_call_target="tpu_custom_call" | custom-call | flops 1024 | bytes 1024 | tf_op jit(solution)/shard_map/finish_kernel/pallas_call | solution.py:365
  48.0 1.9 %collective-permute-start.12 = (f32[2,4,64,256]{3,2,1,0:T(8,128)S(1)}, f32[2,4,64,256]{3,2,1,0:T(8,128)S(1)}, u32[]{:S(2)}, u32[]{:S(2)}) collective-permute-start(f32[2,4,64,256]{3,2,1,0:T(8,128)S(1)} %get-tuple-element.60), channel_id=1, source_target_pairs={{1,2},{2,1},{3,4},{4,3},{5,6},{6,5},{7,8},{8,7},{9,10},{10,9},{11,... | collective-permute-start | bytes 1572872 | tf_op jit(solution)/shard_map/ppermute | solution.py:441
  49.9 2.9 %collective-permute-start.11 = (f32[2,4,64,256]{3,2,1,0:T(8,128)S(1)}, f32[2,4,64,256]{3,2,1,0:T(8,128)S(1)}, u32[]{:S(2)}, u32[]{:S(2)}) collective-permute-start(f32[2,4,64,256]{3,2,1,0:T(8,128)S(1)} %get-tuple-element.60), channel_id=1, source_target_pairs={{0,1},{1,0},{2,3},{3,2},{4,5},{5,4},{6,7},{7,6},{8,9},{9,8},{10,11... | collective-permute-start | bytes 1572872 | tf_op jit(solution)/shard_map/ppermute | solution.py:441
  52.8 5.5 %start_kernel.1.refs_2_ = f32[2,4,128,256]{3,2,1,0:T(8,128)S(1)} custom-call(s32[7]{0:T(128)S(1)} %stack.59.info, f32[2,4,136,256]{3,2,1,0:T(8,128)S(1)} %get-tuple-element.61.refs_0_, f32[4,256,256]{2,1,0:T(8,128)S(1)} %bitcast.27, f32[4,256,256]{2,1,0:T(8,128)S(1)} %bitcast.20, f32[4,256,256]{2,1,0:T(8,128)S(1)} %copy-done.2, f32[4,256,256]{2,1,0:T(8,128)S(1)} %copy-done, ...), custom_call_target="tpu_custom_call" | custom-call | flops 1024 | bytes 1024 | tf_op jit(solution)/shard_map/start_kernel/pallas_call | solution.py:365
  58.4 4.5 %collective-permute-done.15.refs_1_ = f32[2,4,64,256]{3,2,1,0:T(8,128)S(1)} collective-permute-done((f32[2,4,64,256]{3,2,1,0:T(8,128)S(1)}, f32[2,4,64,256]{3,2,1,0:T(8,128)S(1)}, u32[]{:S(2)}, u32[]{:S(2)}) %collective-permute-start.15) | collective-permute-done | bytes 524320 | tf_op jit(solution)/shard_map/ppermute | solution.py:441
  62.9 0.0 collective-permute-done.14.refs_0_
  62.9 1.1 %end_kernel.3 = (f32[4,64,256]{2,1,0:T(8,128)S(1)}, f32[1,4,64,256]{3,2,1,0:T(8,128)S(1)}) custom-call(s32[7]{0:T(128)S(1)} %stack.59.info, f32[2,4,64,256]{3,2,1,0:T(8,128)S(1)} %collective-permute-done.14.refs_0_, f32[2,4,64,256]{3,2,1,0:T(8,128)S(1)} %collective-permute-done.15.refs_1_, f32[2,4,128,256]{3,2,1,0:T(8,128)S(1)} %start_kernel.1.refs_2_, ...), custom_call_target="tpu_custom_call" | custom-call | flops 1024 | bytes 1024 | tf_op jit(solution)/shard_map/end_kernel/pallas_call | solution.py:365
  64.0 0.5 collective-permute-start.16
  64.5 4.1 %collective-permute-done.12.refs_1_ = f32[2,4,64,256]{3,2,1,0:T(8,128)S(1)} collective-permute-done((f32[2,4,64,256]{3,2,1,0:T(8,128)S(1)}, f32[2,4,64,256]{3,2,1,0:T(8,128)S(1)}, u32[]{:S(2)}, u32[]{:S(2)}) %collective-permute-start.12) | collective-permute-done | bytes 524320 | tf_op jit(solution)/shard_map/ppermute | solution.py:441
  68.5 1.1 %end_kernel.2 = (f32[4,64,256]{2,1,0:T(8,128)S(1)}, f32[1,4,64,256]{3,2,1,0:T(8,128)S(1)}) custom-call(s32[7]{0:T(128)S(1)} %stack.59.info, f32[2,4,64,256]{3,2,1,0:T(8,128)S(1)} %collective-permute-done.11.refs_0_, f32[2,4,64,256]{3,2,1,0:T(8,128)S(1)} %collective-permute-done.12.refs_1_, f32[2,4,128,256]{3,2,1,0:T(8,128)S(1)} %start_kernel.1.refs_2_, ...), custom_call_target="tpu_custom_call" | custom-call | flops 1024 | bytes 1024 | tf_op jit(solution)/shard_map/end_kernel/pallas_call | solution.py:365
  69.6 0.5 collective-permute-start.13
  70.1 0.1 pad_add_fusion.rows
  70.2 0.4 collective-permute-done.16.refs_1_
  70.6 1.4 %lay_kernel.2.refs_1_ = f32[4,256,256]{2,1,0:T(8,128)} custom-call(s32[3]{0:T(128)S(1)} %pad_add_fusion.rows, f32[4,64,256]{2,1,0:T(8,128)S(1)} %get-tuple-element.66.refs_0_, f32[4,64,256]{2,1,0:T(8,128)S(1)} %collective-permute-done.16.refs_1_, f32[4,64,256]{2,1,0:T(8,128)S(1)} %get-tuple-element.68.refs_2_), custom_call_target="tpu_custom_call" | custom-call | tf_op jit(solution)/shard_map/lay_kernel/pallas_call | solution.py:394
  72.0 4.0 %collective-permute-done.13.refs_0_ = f32[4,64,256]{2,1,0:T(8,128)S(1)} collective-permute-done((f32[4,64,256]{2,1,0:T(8,128)S(1)}, f32[4,64,256]{2,1,0:T(8,128)S(1)}, u32[]{:S(2)}, u32[]{:S(2)}) %collective-permute-start.13) | collective-permute-done | bytes 262176 | tf_op jit(solution)/shard_map/ppermute | solution.py:450
  76.1 0.7 lay_kernel.3
  (10 shorter events, 0.0 us)
Async XLA Ops:
  0.0 15.6 %copy-start.4 = (f32[1,4,256,256]{3,2,1,0:T(8,128)S(1)}, f32[1,4,256,256]{3,2,1,0:T(8,128)}, u32[]{:S(2)}) copy-start(f32[1,4,256,256]{3,2,1,0:T(8,128)} %param.5) | copy-start | bytes 3145732
  0.0 15.6 %copy-start.1 = (f32[1,4,256,256]{3,2,1,0:T(8,128)S(1)}, f32[1,4,256,256]{3,2,1,0:T(8,128)}, u32[]{:S(2)}) copy-start(f32[1,4,256,256]{3,2,1,0:T(8,128)} %param.9) | copy-start | bytes 3145732
  2.5 15.4 %copy-start = (f32[4,256,256]{2,1,0:T(8,128)S(1)}, f32[4,256,256]{2,1,0:T(8,128)}, u32[]{:S(2)}) copy-start(f32[4,256,256]{2,1,0:T(8,128)} %refs_5_.3) | copy-start | bytes 3145732
  2.5 14.3 %collective-permute-start = (f32[2,4,136,256]{3,2,1,0:T(8,128)S(1)}, f32[2,4,136,256]{3,2,1,0:T(8,128)S(1)}, u32[]{:S(2)}, u32[]{:S(2)}) collective-permute-start(f32[2,4,136,256]{3,2,1,0:T(8,128)S(1)} %get-tuple-element.37), channel_id=1, source_target_pairs={{0,1},{1,0},{2,3},{3,2},{4,5},{5,4},{6,7},{7,6},{8,9},{9,8},{10,11... | collective-permute-start | bytes 3342344 | tf_op jit(solution)/shard_map/ppermute | solution.py:441
  2.6 9.4 %collective-permute-start.1 = (f32[1,4,72,256]{3,2,1,0:T(8,128)S(1)}, f32[1,4,72,256]{3,2,1,0:T(8,128)S(1)}, u32[]{:S(2)}, u32[]{:S(2)}) collective-permute-start(f32[1,4,72,256]{3,2,1,0:T(8,128)S(1)} %get-tuple-element.39), channel_id=1, source_target_pairs={{0,16},{16,0},{1,17},{17,1},{2,18},{18,2},{3,19},{19,3},{4,20},{20... | collective-permute-start | bytes 884744 | tf_op jit(solution)/shard_map/ppermute | solution.py:450
  4.3 29.2 %collective-permute-start.7 = (f32[2,4,72,256]{3,2,1,0:T(8,128)S(1)}, f32[2,4,72,256]{3,2,1,0:T(8,128)S(1)}, u32[]{:S(2)}, u32[]{:S(2)}) collective-permute-start(f32[2,4,72,256]{3,2,1,0:T(8,128)S(1)} %get-tuple-element.55), channel_id=1, source_target_pairs={{1,2},{2,1},{3,4},{4,3},{5,6},{6,5},{7,8},{8,7},{9,10},{10,9},{11,... | collective-permute-start | bytes 1769480 | tf_op jit(solution)/shard_map/ppermute | solution.py:441
  12.0 17.8 %collective-permute-start.9 = (f32[1,4,72,256]{3,2,1,0:T(8,128)S(1)}, f32[1,4,72,256]{3,2,1,0:T(8,128)S(1)}, u32[]{:S(2)}, u32[]{:S(2)}) collective-permute-start(f32[1,4,72,256]{3,2,1,0:T(8,128)S(1)} %collective-permute-done.1.now_a), channel_id=1, source_target_pairs={{1,2},{2,1},{3,4},{4,3},{5,6},{6,5},{7,8},{8,7},{9,10},{10,9},{11,... | collective-permute-start | bytes 884744 | tf_op jit(solution)/shard_map/ppermute | solution.py:441
  13.9 8.6 %collective-permute-start.3 = (f32[1,4,64,256]{3,2,1,0:T(8,128)S(1)}, f32[1,4,64,256]{3,2,1,0:T(8,128)S(1)}, u32[]{:S(2)}, u32[]{:S(2)}) collective-permute-start(f32[1,4,64,256]{3,2,1,0:T(8,128)S(1)} %get-tuple-element.41), channel_id=1, source_target_pairs={{0,16},{16,0},{1,17},{17,1},{2,18},{18,2},{3,19},{19,3},{4,20},{20... | collective-permute-start | bytes 786440 | tf_op jit(solution)/shard_map/ppermute | solution.py:450
  16.3 23.4 %collective-permute-start.10 = (f32[2,4,72,256]{3,2,1,0:T(8,128)S(1)}, f32[2,4,72,256]{3,2,1,0:T(8,128)S(1)}, u32[]{:S(2)}, u32[]{:S(2)}) collective-permute-start(f32[2,4,72,256]{3,2,1,0:T(8,128)S(1)} %get-tuple-element.56), channel_id=1, source_target_pairs={{0,16},{16,0},{1,17},{17,1},{2,18},{18,2},{3,19},{19,3},{4,20},{20... | collective-permute-start | bytes 1769480 | tf_op jit(solution)/shard_map/ppermute | solution.py:450
  16.8 14.7 %collective-permute-start.8 = (f32[1,4,72,256]{3,2,1,0:T(8,128)S(1)}, f32[1,4,72,256]{3,2,1,0:T(8,128)S(1)}, u32[]{:S(2)}, u32[]{:S(2)}) collective-permute-start(f32[1,4,72,256]{3,2,1,0:T(8,128)S(1)} %collective-permute-done.1.now_a), channel_id=1, source_target_pairs={{0,1},{1,0},{2,3},{3,2},{4,5},{5,4},{6,7},{7,6},{8,9},{9,8},{10,11... | collective-permute-start | bytes 884744 | tf_op jit(solution)/shard_map/ppermute | solution.py:441
  22.6 20.6 %collective-permute-start.2 = (f32[2,4,64,256]{3,2,1,0:T(8,128)S(1)}, f32[2,4,64,256]{3,2,1,0:T(8,128)S(1)}, u32[]{:S(2)}, u32[]{:S(2)}) collective-permute-start(f32[2,4,64,256]{3,2,1,0:T(8,128)S(1)} %get-tuple-element.40), channel_id=1, source_target_pairs={{1,2},{2,1},{3,4},{4,3},{5,6},{6,5},{7,8},{8,7},{9,10},{10,9},{11,... | collective-permute-start | bytes 1572872 | tf_op jit(solution)/shard_map/ppermute | solution.py:441
  26.0 9.9 %copy-start.3 = (f32[1,4,256,256]{3,2,1,0:T(8,128)S(1)}, f32[1,4,256,256]{3,2,1,0:T(8,128)}, u32[]{:S(2)}) copy-start(f32[1,4,256,256]{3,2,1,0:T(8,128)} %param.6) | copy-start | bytes 3145732
  29.8 9.9 %copy-start.2 = (f32[4,256,256]{2,1,0:T(8,128)S(1)}, f32[4,256,256]{2,1,0:T(8,128)}, u32[]{:S(2)}) copy-start(f32[4,256,256]{2,1,0:T(8,128)} %refs_4_.5) | copy-start | bytes 3145732
  29.8 16.6 %collective-permute-start.6 = (f32[2,4,64,256]{3,2,1,0:T(8,128)S(1)}, f32[2,4,64,256]{3,2,1,0:T(8,128)S(1)}, u32[]{:S(2)}, u32[]{:S(2)}) collective-permute-start(f32[2,4,64,256]{3,2,1,0:T(8,128)S(1)} %get-tuple-element.51), channel_id=1, source_target_pairs={{0,16},{16,0},{1,17},{17,1},{2,18},{18,2},{3,19},{19,3},{4,20},{20... | collective-permute-start | bytes 1572872 | tf_op jit(solution)/shard_map/ppermute | solution.py:450
  31.5 13.4 %collective-permute-start.5 = (f32[1,4,64,256]{3,2,1,0:T(8,128)S(1)}, f32[1,4,64,256]{3,2,1,0:T(8,128)S(1)}, u32[]{:S(2)}, u32[]{:S(2)}) collective-permute-start(f32[1,4,64,256]{3,2,1,0:T(8,128)S(1)} %collective-permute-done.3.now_b), channel_id=1, source_target_pairs={{1,2},{2,1},{3,4},{4,3},{5,6},{6,5},{7,8},{8,7},{9,10},{10,9},{11,... | collective-permute-start | bytes 786440 | tf_op jit(solution)/shard_map/ppermute | solution.py:441
  33.4 11.5 %collective-permute-start.4 = (f32[1,4,64,256]{3,2,1,0:T(8,128)S(1)}, f32[1,4,64,256]{3,2,1,0:T(8,128)S(1)}, u32[]{:S(2)}, u32[]{:S(2)}) collective-permute-start(f32[1,4,64,256]{3,2,1,0:T(8,128)S(1)} %collective-permute-done.3.now_b), channel_id=1, source_target_pairs={{0,1},{1,0},{2,3},{3,2},{4,5},{5,4},{6,7},{7,6},{8,9},{9,8},{10,11... | collective-permute-start | bytes 786440 | tf_op jit(solution)/shard_map/ppermute | solution.py:441
  41.2 21.7 %collective-permute-start.15 = (f32[2,4,64,256]{3,2,1,0:T(8,128)S(1)}, f32[2,4,64,256]{3,2,1,0:T(8,128)S(1)}, u32[]{:S(2)}, u32[]{:S(2)}) collective-permute-start(f32[2,4,64,256]{3,2,1,0:T(8,128)S(1)} %get-tuple-element.65), channel_id=1, source_target_pairs={{1,2},{2,1},{3,4},{4,3},{5,6},{6,5},{7,8},{8,7},{9,10},{10,9},{11,... | collective-permute-start | bytes 1572872 | tf_op jit(solution)/shard_map/ppermute | solution.py:441
  43.1 19.8 %collective-permute-start.14 = (f32[2,4,64,256]{3,2,1,0:T(8,128)S(1)}, f32[2,4,64,256]{3,2,1,0:T(8,128)S(1)}, u32[]{:S(2)}, u32[]{:S(2)}) collective-permute-start(f32[2,4,64,256]{3,2,1,0:T(8,128)S(1)} %get-tuple-element.65), channel_id=1, source_target_pairs={{0,1},{1,0},{2,3},{3,2},{4,5},{5,4},{6,7},{7,6},{8,9},{9,8},{10,11... | collective-permute-start | bytes 1572872 | tf_op jit(solution)/shard_map/ppermute | solution.py:441
  48.0 20.6 %collective-permute-start.12 = (f32[2,4,64,256]{3,2,1,0:T(8,128)S(1)}, f32[2,4,64,256]{3,2,1,0:T(8,128)S(1)}, u32[]{:S(2)}, u32[]{:S(2)}) collective-permute-start(f32[2,4,64,256]{3,2,1,0:T(8,128)S(1)} %get-tuple-element.60), channel_id=1, source_target_pairs={{1,2},{2,1},{3,4},{4,3},{5,6},{6,5},{7,8},{8,7},{9,10},{10,9},{11,... | collective-permute-start | bytes 1572872 | tf_op jit(solution)/shard_map/ppermute | solution.py:441
  49.9 18.7 %collective-permute-start.11 = (f32[2,4,64,256]{3,2,1,0:T(8,128)S(1)}, f32[2,4,64,256]{3,2,1,0:T(8,128)S(1)}, u32[]{:S(2)}, u32[]{:S(2)}) collective-permute-start(f32[2,4,64,256]{3,2,1,0:T(8,128)S(1)} %get-tuple-element.60), channel_id=1, source_target_pairs={{0,1},{1,0},{2,3},{3,2},{4,5},{5,4},{6,7},{7,6},{8,9},{9,8},{10,11... | collective-permute-start | bytes 1572872 | tf_op jit(solution)/shard_map/ppermute | solution.py:441
  64.0 6.6 %collective-permute-start.16 = (f32[4,64,256]{2,1,0:T(8,128)S(1)}, f32[4,64,256]{2,1,0:T(8,128)S(1)}, u32[]{:S(2)}, u32[]{:S(2)}) collective-permute-start(f32[4,64,256]{2,1,0:T(8,128)S(1)} %bitcast.31), channel_id=1, source_target_pairs={{0,16},{16,0},{1,17},{17,1},{2,18},{18,2},{3,19},{19,3},{4,20},{20... | collective-permute-start | bytes 786440 | tf_op jit(solution)/shard_map/ppermute | solution.py:450
  69.6 6.4 %collective-permute-start.13 = (f32[4,64,256]{2,1,0:T(8,128)S(1)}, f32[4,64,256]{2,1,0:T(8,128)S(1)}, u32[]{:S(2)}, u32[]{:S(2)}) collective-permute-start(f32[4,64,256]{2,1,0:T(8,128)S(1)} %bitcast.32), channel_id=1, source_target_pairs={{0,16},{16,0},{1,17},{17,1},{2,18},{18,2},{3,19},{19,3},{4,20},{20... | collective-permute-start | bytes 786440 | tf_op jit(solution)/shard_map/ppermute | solution.py:450

commit v3 on v2

--- a/solution.py
+++ b/solution.py
@@ -475,13 +475,16 @@
 
     out_own = [outside(face_a)]
     in_own = inside(face)
-    nows = [[turn(turning[2 * (s - 1) + c], s) for s in range(1, parts)] for c in range(2)]
+    nows = [[turn(turning[2 * (s - 1)], s) for s in range(1, parts)]]
+    out_far = [[outside(field) for field in nows[0]]]
+    in_far = [[inside(field) for field in nows[0]]]
+    nows.append([turn(after(turning[2 * s - 1], *in_far[0]), s) for s in range(1, parts)])
     out_own.append(outside(after(face_b, *nows[0])))
 
     scr = pltpu.VMEM((slab, depth // LANES, width + 2 * SUB, LANES), jnp.float32)
     wide = (slab, width, depth)
     cells = slab * width * depth
-    s1, s2, s3 = call(functools.partial(slope_kernel, width), info, (after(buoyancy, in_own),), [wide] * 3, [scr], 33 * cells)
+    s1, s2, s3 = call(functools.partial(slope_kernel, width), info, (after(buoyancy, in_own, out_own[0]),), [wide] * 3, [scr], 33 * cells)
 
     copies, outs = [], []
     for s in range(1, parts):
@@ -497,9 +500,6 @@
     )
     images, alongs = [image], [along]
 
-    sent = nows[0]
-    out_far = [[outside(field) for field in sent]]
-    in_far = [[inside(field) for field in sent]]
     wholes = []
     for s in range(1, parts):
         image, along, whole = call(

time: 77.5 us -> 76.7 us (0.990)
  starting transfers between devices: 27.7 us -> 23.1 us
  waiting for transfers between devices: 21.6 us -> 25.9 us
    ppermute x11, waiting for transfers between devices: 9.08 us -> 15.7 us  [swap(): return lax.ppermute(stack, 'space', pairs)]
    ppermute x11, starting transfers between devices: 21.2 us -> 16.6 us  [swap(): return lax.ppermute(stack, 'space', pairs)]
    ppermute x6, waiting for transfers between devices: 12.6 us -> 10.2 us  [turn(): lax.ppermute(field, 'probe', [(i, (i + s) % parts) for i in range(parts)])]
where the time goes in v3:
time: 76.7 us; the launch traced here: 76.5 us
  Pallas kernels  27.1 us (35%)
  waiting for transfers between devices  25.9 us (34%)
  starting transfers between devices  23.1 us (30%)
    pallas_call x10, Pallas kernels, call(): pl.pallas_call(kernel, name=kernel.func.__name__, out_shape=outs, in_spec...  24.9 us
    ppermute x11, starting transfers between devices, swap(): return lax.ppermute(stack, 'space', pairs)  16.6 us
    ppermute x11, waiting for transfers between devices, swap(): return lax.ppermute(stack, 'space', pairs)  15.7 us
    ppermute x6, waiting for transfers between devices, turn(): lax.ppermute(field, 'probe', [(i, (i + s) % parts) for i in range(parts)])  10.2 us
    ppermute x6, starting transfers between devices, turn(): lax.ppermute(field, 'probe', [(i, (i + s) % parts) for i in range(parts)])  6.54 us
    pallas_call x2, Pallas kernels, lay(): pl.pallas_call(functools.partial(lay_kernel, len(pieces)), name='lay_kern...  2.16 us
  transfers between devices with their start and end apart: 17, of which 8 were waited for; matrix products, arithmetic and copies ran while one was open for 0% of the time, Pallas kernels for 31%

profile of v3, /device:TPU:4, one launch (start us, length us, event | category | flops | bytes accessed | tf_op | source)
XLA Modules:
  0.0 76.5 jit_solution(12433059959309825332)
XLA Ops:
  0.0 0.1 stack.59.info
  0.1 2.4 %pack_kernel.2 = (f32[2,4,136,256]{3,2,1,0:T(8,128)S(1)}, f32[2,4,72,256]{3,2,1,0:T(8,128)S(1)}, f32[2,4,64,256]{3,2,1,0:T(8,128)S(1)}, f32[1,4,72,256]{3,2,1,0:T(8,128)S(1)}, f32[1,4,64,256]{3,2,1,0:T(8,128)S(1)}) custom-call(s32[7]{0:T(128)S(1)} %stack.59.info, f32[4,256,256]{2,1,0:T(8,128)} %refs_5_.3, f32[4,256,256]{2,1,0:T(8,128)} %bitcast.23), custom_call_target="tpu_custom_call" | custom-call | flops 1024 | bytes 1024 | tf_op jit(solution)/shard_map/pack_kernel/pallas_call | solution.py:365
  2.5 0.0 copy-start
  2.5 0.1 collective-permute-start
  2.6 1.7 %collective-permute-start.1 = (f32[1,4,72,256]{3,2,1,0:T(8,128)S(1)}, f32[1,4,72,256]{3,2,1,0:T(8,128)S(1)}, u32[]{:S(2)}, u32[]{:S(2)}) collective-permute-start(f32[1,4,72,256]{3,2,1,0:T(8,128)S(1)} %get-tuple-element.40), channel_id=1, source_target_pairs={{0,16},{16,0},{1,17},{17,1},{2,18},{18,2},{3,19},{19,3},{4,20},{20... | collective-permute-start | bytes 884744 | tf_op jit(solution)/shard_map/ppermute | solution.py:450
  4.3 2.2 %collective-permute-start.5 = (f32[2,4,72,256]{3,2,1,0:T(8,128)S(1)}, f32[2,4,72,256]{3,2,1,0:T(8,128)S(1)}, u32[]{:S(2)}, u32[]{:S(2)}) collective-permute-start(f32[2,4,72,256]{3,2,1,0:T(8,128)S(1)} %get-tuple-element.44), channel_id=1, source_target_pairs={{1,2},{2,1},{3,4},{4,3},{5,6},{6,5},{7,8},{8,7},{9,10},{10,9},{11,... | collective-permute-start | bytes 1769480 | tf_op jit(solution)/shard_map/ppermute | solution.py:441
  6.4 5.6 %collective-permute-done.1.now_a = f32[1,4,72,256]{3,2,1,0:T(8,128)S(1)} collective-permute-done((f32[1,4,72,256]{3,2,1,0:T(8,128)S(1)}, f32[1,4,72,256]{3,2,1,0:T(8,128)S(1)}, u32[]{:S(2)}, u32[]{:S(2)}) %collective-permute-start.1) | collective-permute-done | bytes 294944 | tf_op jit(solution)/shard_map/ppermute | solution.py:450
  12.0 0.0 collective-permute-start.3
  12.0 1.6 %collective-permute-done.3.refs_2_ = f32[1,4,72,256]{3,2,1,0:T(8,128)S(1)} collective-permute-done((f32[1,4,72,256]{3,2,1,0:T(8,128)S(1)}, f32[1,4,72,256]{3,2,1,0:T(8,128)S(1)}, u32[]{:S(2)}, u32[]{:S(2)}) %collective-permute-start.3) | collective-permute-done | bytes 294944 | tf_op jit(solution)/shard_map/ppermute | solution.py:441
  13.6 1.6 %collective-permute-start.4 = (f32[1,4,64,256]{3,2,1,0:T(8,128)S(1)}, f32[1,4,64,256]{3,2,1,0:T(8,128)S(1)}, u32[]{:S(2)}, u32[]{:S(2)}) collective-permute-start(f32[1,4,64,256]{3,2,1,0:T(8,128)S(1)} %get-tuple-element.43), channel_id=1, source_target_pairs={{0,16},{16,0},{1,17},{17,1},{2,18},{18,2},{3,19},{19,3},{4,20},{20... | collective-permute-start | bytes 786440 | tf_op jit(solution)/shard_map/ppermute | solution.py:450
  15.2 0.7 pack_kernel.3
  15.9 0.5 collective-permute-start.10
  16.4 1.9 %collective-permute-start.9 = (f32[1,4,72,256]{3,2,1,0:T(8,128)S(1)}, f32[1,4,72,256]{3,2,1,0:T(8,128)S(1)}, u32[]{:S(2)}, u32[]{:S(2)}) collective-permute-start(f32[1,4,72,256]{3,2,1,0:T(8,128)S(1)} %collective-permute-done.1.now_a), channel_id=1, source_target_pairs={{1,2},{2,1},{3,4},{4,3},{5,6},{6,5},{7,8},{8,7},{9,10},{10,9},{11,... | collective-permute-start | bytes 884744 | tf_op jit(solution)/shard_map/ppermute | solution.py:441
  18.3 3.5 %collective-permute-done.5.refs_1_ = f32[2,4,72,256]{3,2,1,0:T(8,128)S(1)} collective-permute-done((f32[2,4,72,256]{3,2,1,0:T(8,128)S(1)}, f32[2,4,72,256]{3,2,1,0:T(8,128)S(1)}, u32[]{:S(2)}, u32[]{:S(2)}) %collective-permute-start.5) | collective-permute-done | bytes 589856 | tf_op jit(solution)/shard_map/ppermute | solution.py:441
  21.8 1.9 %collective-permute-start.2 = (f32[2,4,64,256]{3,2,1,0:T(8,128)S(1)}, f32[2,4,64,256]{3,2,1,0:T(8,128)S(1)}, u32[]{:S(2)}, u32[]{:S(2)}) collective-permute-start(f32[2,4,64,256]{3,2,1,0:T(8,128)S(1)} %get-tuple-element.41), channel_id=1, source_target_pairs={{1,2},{2,1},{3,4},{4,3},{5,6},{6,5},{7,8},{8,7},{9,10},{10,9},{11,... | collective-permute-start | bytes 1572872 | tf_op jit(solution)/shard_map/ppermute | solution.py:441
  23.7 0.0 collective-permute-done.refs_0_
  23.7 3.6 %slope_kernel.1 = (f32[4,136,256]{2,1,0:T(8,128)S(1)}, f32[4,136,256]{2,1,0:T(8,128)S(1)}, f32[4,136,256]{2,1,0:T(8,128)S(1)}) custom-call(s32[7]{0:T(128)S(1)} %stack.59.info, f32[4,256,256]{2,1,0:T(8,128)S(1)} %copy-done), custom_call_target="tpu_custom_call" | custom-call | flops 1024 | bytes 1024 | tf_op jit(solution)/shard_map/slope_kernel/pallas_call | solution.py:365
  27.4 0.0 collective-permute-done.4.now_b
  27.4 0.0 copy-start.3
  27.4 3.8 %far_kernel.1 = (f32[4,136,256]{2,1,0:T(8,128)S(1)}, f32[4,136,256]{2,1,0:T(8,128)S(1)}, f32[4,136,256]{2,1,0:T(8,128)S(1)}) custom-call(s32[7]{0:T(128)S(1)} %stack.59.info, f32[1,4,72,256]{3,2,1,0:T(8,128)S(1)} %collective-permute-done.1.now_a, f32[1,4,64,256]{3,2,1,0:T(8,128)S(1)} %collective-permute-done.4.now_b, f32[4,256,256]{2,1,0:T(8,128)S(1)} %copy-done, ...), custom_call_target="tpu_custom_call" | custom-call | flops 1024 | bytes 1024 | tf_op jit(solution)/shard_map/far_kernel/pallas_call | solution.py:365
  31.1 0.0 copy-start.2
  31.2 0.5 collective-permute-start.8
  31.6 3.5 %collective-permute-start.7 = (f32[1,4,64,256]{3,2,1,0:T(8,128)S(1)}, f32[1,4,64,256]{3,2,1,0:T(8,128)S(1)}, u32[]{:S(2)}, u32[]{:S(2)}) collective-permute-start(f32[1,4,64,256]{3,2,1,0:T(8,128)S(1)} %collective-permute-done.4.now_b), channel_id=1, source_target_pairs={{1,2},{2,1},{3,4},{4,3},{5,6},{6,5},{7,8},{8,7},{9,10},{10,9},{11,... | collective-permute-start | bytes 786440 | tf_op jit(solution)/shard_map/ppermute | solution.py:441
  35.1 0.0 collective-permute-done.9.refs_3_
  35.1 0.5 collective-permute-start.6
  35.6 3.8 %own_kernel.1 = (f32[4,136,256]{2,1,0:T(8,128)S(1)}, f32[4,136,256]{2,1,0:T(8,128)S(1)}) custom-call(s32[7]{0:T(128)S(1)} %stack.59.info, f32[4,256,256]{2,1,0:T(8,128)S(1)} %bitcast.24, f32[4,256,256]{2,1,0:T(8,128)S(1)} %copy-done, f32[4,136,256]{2,1,0:T(8,128)S(1)} %get-tuple-element.46.s2.refs_6_, f32[4,136,256]{2,1,0:T(8,128)S(1)} %get-tuple-element.47.s3.refs_7_), custom_call_target="tpu_custom_call" | custom-call | flops 1024 | bytes 1024 | tf_op jit(solution)/shard_map/own_kernel/pallas_call | solution.py:365
  39.4 0.0 collective-permute-done.10.refs_11_
  39.4 1.5 %finish_kernel.2 = (f32[2,4,136,256]{3,2,1,0:T(8,128)S(1)}, f32[4,136,256]{2,1,0:T(8,128)S(1)}, f32[4,136,256]{2,1,0:T(8,128)S(1)}, f32[2,4,64,256]{3,2,1,0:T(8,128)S(1)}) custom-call(s32[7]{0:T(128)S(1)} %stack.59.info, f32[2,4,136,256]{3,2,1,0:T(8,128)S(1)} %collective-permute-done.refs_0_, f32[2,4,72,256]{3,2,1,0:T(8,128)S(1)} %collective-permute-done.5.refs_1_, ...), custom_call_target="tpu_custom_call" | custom-call | flops 1024 | bytes 1024 | tf_op jit(solution)/shard_map/finish_kernel/pallas_call | solution.py:365
  40.9 1.9 %collective-permute-start.15 = (f32[2,4,64,256]{3,2,1,0:T(8,128)S(1)}, f32[2,4,64,256]{3,2,1,0:T(8,128)S(1)}, u32[]{:S(2)}, u32[]{:S(2)}) collective-permute-start(f32[2,4,64,256]{3,2,1,0:T(8,128)S(1)} %get-tuple-element.67), channel_id=1, source_target_pairs={{1,2},{2,1},{3,4},{4,3},{5,6},{6,5},{7,8},{8,7},{9,10},{10,9},{11,... | collective-permute-start | bytes 1572872 | tf_op jit(solution)/shard_map/ppermute | solution.py:441
  42.8 0.0 collective-permute-done.2.refs_1_
  42.9 1.9 %collective-permute-start.14 = (f32[2,4,64,256]{3,2,1,0:T(8,128)S(1)}, f32[2,4,64,256]{3,2,1,0:T(8,128)S(1)}, u32[]{:S(2)}, u32[]{:S(2)}) collective-permute-start(f32[2,4,64,256]{3,2,1,0:T(8,128)S(1)} %get-tuple-element.67), channel_id=1, source_target_pairs={{0,1},{1,0},{2,3},{3,2},{4,5},{5,4},{6,7},{7,6},{8,9},{9,8},{10,11... | collective-permute-start | bytes 1572872 | tf_op jit(solution)/shard_map/ppermute | solution.py:441
  44.7 0.2 collective-permute-done.7.refs_3_
  45.0 0.9 %collective-permute-done.8.refs_11_ = f32[2,4,64,256]{3,2,1,0:T(8,128)S(1)} collective-permute-done((f32[2,4,64,256]{3,2,1,0:T(8,128)S(1)}, f32[2,4,64,256]{3,2,1,0:T(8,128)S(1)}, u32[]{:S(2)}, u32[]{:S(2)}) %collective-permute-start.8) | collective-permute-done | bytes 524320 | tf_op jit(solution)/shard_map/ppermute | solution.py:450
  45.8 1.5 %finish_kernel.3 = (f32[2,4,136,256]{3,2,1,0:T(8,128)S(1)}, f32[4,136,256]{2,1,0:T(8,128)S(1)}, f32[4,136,256]{2,1,0:T(8,128)S(1)}, f32[2,4,64,256]{3,2,1,0:T(8,128)S(1)}) custom-call(s32[7]{0:T(128)S(1)} %stack.59.info, f32[2,4,136,256]{3,2,1,0:T(8,128)S(1)} %collective-permute-done.refs_0_, f32[2,4,64,256]{3,2,1,0:T(8,128)S(1)} %collective-permute-done.2.refs_1_, ...), custom_call_target="tpu_custom_call" | custom-call | flops 1024 | bytes 1024 | tf_op jit(solution)/shard_map/finish_kernel/pallas_call | solution.py:365
  47.3 1.9 %collective-permute-start.12 = (f32[2,4,64,256]{3,2,1,0:T(8,128)S(1)}, f32[2,4,64,256]{3,2,1,0:T(8,128)S(1)}, u32[]{:S(2)}, u32[]{:S(2)}) collective-permute-start(f32[2,4,64,256]{3,2,1,0:T(8,128)S(1)} %get-tuple-element.62), channel_id=1, source_target_pairs={{1,2},{2,1},{3,4},{4,3},{5,6},{6,5},{7,8},{8,7},{9,10},{10,9},{11,... | collective-permute-start | bytes 1572872 | tf_op jit(solution)/shard_map/ppermute | solution.py:441
  49.3 0.8 %collective-permute-start.11 = (f32[2,4,64,256]{3,2,1,0:T(8,128)S(1)}, f32[2,4,64,256]{3,2,1,0:T(8,128)S(1)}, u32[]{:S(2)}, u32[]{:S(2)}) collective-permute-start(f32[2,4,64,256]{3,2,1,0:T(8,128)S(1)} %get-tuple-element.62), channel_id=1, source_target_pairs={{0,1},{1,0},{2,3},{3,2},{4,5},{5,4},{6,7},{7,6},{8,9},{9,8},{10,11... | collective-permute-start | bytes 1572872 | tf_op jit(solution)/shard_map/ppermute | solution.py:441
  50.1 5.5 %start_kernel.1.refs_2_ = f32[2,4,128,256]{3,2,1,0:T(8,128)S(1)} custom-call(s32[7]{0:T(128)S(1)} %stack.59.info, f32[2,4,136,256]{3,2,1,0:T(8,128)S(1)} %get-tuple-element.63.refs_0_, f32[4,256,256]{2,1,0:T(8,128)S(1)} %bitcast.27, f32[4,256,256]{2,1,0:T(8,128)S(1)} %bitcast.20, f32[4,256,256]{2,1,0:T(8,128)S(1)} %copy-done.2, f32[4,256,256]{2,1,0:T(8,128)S(1)} %copy-done, ...), custom_call_target="tpu_custom_call" | custom-call | flops 1024 | bytes 1024 | tf_op jit(solution)/shard_map/start_kernel/pallas_call | solution.py:365
  55.6 7.0 %collective-permute-done.15.refs_1_ = f32[2,4,64,256]{3,2,1,0:T(8,128)S(1)} collective-permute-done((f32[2,4,64,256]{3,2,1,0:T(8,128)S(1)}, f32[2,4,64,256]{3,2,1,0:T(8,128)S(1)}, u32[]{:S(2)}, u32[]{:S(2)}) %collective-permute-start.15) | collective-permute-done | bytes 524320 | tf_op jit(solution)/shard_map/ppermute | solution.py:441
  62.6 0.0 collective-permute-done.14.refs_0_
  62.7 1.1 %end_kernel.3 = (f32[4,64,256]{2,1,0:T(8,128)S(1)}, f32[1,4,64,256]{3,2,1,0:T(8,128)S(1)}) custom-call(s32[7]{0:T(128)S(1)} %stack.59.info, f32[2,4,64,256]{3,2,1,0:T(8,128)S(1)} %collective-permute-done.14.refs_0_, f32[2,4,64,256]{3,2,1,0:T(8,128)S(1)} %collective-permute-done.15.refs_1_, f32[2,4,128,256]{3,2,1,0:T(8,128)S(1)} %start_kernel.1.refs_2_, ...), custom_call_target="tpu_custom_call" | custom-call | flops 1024 | bytes 1024 | tf_op jit(solution)/shard_map/end_kernel/pallas_call | solution.py:365
  63.7 1.1 %collective-permute-start.16 = (f32[4,64,256]{2,1,0:T(8,128)S(1)}, f32[4,64,256]{2,1,0:T(8,128)S(1)}, u32[]{:S(2)}, u32[]{:S(2)}) collective-permute-start(f32[4,64,256]{2,1,0:T(8,128)S(1)} %bitcast.31), channel_id=1, source_target_pairs={{0,16},{16,0},{1,17},{17,1},{2,18},{18,2},{3,19},{19,3},{4,20},{20... | collective-permute-start | bytes 786440 | tf_op jit(solution)/shard_map/ppermute | solution.py:450
  64.9 3.4 %collective-permute-done.12.refs_1_ = f32[2,4,64,256]{3,2,1,0:T(8,128)S(1)} collective-permute-done((f32[2,4,64,256]{3,2,1,0:T(8,128)S(1)}, f32[2,4,64,256]{3,2,1,0:T(8,128)S(1)}, u32[]{:S(2)}, u32[]{:S(2)}) %collective-permute-start.12) | collective-permute-done | bytes 524320 | tf_op jit(solution)/shard_map/ppermute | solution.py:441
  68.3 1.1 %end_kernel.2 = (f32[4,64,256]{2,1,0:T(8,128)S(1)}, f32[1,4,64,256]{3,2,1,0:T(8,128)S(1)}) custom-call(s32[7]{0:T(128)S(1)} %stack.59.info, f32[2,4,64,256]{3,2,1,0:T(8,128)S(1)} %collective-permute-done.11.refs_0_, f32[2,4,64,256]{3,2,1,0:T(8,128)S(1)} %collective-permute-done.12.refs_1_, f32[2,4,128,256]{3,2,1,0:T(8,128)S(1)} %start_kernel.1.refs_2_, ...), custom_call_target="tpu_custom_call" | custom-call | flops 1024 | bytes 1024 | tf_op jit(solution)/shard_map/end_kernel/pallas_call | solution.py:365
  69.3 1.1 %collective-permute-start.13 = (f32[4,64,256]{2,1,0:T(8,128)S(1)}, f32[4,64,256]{2,1,0:T(8,128)S(1)}, u32[]{:S(2)}, u32[]{:S(2)}) collective-permute-start(f32[4,64,256]{2,1,0:T(8,128)S(1)} %bitcast.32), channel_id=1, source_target_pairs={{0,16},{16,0},{1,17},{17,1},{2,18},{18,2},{3,19},{19,3},{4,20},{20... | collective-permute-start | bytes 786440 | tf_op jit(solution)/shard_map/ppermute | solution.py:450
  70.5 0.1 pad_add_fusion.rows
  70.6 1.4 %lay_kernel.2.refs_1_ = f32[4,256,256]{2,1,0:T(8,128)} custom-call(s32[3]{0:T(128)S(1)} %pad_add_fusion.rows, f32[4,64,256]{2,1,0:T(8,128)S(1)} %get-tuple-element.68.refs_0_, f32[4,64,256]{2,1,0:T(8,128)S(1)} %collective-permute-done.16.refs_1_, f32[4,64,256]{2,1,0:T(8,128)S(1)} %get-tuple-element.70.refs_2_), custom_call_target="tpu_custom_call" | custom-call | tf_op jit(solution)/shard_map/lay_kernel/pallas_call | solution.py:394
  72.0 3.8 %collective-permute-done.13.refs_0_ = f32[4,64,256]{2,1,0:T(8,128)S(1)} collective-permute-done((f32[4,64,256]{2,1,0:T(8,128)S(1)}, f32[4,64,256]{2,1,0:T(8,128)S(1)}, u32[]{:S(2)}, u32[]{:S(2)}) %collective-permute-start.13) | collective-permute-done | bytes 262176 | tf_op jit(solution)/shard_map/ppermute | solution.py:450
  75.8 0.7 lay_kernel.3
  (10 shorter events, 0.0 us)
Async XLA Ops:
  0.0 15.2 %copy-start.4 = (f32[1,4,256,256]{3,2,1,0:T(8,128)S(1)}, f32[1,4,256,256]{3,2,1,0:T(8,128)}, u32[]{:S(2)}) copy-start(f32[1,4,256,256]{3,2,1,0:T(8,128)} %param.5) | copy-start | bytes 3145732
  0.0 15.2 %copy-start.1 = (f32[1,4,256,256]{3,2,1,0:T(8,128)S(1)}, f32[1,4,256,256]{3,2,1,0:T(8,128)}, u32[]{:S(2)}) copy-start(f32[1,4,256,256]{3,2,1,0:T(8,128)} %param.9) | copy-start | bytes 3145732
  2.5 21.2 %copy-start = (f32[4,256,256]{2,1,0:T(8,128)S(1)}, f32[4,256,256]{2,1,0:T(8,128)}, u32[]{:S(2)}) copy-start(f32[4,256,256]{2,1,0:T(8,128)} %refs_5_.3) | copy-start | bytes 3145732
  2.5 21.2 %collective-permute-start = (f32[2,4,136,256]{3,2,1,0:T(8,128)S(1)}, f32[2,4,136,256]{3,2,1,0:T(8,128)S(1)}, u32[]{:S(2)}, u32[]{:S(2)}) collective-permute-start(f32[2,4,136,256]{3,2,1,0:T(8,128)S(1)} %get-tuple-element.38), channel_id=1, source_target_pairs={{0,1},{1,0},{2,3},{3,2},{4,5},{5,4},{6,7},{7,6},{8,9},{9,8},{10,11... | collective-permute-start | bytes 3342344 | tf_op jit(solution)/shard_map/ppermute | solution.py:441
  2.6 9.4 %collective-permute-start.1 = (f32[1,4,72,256]{3,2,1,0:T(8,128)S(1)}, f32[1,4,72,256]{3,2,1,0:T(8,128)S(1)}, u32[]{:S(2)}, u32[]{:S(2)}) collective-permute-start(f32[1,4,72,256]{3,2,1,0:T(8,128)S(1)} %get-tuple-element.40), channel_id=1, source_target_pairs={{0,16},{16,0},{1,17},{17,1},{2,18},{18,2},{3,19},{19,3},{4,20},{20... | collective-permute-start | bytes 884744 | tf_op jit(solution)/shard_map/ppermute | solution.py:450
  4.3 17.5 %collective-permute-start.5 = (f32[2,4,72,256]{3,2,1,0:T(8,128)S(1)}, f32[2,4,72,256]{3,2,1,0:T(8,128)S(1)}, u32[]{:S(2)}, u32[]{:S(2)}) collective-permute-start(f32[2,4,72,256]{3,2,1,0:T(8,128)S(1)} %get-tuple-element.44), channel_id=1, source_target_pairs={{1,2},{2,1},{3,4},{4,3},{5,6},{6,5},{7,8},{8,7},{9,10},{10,9},{11,... | collective-permute-start | bytes 1769480 | tf_op jit(solution)/shard_map/ppermute | solution.py:441
  12.0 1.6 %collective-permute-start.3 = (f32[1,4,72,256]{3,2,1,0:T(8,128)S(1)}, f32[1,4,72,256]{3,2,1,0:T(8,128)S(1)}, u32[]{:S(2)}, u32[]{:S(2)}) collective-permute-start(f32[1,4,72,256]{3,2,1,0:T(8,128)S(1)} %collective-permute-done.1.now_a), channel_id=1, source_target_pairs={{0,1},{1,0},{2,3},{3,2},{4,5},{5,4},{6,7},{7,6},{8,9},{9,8},{10,11... | collective-permute-start | bytes 884744 | tf_op jit(solution)/shard_map/ppermute | solution.py:441
  13.6 13.8 %collective-permute-start.4 = (f32[1,4,64,256]{3,2,1,0:T(8,128)S(1)}, f32[1,4,64,256]{3,2,1,0:T(8,128)S(1)}, u32[]{:S(2)}, u32[]{:S(2)}) collective-permute-start(f32[1,4,64,256]{3,2,1,0:T(8,128)S(1)} %get-tuple-element.43), channel_id=1, source_target_pairs={{0,16},{16,0},{1,17},{17,1},{2,18},{18,2},{3,19},{19,3},{4,20},{20... | collective-permute-start | bytes 786440 | tf_op jit(solution)/shard_map/ppermute | solution.py:450
  15.9 23.5 %collective-permute-start.10 = (f32[2,4,72,256]{3,2,1,0:T(8,128)S(1)}, f32[2,4,72,256]{3,2,1,0:T(8,128)S(1)}, u32[]{:S(2)}, u32[]{:S(2)}) collective-permute-start(f32[2,4,72,256]{3,2,1,0:T(8,128)S(1)} %get-tuple-element.58), channel_id=1, source_target_pairs={{0,16},{16,0},{1,17},{17,1},{2,18},{18,2},{3,19},{19,3},{4,20},{20... | collective-permute-start | bytes 1769480 | tf_op jit(solution)/shard_map/ppermute | solution.py:450
  16.4 18.7 %collective-permute-start.9 = (f32[1,4,72,256]{3,2,1,0:T(8,128)S(1)}, f32[1,4,72,256]{3,2,1,0:T(8,128)S(1)}, u32[]{:S(2)}, u32[]{:S(2)}) collective-permute-start(f32[1,4,72,256]{3,2,1,0:T(8,128)S(1)} %collective-permute-done.1.now_a), channel_id=1, source_target_pairs={{1,2},{2,1},{3,4},{4,3},{5,6},{6,5},{7,8},{8,7},{9,10},{10,9},{11,... | collective-permute-start | bytes 884744 | tf_op jit(solution)/shard_map/ppermute | solution.py:441
  21.8 21.1 %collective-permute-start.2 = (f32[2,4,64,256]{3,2,1,0:T(8,128)S(1)}, f32[2,4,64,256]{3,2,1,0:T(8,128)S(1)}, u32[]{:S(2)}, u32[]{:S(2)}) collective-permute-start(f32[2,4,64,256]{3,2,1,0:T(8,128)S(1)} %get-tuple-element.41), channel_id=1, source_target_pairs={{1,2},{2,1},{3,4},{4,3},{5,6},{6,5},{7,8},{8,7},{9,10},{10,9},{11,... | collective-permute-start | bytes 1572872 | tf_op jit(solution)/shard_map/ppermute | solution.py:441
  27.4 8.3 %copy-start.3 = (f32[1,4,256,256]{3,2,1,0:T(8,128)S(1)}, f32[1,4,256,256]{3,2,1,0:T(8,128)}, u32[]{:S(2)}) copy-start(f32[1,4,256,256]{3,2,1,0:T(8,128)} %param.6) | copy-start | bytes 3145732
  31.1 8.3 %copy-start.2 = (f32[4,256,256]{2,1,0:T(8,128)S(1)}, f32[4,256,256]{2,1,0:T(8,128)}, u32[]{:S(2)}) copy-start(f32[4,256,256]{2,1,0:T(8,128)} %refs_4_.5) | copy-start | bytes 3145732
  31.2 14.7 %collective-permute-start.8 = (f32[2,4,64,256]{3,2,1,0:T(8,128)S(1)}, f32[2,4,64,256]{3,2,1,0:T(8,128)S(1)}, u32[]{:S(2)}, u32[]{:S(2)}) collective-permute-start(f32[2,4,64,256]{3,2,1,0:T(8,128)S(1)} %get-tuple-element.54), channel_id=1, source_target_pairs={{0,16},{16,0},{1,17},{17,1},{2,18},{18,2},{3,19},{19,3},{4,20},{20... | collective-permute-start | bytes 1572872 | tf_op jit(solution)/shard_map/ppermute | solution.py:450
  31.6 13.3 %collective-permute-start.7 = (f32[1,4,64,256]{3,2,1,0:T(8,128)S(1)}, f32[1,4,64,256]{3,2,1,0:T(8,128)S(1)}, u32[]{:S(2)}, u32[]{:S(2)}) collective-permute-start(f32[1,4,64,256]{3,2,1,0:T(8,128)S(1)} %collective-permute-done.4.now_b), channel_id=1, source_target_pairs={{1,2},{2,1},{3,4},{4,3},{5,6},{6,5},{7,8},{8,7},{9,10},{10,9},{11,... | collective-permute-start | bytes 786440 | tf_op jit(solution)/shard_map/ppermute | solution.py:441
  35.1 9.8 %collective-permute-start.6 = (f32[1,4,64,256]{3,2,1,0:T(8,128)S(1)}, f32[1,4,64,256]{3,2,1,0:T(8,128)S(1)}, u32[]{:S(2)}, u32[]{:S(2)}) collective-permute-start(f32[1,4,64,256]{3,2,1,0:T(8,128)S(1)} %collective-permute-done.4.now_b), channel_id=1, source_target_pairs={{0,1},{1,0},{2,3},{3,2},{4,5},{5,4},{6,7},{7,6},{8,9},{9,8},{10,11... | collective-permute-start | bytes 786440 | tf_op jit(solution)/shard_map/ppermute | solution.py:441
  40.9 21.7 %collective-permute-start.15 = (f32[2,4,64,256]{3,2,1,0:T(8,128)S(1)}, f32[2,4,64,256]{3,2,1,0:T(8,128)S(1)}, u32[]{:S(2)}, u32[]{:S(2)}) collective-permute-start(f32[2,4,64,256]{3,2,1,0:T(8,128)S(1)} %get-tuple-element.67), channel_id=1, source_target_pairs={{1,2},{2,1},{3,4},{4,3},{5,6},{6,5},{7,8},{8,7},{9,10},{10,9},{11,... | collective-permute-start | bytes 1572872 | tf_op jit(solution)/shard_map/ppermute | solution.py:441
  42.9 19.8 %collective-permute-start.14 = (f32[2,4,64,256]{3,2,1,0:T(8,128)S(1)}, f32[2,4,64,256]{3,2,1,0:T(8,128)S(1)}, u32[]{:S(2)}, u32[]{:S(2)}) collective-permute-start(f32[2,4,64,256]{3,2,1,0:T(8,128)S(1)} %get-tuple-element.67), channel_id=1, source_target_pairs={{0,1},{1,0},{2,3},{3,2},{4,5},{5,4},{6,7},{7,6},{8,9},{9,8},{10,11... | collective-permute-start | bytes 1572872 | tf_op jit(solution)/shard_map/ppermute | solution.py:441
  47.3 20.9 %collective-permute-start.12 = (f32[2,4,64,256]{3,2,1,0:T(8,128)S(1)}, f32[2,4,64,256]{3,2,1,0:T(8,128)S(1)}, u32[]{:S(2)}, u32[]{:S(2)}) collective-permute-start(f32[2,4,64,256]{3,2,1,0:T(8,128)S(1)} %get-tuple-element.62), channel_id=1, source_target_pairs={{1,2},{2,1},{3,4},{4,3},{5,6},{6,5},{7,8},{8,7},{9,10},{10,9},{11,... | collective-permute-start | bytes 1572872 | tf_op jit(solution)/shard_map/ppermute | solution.py:441
  49.3 19.0 %collective-permute-start.11 = (f32[2,4,64,256]{3,2,1,0:T(8,128)S(1)}, f32[2,4,64,256]{3,2,1,0:T(8,128)S(1)}, u32[]{:S(2)}, u32[]{:S(2)}) collective-permute-start(f32[2,4,64,256]{3,2,1,0:T(8,128)S(1)} %get-tuple-element.62), channel_id=1, source_target_pairs={{0,1},{1,0},{2,3},{3,2},{4,5},{5,4},{6,7},{7,6},{8,9},{9,8},{10,11... | collective-permute-start | bytes 1572872 | tf_op jit(solution)/shard_map/ppermute | solution.py:441
  63.7 6.8 %collective-permute-start.16 = (f32[4,64,256]{2,1,0:T(8,128)S(1)}, f32[4,64,256]{2,1,0:T(8,128)S(1)}, u32[]{:S(2)}, u32[]{:S(2)}) collective-permute-start(f32[4,64,256]{2,1,0:T(8,128)S(1)} %bitcast.31), channel_id=1, source_target_pairs={{0,16},{16,0},{1,17},{17,1},{2,18},{18,2},{3,19},{19,3},{4,20},{20... | collective-permute-start | bytes 786440 | tf_op jit(solution)/shard_map/ppermute | solution.py:450
  69.3 6.4 %collective-permute-start.13 = (f32[4,64,256]{2,1,0:T(8,128)S(1)}, f32[4,64,256]{2,1,0:T(8,128)S(1)}, u32[]{:S(2)}, u32[]{:S(2)}) collective-permute-start(f32[4,64,256]{2,1,0:T(8,128)S(1)} %bitcast.32), channel_id=1, source_target_pairs={{0,16},{16,0},{1,17},{17,1},{2,18},{18,2},{3,19},{19,3},{4,20},{20... | collective-permute-start | bytes 786440 | tf_op jit(solution)/shard_map/ppermute | solution.py:450

commit v4 on v3

--- a/solution.py
+++ b/solution.py
@@ -253,7 +253,7 @@
                     following[s, :, rows, cols] = 2.0 * now - before + k * values[s] + scale * source
             return 0
 
-        lax.fori_loop(0, count // SUB, body, 0)
+        lax.fori_loop(0, count // SUB, body, 0, unroll=2)
 
     pl.when(info[EVEN] == 1)(lambda: loop(True))
     pl.when(info[EVEN] == 0)(lambda: loop(False))
@@ -351,7 +351,7 @@
                         others[s - 1, :, part, cols] = value
             return 0
 
-        lax.fori_loop(0, count // SUB, body, 0)
+        lax.fori_loop(0, count // SUB, body, 0, unroll=2)
 
     pl.when(info[EVEN] == 1)(lambda: loop(True))
     pl.when(info[EVEN] == 0)(lambda: loop(False))

time: 76.7 us -> 76.6 us (level)
  no operation moved by 1% of the time
where the time goes in v4:
time: 76.6 us; the launch traced here: 76.4 us
  Pallas kernels  26.9 us (35%)
  waiting for transfers between devices  25.8 us (34%)
  starting transfers between devices  23.2 us (30%)
    pallas_call x10, Pallas kernels, call(): pl.pallas_call(kernel, name=kernel.func.__name__, out_shape=outs, in_spec...  24.7 us
    ppermute x11, starting transfers between devices, swap(): return lax.ppermute(stack, 'space', pairs)  16.6 us
    ppermute x11, waiting for transfers between devices, swap(): return lax.ppermute(stack, 'space', pairs)  15.7 us
    ppermute x6, waiting for transfers between devices, turn(): lax.ppermute(field, 'probe', [(i, (i + s) % parts) for i in range(parts)])  10.1 us
    ppermute x6, starting transfers between devices, turn(): lax.ppermute(field, 'probe', [(i, (i + s) % parts) for i in range(parts)])  6.65 us
    pallas_call x2, Pallas kernels, lay(): pl.pallas_call(functools.partial(lay_kernel, len(pieces)), name='lay_kern...  2.16 us
  transfers between devices with their start and end apart: 17, of which 8 were waited for; matrix products, arithmetic and copies ran while one was open for 0% of the time, Pallas kernels for 31%

profile of v4, /device:TPU:4, one launch (start us, length us, event | category | flops | bytes accessed | tf_op | source)
XLA Modules:
  0.0 76.4 jit_solution(14518764675562996538)
XLA Ops:
  0.0 0.1 stack.59.info
  0.1 2.4 %pack_kernel.2 = (f32[2,4,136,256]{3,2,1,0:T(8,128)S(1)}, f32[2,4,72,256]{3,2,1,0:T(8,128)S(1)}, f32[2,4,64,256]{3,2,1,0:T(8,128)S(1)}, f32[1,4,72,256]{3,2,1,0:T(8,128)S(1)}, f32[1,4,64,256]{3,2,1,0:T(8,128)S(1)}) custom-call(s32[7]{0:T(128)S(1)} %stack.59.info, f32[4,256,256]{2,1,0:T(8,128)} %refs_5_.3, f32[4,256,256]{2,1,0:T(8,128)} %bitcast.23), custom_call_target="tpu_custom_call" | custom-call | flops 1024 | bytes 1024 | tf_op jit(solution)/shard_map/pack_kernel/pallas_call | solution.py:365
  2.5 0.0 copy-start
  2.5 0.1 collective-permute-start
  2.6 1.7 %collective-permute-start.1 = (f32[1,4,72,256]{3,2,1,0:T(8,128)S(1)}, f32[1,4,72,256]{3,2,1,0:T(8,128)S(1)}, u32[]{:S(2)}, u32[]{:S(2)}) collective-permute-start(f32[1,4,72,256]{3,2,1,0:T(8,128)S(1)} %get-tuple-element.40), channel_id=1, source_target_pairs={{0,16},{16,0},{1,17},{17,1},{2,18},{18,2},{3,19},{19,3},{4,20},{20... | collective-permute-start | bytes 884744 | tf_op jit(solution)/shard_map/ppermute | solution.py:450
  4.3 2.2 %collective-permute-start.5 = (f32[2,4,72,256]{3,2,1,0:T(8,128)S(1)}, f32[2,4,72,256]{3,2,1,0:T(8,128)S(1)}, u32[]{:S(2)}, u32[]{:S(2)}) collective-permute-start(f32[2,4,72,256]{3,2,1,0:T(8,128)S(1)} %get-tuple-element.44), channel_id=1, source_target_pairs={{1,2},{2,1},{3,4},{4,3},{5,6},{6,5},{7,8},{8,7},{9,10},{10,9},{11,... | collective-permute-start | bytes 1769480 | tf_op jit(solution)/shard_map/ppermute | solution.py:441
  6.4 5.6 %collective-permute-done.1.now_a = f32[1,4,72,256]{3,2,1,0:T(8,128)S(1)} collective-permute-done((f32[1,4,72,256]{3,2,1,0:T(8,128)S(1)}, f32[1,4,72,256]{3,2,1,0:T(8,128)S(1)}, u32[]{:S(2)}, u32[]{:S(2)}) %collective-permute-start.1) | collective-permute-done | bytes 294944 | tf_op jit(solution)/shard_map/ppermute | solution.py:450
  12.0 0.0 collective-permute-start.3
  12.0 1.6 %collective-permute-done.3.refs_2_ = f32[1,4,72,256]{3,2,1,0:T(8,128)S(1)} collective-permute-done((f32[1,4,72,256]{3,2,1,0:T(8,128)S(1)}, f32[1,4,72,256]{3,2,1,0:T(8,128)S(1)}, u32[]{:S(2)}, u32[]{:S(2)}) %collective-permute-start.3) | collective-permute-done | bytes 294944 | tf_op jit(solution)/shard_map/ppermute | solution.py:441
  13.6 1.6 %collective-permute-start.4 = (f32[1,4,64,256]{3,2,1,0:T(8,128)S(1)}, f32[1,4,64,256]{3,2,1,0:T(8,128)S(1)}, u32[]{:S(2)}, u32[]{:S(2)}) collective-permute-start(f32[1,4,64,256]{3,2,1,0:T(8,128)S(1)} %get-tuple-element.43), channel_id=1, source_target_pairs={{0,16},{16,0},{1,17},{17,1},{2,18},{18,2},{3,19},{19,3},{4,20},{20... | collective-permute-start | bytes 786440 | tf_op jit(solution)/shard_map/ppermute | solution.py:450
  15.2 0.7 pack_kernel.3
  15.9 0.5 collective-permute-start.10
  16.4 1.9 %collective-permute-start.9 = (f32[1,4,72,256]{3,2,1,0:T(8,128)S(1)}, f32[1,4,72,256]{3,2,1,0:T(8,128)S(1)}, u32[]{:S(2)}, u32[]{:S(2)}) collective-permute-start(f32[1,4,72,256]{3,2,1,0:T(8,128)S(1)} %collective-permute-done.1.now_a), channel_id=1, source_target_pairs={{1,2},{2,1},{3,4},{4,3},{5,6},{6,5},{7,8},{8,7},{9,10},{10,9},{11,... | collective-permute-start | bytes 884744 | tf_op jit(solution)/shard_map/ppermute | solution.py:441
  18.3 3.5 %collective-permute-done.5.refs_1_ = f32[2,4,72,256]{3,2,1,0:T(8,128)S(1)} collective-permute-done((f32[2,4,72,256]{3,2,1,0:T(8,128)S(1)}, f32[2,4,72,256]{3,2,1,0:T(8,128)S(1)}, u32[]{:S(2)}, u32[]{:S(2)}) %collective-permute-start.5) | collective-permute-done | bytes 589856 | tf_op jit(solution)/shard_map/ppermute | solution.py:441
  21.8 1.9 %collective-permute-start.2 = (f32[2,4,64,256]{3,2,1,0:T(8,128)S(1)}, f32[2,4,64,256]{3,2,1,0:T(8,128)S(1)}, u32[]{:S(2)}, u32[]{:S(2)}) collective-permute-start(f32[2,4,64,256]{3,2,1,0:T(8,128)S(1)} %get-tuple-element.41), channel_id=1, source_target_pairs={{1,2},{2,1},{3,4},{4,3},{5,6},{6,5},{7,8},{8,7},{9,10},{10,9},{11,... | collective-permute-start | bytes 1572872 | tf_op jit(solution)/shard_map/ppermute | solution.py:441
  23.7 0.0 collective-permute-done.refs_0_
  23.7 3.6 %slope_kernel.1 = (f32[4,136,256]{2,1,0:T(8,128)S(1)}, f32[4,136,256]{2,1,0:T(8,128)S(1)}, f32[4,136,256]{2,1,0:T(8,128)S(1)}) custom-call(s32[7]{0:T(128)S(1)} %stack.59.info, f32[4,256,256]{2,1,0:T(8,128)S(1)} %copy-done), custom_call_target="tpu_custom_call" | custom-call | flops 1024 | bytes 1024 | tf_op jit(solution)/shard_map/slope_kernel/pallas_call | solution.py:365
  27.4 0.0 collective-permute-done.4.now_b
  27.4 0.0 copy-start.3
  27.4 3.8 %far_kernel.1 = (f32[4,136,256]{2,1,0:T(8,128)S(1)}, f32[4,136,256]{2,1,0:T(8,128)S(1)}, f32[4,136,256]{2,1,0:T(8,128)S(1)}) custom-call(s32[7]{0:T(128)S(1)} %stack.59.info, f32[1,4,72,256]{3,2,1,0:T(8,128)S(1)} %collective-permute-done.1.now_a, f32[1,4,64,256]{3,2,1,0:T(8,128)S(1)} %collective-permute-done.4.now_b, f32[4,256,256]{2,1,0:T(8,128)S(1)} %copy-done, ...), custom_call_target="tpu_custom_call" | custom-call | flops 1024 | bytes 1024 | tf_op jit(solution)/shard_map/far_kernel/pallas_call | solution.py:365
  31.1 0.0 copy-start.2
  31.2 0.5 collective-permute-start.8
  31.6 3.5 %collective-permute-start.7 = (f32[1,4,64,256]{3,2,1,0:T(8,128)S(1)}, f32[1,4,64,256]{3,2,1,0:T(8,128)S(1)}, u32[]{:S(2)}, u32[]{:S(2)}) collective-permute-start(f32[1,4,64,256]{3,2,1,0:T(8,128)S(1)} %collective-permute-done.4.now_b), channel_id=1, source_target_pairs={{1,2},{2,1},{3,4},{4,3},{5,6},{6,5},{7,8},{8,7},{9,10},{10,9},{11,... | collective-permute-start | bytes 786440 | tf_op jit(solution)/shard_map/ppermute | solution.py:441
  35.1 0.0 collective-permute-done.9.refs_3_
  35.1 0.5 collective-permute-start.6
  35.6 3.8 %own_kernel.1 = (f32[4,136,256]{2,1,0:T(8,128)S(1)}, f32[4,136,256]{2,1,0:T(8,128)S(1)}) custom-call(s32[7]{0:T(128)S(1)} %stack.59.info, f32[4,256,256]{2,1,0:T(8,128)S(1)} %bitcast.24, f32[4,256,256]{2,1,0:T(8,128)S(1)} %copy-done, f32[4,136,256]{2,1,0:T(8,128)S(1)} %get-tuple-element.46.s2.refs_6_, f32[4,136,256]{2,1,0:T(8,128)S(1)} %get-tuple-element.47.s3.refs_7_), custom_call_target="tpu_custom_call" | custom-call | flops 1024 | bytes 1024 | tf_op jit(solution)/shard_map/own_kernel/pallas_call | solution.py:365
  39.4 0.0 collective-permute-done.10.refs_11_
  39.4 1.4 %finish_kernel.2 = (f32[2,4,136,256]{3,2,1,0:T(8,128)S(1)}, f32[4,136,256]{2,1,0:T(8,128)S(1)}, f32[4,136,256]{2,1,0:T(8,128)S(1)}, f32[2,4,64,256]{3,2,1,0:T(8,128)S(1)}) custom-call(s32[7]{0:T(128)S(1)} %stack.59.info, f32[2,4,136,256]{3,2,1,0:T(8,128)S(1)} %collective-permute-done.refs_0_, f32[2,4,72,256]{3,2,1,0:T(8,128)S(1)} %collective-permute-done.5.refs_1_, ...), custom_call_target="tpu_custom_call" | custom-call | flops 1024 | bytes 1024 | tf_op jit(solution)/shard_map/finish_kernel/pallas_call | solution.py:365
  40.8 1.9 %collective-permute-start.15 = (f32[2,4,64,256]{3,2,1,0:T(8,128)S(1)}, f32[2,4,64,256]{3,2,1,0:T(8,128)S(1)}, u32[]{:S(2)}, u32[]{:S(2)}) collective-permute-start(f32[2,4,64,256]{3,2,1,0:T(8,128)S(1)} %get-tuple-element.67), channel_id=1, source_target_pairs={{1,2},{2,1},{3,4},{4,3},{5,6},{6,5},{7,8},{8,7},{9,10},{10,9},{11,... | collective-permute-start | bytes 1572872 | tf_op jit(solution)/shard_map/ppermute | solution.py:441
  42.8 0.0 collective-permute-done.2.refs_1_
  42.8 1.9 %collective-permute-start.14 = (f32[2,4,64,256]{3,2,1,0:T(8,128)S(1)}, f32[2,4,64,256]{3,2,1,0:T(8,128)S(1)}, u32[]{:S(2)}, u32[]{:S(2)}) collective-permute-start(f32[2,4,64,256]{3,2,1,0:T(8,128)S(1)} %get-tuple-element.67), channel_id=1, source_target_pairs={{0,1},{1,0},{2,3},{3,2},{4,5},{5,4},{6,7},{7,6},{8,9},{9,8},{10,11... | collective-permute-start | bytes 1572872 | tf_op jit(solution)/shard_map/ppermute | solution.py:441
  44.6 0.3 collective-permute-done.7.refs_3_
  45.0 0.9 %collective-permute-done.8.refs_11_ = f32[2,4,64,256]{3,2,1,0:T(8,128)S(1)} collective-permute-done((f32[2,4,64,256]{3,2,1,0:T(8,128)S(1)}, f32[2,4,64,256]{3,2,1,0:T(8,128)S(1)}, u32[]{:S(2)}, u32[]{:S(2)}) %collective-permute-start.8) | collective-permute-done | bytes 524320 | tf_op jit(solution)/shard_map/ppermute | solution.py:450
  45.8 1.5 %finish_kernel.3 = (f32[2,4,136,256]{3,2,1,0:T(8,128)S(1)}, f32[4,136,256]{2,1,0:T(8,128)S(1)}, f32[4,136,256]{2,1,0:T(8,128)S(1)}, f32[2,4,64,256]{3,2,1,0:T(8,128)S(1)}) custom-call(s32[7]{0:T(128)S(1)} %stack.59.info, f32[2,4,136,256]{3,2,1,0:T(8,128)S(1)} %collective-permute-done.refs_0_, f32[2,4,64,256]{3,2,1,0:T(8,128)S(1)} %collective-permute-done.2.refs_1_, ...), custom_call_target="tpu_custom_call" | custom-call | flops 1024 | bytes 1024 | tf_op jit(solution)/shard_map/finish_kernel/pallas_call | solution.py:365
  47.3 1.9 %collective-permute-start.12 = (f32[2,4,64,256]{3,2,1,0:T(8,128)S(1)}, f32[2,4,64,256]{3,2,1,0:T(8,128)S(1)}, u32[]{:S(2)}, u32[]{:S(2)}) collective-permute-start(f32[2,4,64,256]{3,2,1,0:T(8,128)S(1)} %get-tuple-element.62), channel_id=1, source_target_pairs={{1,2},{2,1},{3,4},{4,3},{5,6},{6,5},{7,8},{8,7},{9,10},{10,9},{11,... | collective-permute-start | bytes 1572872 | tf_op jit(solution)/shard_map/ppermute | solution.py:441
  49.3 0.8 %collective-permute-start.11 = (f32[2,4,64,256]{3,2,1,0:T(8,128)S(1)}, f32[2,4,64,256]{3,2,1,0:T(8,128)S(1)}, u32[]{:S(2)}, u32[]{:S(2)}) collective-permute-start(f32[2,4,64,256]{3,2,1,0:T(8,128)S(1)} %get-tuple-element.62), channel_id=1, source_target_pairs={{0,1},{1,0},{2,3},{3,2},{4,5},{5,4},{6,7},{7,6},{8,9},{9,8},{10,11... | collective-permute-start | bytes 1572872 | tf_op jit(solution)/shard_map/ppermute | solution.py:441
  50.1 5.5 %start_kernel.1.refs_2_ = f32[2,4,128,256]{3,2,1,0:T(8,128)S(1)} custom-call(s32[7]{0:T(128)S(1)} %stack.59.info, f32[2,4,136,256]{3,2,1,0:T(8,128)S(1)} %get-tuple-element.63.refs_0_, f32[4,256,256]{2,1,0:T(8,128)S(1)} %bitcast.27, f32[4,256,256]{2,1,0:T(8,128)S(1)} %bitcast.20, f32[4,256,256]{2,1,0:T(8,128)S(1)} %copy-done.2, f32[4,256,256]{2,1,0:T(8,128)S(1)} %copy-done, ...), custom_call_target="tpu_custom_call" | custom-call | flops 1024 | bytes 1024 | tf_op jit(solution)/shard_map/start_kernel/pallas_call | solution.py:365
  55.6 6.9 %collective-permute-done.15.refs_1_ = f32[2,4,64,256]{3,2,1,0:T(8,128)S(1)} collective-permute-done((f32[2,4,64,256]{3,2,1,0:T(8,128)S(1)}, f32[2,4,64,256]{3,2,1,0:T(8,128)S(1)}, u32[]{:S(2)}, u32[]{:S(2)}) %collective-permute-start.15) | collective-permute-done | bytes 524320 | tf_op jit(solution)/shard_map/ppermute | solution.py:441
  62.6 0.0 collective-permute-done.14.refs_0_
  62.6 1.0 %end_kernel.3 = (f32[4,64,256]{2,1,0:T(8,128)S(1)}, f32[1,4,64,256]{3,2,1,0:T(8,128)S(1)}) custom-call(s32[7]{0:T(128)S(1)} %stack.59.info, f32[2,4,64,256]{3,2,1,0:T(8,128)S(1)} %collective-permute-done.14.refs_0_, f32[2,4,64,256]{3,2,1,0:T(8,128)S(1)} %collective-permute-done.15.refs_1_, f32[2,4,128,256]{3,2,1,0:T(8,128)S(1)} %start_kernel.1.refs_2_, ...), custom_call_target="tpu_custom_call" | custom-call | flops 1024 | bytes 1024 | tf_op jit(solution)/shard_map/end_kernel/pallas_call | solution.py:365
  63.6 1.2 %collective-permute-start.16 = (f32[4,64,256]{2,1,0:T(8,128)S(1)}, f32[4,64,256]{2,1,0:T(8,128)S(1)}, u32[]{:S(2)}, u32[]{:S(2)}) collective-permute-start(f32[4,64,256]{2,1,0:T(8,128)S(1)} %bitcast.31), channel_id=1, source_target_pairs={{0,16},{16,0},{1,17},{17,1},{2,18},{18,2},{3,19},{19,3},{4,20},{20... | collective-permute-start | bytes 786440 | tf_op jit(solution)/shard_map/ppermute | solution.py:450
  64.8 3.4 %collective-permute-done.12.refs_1_ = f32[2,4,64,256]{3,2,1,0:T(8,128)S(1)} collective-permute-done((f32[2,4,64,256]{3,2,1,0:T(8,128)S(1)}, f32[2,4,64,256]{3,2,1,0:T(8,128)S(1)}, u32[]{:S(2)}, u32[]{:S(2)}) %collective-permute-start.12) | collective-permute-done | bytes 524320 | tf_op jit(solution)/shard_map/ppermute | solution.py:441
  68.2 1.0 %end_kernel.2 = (f32[4,64,256]{2,1,0:T(8,128)S(1)}, f32[1,4,64,256]{3,2,1,0:T(8,128)S(1)}) custom-call(s32[7]{0:T(128)S(1)} %stack.59.info, f32[2,4,64,256]{3,2,1,0:T(8,128)S(1)} %collective-permute-done.11.refs_0_, f32[2,4,64,256]{3,2,1,0:T(8,128)S(1)} %collective-permute-done.12.refs_1_, f32[2,4,128,256]{3,2,1,0:T(8,128)S(1)} %start_kernel.1.refs_2_, ...), custom_call_target="tpu_custom_call" | custom-call | flops 1024 | bytes 1024 | tf_op jit(solution)/shard_map/end_kernel/pallas_call | solution.py:365
  69.2 1.2 %collective-permute-start.13 = (f32[4,64,256]{2,1,0:T(8,128)S(1)}, f32[4,64,256]{2,1,0:T(8,128)S(1)}, u32[]{:S(2)}, u32[]{:S(2)}) collective-permute-start(f32[4,64,256]{2,1,0:T(8,128)S(1)} %bitcast.32), channel_id=1, source_target_pairs={{0,16},{16,0},{1,17},{17,1},{2,18},{18,2},{3,19},{19,3},{4,20},{20... | collective-permute-start | bytes 786440 | tf_op jit(solution)/shard_map/ppermute | solution.py:450
  70.4 0.1 pad_add_fusion.rows
  70.5 1.4 %lay_kernel.2.refs_1_ = f32[4,256,256]{2,1,0:T(8,128)} custom-call(s32[3]{0:T(128)S(1)} %pad_add_fusion.rows, f32[4,64,256]{2,1,0:T(8,128)S(1)} %get-tuple-element.68.refs_0_, f32[4,64,256]{2,1,0:T(8,128)S(1)} %collective-permute-done.16.refs_1_, f32[4,64,256]{2,1,0:T(8,128)S(1)} %get-tuple-element.70.refs_2_), custom_call_target="tpu_custom_call" | custom-call | tf_op jit(solution)/shard_map/lay_kernel/pallas_call | solution.py:394
  71.9 3.7 %collective-permute-done.13.refs_0_ = f32[4,64,256]{2,1,0:T(8,128)S(1)} collective-permute-done((f32[4,64,256]{2,1,0:T(8,128)S(1)}, f32[4,64,256]{2,1,0:T(8,128)S(1)}, u32[]{:S(2)}, u32[]{:S(2)}) %collective-permute-start.13) | collective-permute-done | bytes 262176 | tf_op jit(solution)/shard_map/ppermute | solution.py:450
  75.6 0.7 lay_kernel.3
  (10 shorter events, 0.0 us)
Async XLA Ops:
  0.0 15.2 %copy-start.4 = (f32[1,4,256,256]{3,2,1,0:T(8,128)S(1)}, f32[1,4,256,256]{3,2,1,0:T(8,128)}, u32[]{:S(2)}) copy-start(f32[1,4,256,256]{3,2,1,0:T(8,128)} %param.5) | copy-start | bytes 3145732
  0.0 15.2 %copy-start.1 = (f32[1,4,256,256]{3,2,1,0:T(8,128)S(1)}, f32[1,4,256,256]{3,2,1,0:T(8,128)}, u32[]{:S(2)}) copy-start(f32[1,4,256,256]{3,2,1,0:T(8,128)} %param.9) | copy-start | bytes 3145732
  2.5 21.2 %copy-start = (f32[4,256,256]{2,1,0:T(8,128)S(1)}, f32[4,256,256]{2,1,0:T(8,128)}, u32[]{:S(2)}) copy-start(f32[4,256,256]{2,1,0:T(8,128)} %refs_5_.3) | copy-start | bytes 3145732
  2.5 21.2 %collective-permute-start = (f32[2,4,136,256]{3,2,1,0:T(8,128)S(1)}, f32[2,4,136,256]{3,2,1,0:T(8,128)S(1)}, u32[]{:S(2)}, u32[]{:S(2)}) collective-permute-start(f32[2,4,136,256]{3,2,1,0:T(8,128)S(1)} %get-tuple-element.38), channel_id=1, source_target_pairs={{0,1},{1,0},{2,3},{3,2},{4,5},{5,4},{6,7},{7,6},{8,9},{9,8},{10,11... | collective-permute-start | bytes 3342344 | tf_op jit(solution)/shard_map/ppermute | solution.py:441
  2.6 9.4 %collective-permute-start.1 = (f32[1,4,72,256]{3,2,1,0:T(8,128)S(1)}, f32[1,4,72,256]{3,2,1,0:T(8,128)S(1)}, u32[]{:S(2)}, u32[]{:S(2)}) collective-permute-start(f32[1,4,72,256]{3,2,1,0:T(8,128)S(1)} %get-tuple-element.40), channel_id=1, source_target_pairs={{0,16},{16,0},{1,17},{17,1},{2,18},{18,2},{3,19},{19,3},{4,20},{20... | collective-permute-start | bytes 884744 | tf_op jit(solution)/shard_map/ppermute | solution.py:450
  4.3 17.5 %collective-permute-start.5 = (f32[2,4,72,256]{3,2,1,0:T(8,128)S(1)}, f32[2,4,72,256]{3,2,1,0:T(8,128)S(1)}, u32[]{:S(2)}, u32[]{:S(2)}) collective-permute-start(f32[2,4,72,256]{3,2,1,0:T(8,128)S(1)} %get-tuple-element.44), channel_id=1, source_target_pairs={{1,2},{2,1},{3,4},{4,3},{5,6},{6,5},{7,8},{8,7},{9,10},{10,9},{11,... | collective-permute-start | bytes 1769480 | tf_op jit(solution)/shard_map/ppermute | solution.py:441
  12.0 1.6 %collective-permute-start.3 = (f32[1,4,72,256]{3,2,1,0:T(8,128)S(1)}, f32[1,4,72,256]{3,2,1,0:T(8,128)S(1)}, u32[]{:S(2)}, u32[]{:S(2)}) collective-permute-start(f32[1,4,72,256]{3,2,1,0:T(8,128)S(1)} %collective-permute-done.1.now_a), channel_id=1, source_target_pairs={{0,1},{1,0},{2,3},{3,2},{4,5},{5,4},{6,7},{7,6},{8,9},{9,8},{10,11... | collective-permute-start | bytes 884744 | tf_op jit(solution)/shard_map/ppermute | solution.py:441
  13.6 13.8 %collective-permute-start.4 = (f32[1,4,64,256]{3,2,1,0:T(8,128)S(1)}, f32[1,4,64,256]{3,2,1,0:T(8,128)S(1)}, u32[]{:S(2)}, u32[]{:S(2)}) collective-permute-start(f32[1,4,64,256]{3,2,1,0:T(8,128)S(1)} %get-tuple-element.43), channel_id=1, source_target_pairs={{0,16},{16,0},{1,17},{17,1},{2,18},{18,2},{3,19},{19,3},{4,20},{20... | collective-permute-start | bytes 786440 | tf_op jit(solution)/shard_map/ppermute | solution.py:450
  15.9 23.5 %collective-permute-start.10 = (f32[2,4,72,256]{3,2,1,0:T(8,128)S(1)}, f32[2,4,72,256]{3,2,1,0:T(8,128)S(1)}, u32[]{:S(2)}, u32[]{:S(2)}) collective-permute-start(f32[2,4,72,256]{3,2,1,0:T(8,128)S(1)} %get-tuple-element.58), channel_id=1, source_target_pairs={{0,16},{16,0},{1,17},{17,1},{2,18},{18,2},{3,19},{19,3},{4,20},{20... | collective-permute-start | bytes 1769480 | tf_op jit(solution)/shard_map/ppermute | solution.py:450
  16.4 18.7 %collective-permute-start.9 = (f32[1,4,72,256]{3,2,1,0:T(8,128)S(1)}, f32[1,4,72,256]{3,2,1,0:T(8,128)S(1)}, u32[]{:S(2)}, u32[]{:S(2)}) collective-permute-start(f32[1,4,72,256]{3,2,1,0:T(8,128)S(1)} %collective-permute-done.1.now_a), channel_id=1, source_target_pairs={{1,2},{2,1},{3,4},{4,3},{5,6},{6,5},{7,8},{8,7},{9,10},{10,9},{11,... | collective-permute-start | bytes 884744 | tf_op jit(solution)/shard_map/ppermute | solution.py:441
  21.8 21.0 %collective-permute-start.2 = (f32[2,4,64,256]{3,2,1,0:T(8,128)S(1)}, f32[2,4,64,256]{3,2,1,0:T(8,128)S(1)}, u32[]{:S(2)}, u32[]{:S(2)}) collective-permute-start(f32[2,4,64,256]{3,2,1,0:T(8,128)S(1)} %get-tuple-element.41), channel_id=1, source_target_pairs={{1,2},{2,1},{3,4},{4,3},{5,6},{6,5},{7,8},{8,7},{9,10},{10,9},{11,... | collective-permute-start | bytes 1572872 | tf_op jit(solution)/shard_map/ppermute | solution.py:441
  27.4 8.3 %copy-start.3 = (f32[1,4,256,256]{3,2,1,0:T(8,128)S(1)}, f32[1,4,256,256]{3,2,1,0:T(8,128)}, u32[]{:S(2)}) copy-start(f32[1,4,256,256]{3,2,1,0:T(8,128)} %param.6) | copy-start | bytes 3145732
  31.1 8.3 %copy-start.2 = (f32[4,256,256]{2,1,0:T(8,128)S(1)}, f32[4,256,256]{2,1,0:T(8,128)}, u32[]{:S(2)}) copy-start(f32[4,256,256]{2,1,0:T(8,128)} %refs_4_.5) | copy-start | bytes 3145732
  31.2 14.7 %collective-permute-start.8 = (f32[2,4,64,256]{3,2,1,0:T(8,128)S(1)}, f32[2,4,64,256]{3,2,1,0:T(8,128)S(1)}, u32[]{:S(2)}, u32[]{:S(2)}) collective-permute-start(f32[2,4,64,256]{3,2,1,0:T(8,128)S(1)} %get-tuple-element.54), channel_id=1, source_target_pairs={{0,16},{16,0},{1,17},{17,1},{2,18},{18,2},{3,19},{19,3},{4,20},{20... | collective-permute-start | bytes 1572872 | tf_op jit(solution)/shard_map/ppermute | solution.py:450
  31.6 13.3 %collective-permute-start.7 = (f32[1,4,64,256]{3,2,1,0:T(8,128)S(1)}, f32[1,4,64,256]{3,2,1,0:T(8,128)S(1)}, u32[]{:S(2)}, u32[]{:S(2)}) collective-permute-start(f32[1,4,64,256]{3,2,1,0:T(8,128)S(1)} %collective-permute-done.4.now_b), channel_id=1, source_target_pairs={{1,2},{2,1},{3,4},{4,3},{5,6},{6,5},{7,8},{8,7},{9,10},{10,9},{11,... | collective-permute-start | bytes 786440 | tf_op jit(solution)/shard_map/ppermute | solution.py:441
  35.1 9.8 %collective-permute-start.6 = (f32[1,4,64,256]{3,2,1,0:T(8,128)S(1)}, f32[1,4,64,256]{3,2,1,0:T(8,128)S(1)}, u32[]{:S(2)}, u32[]{:S(2)}) collective-permute-start(f32[1,4,64,256]{3,2,1,0:T(8,128)S(1)} %collective-permute-done.4.now_b), channel_id=1, source_target_pairs={{0,1},{1,0},{2,3},{3,2},{4,5},{5,4},{6,7},{7,6},{8,9},{9,8},{10,11... | collective-permute-start | bytes 786440 | tf_op jit(solution)/shard_map/ppermute | solution.py:441
  40.8 21.7 %collective-permute-start.15 = (f32[2,4,64,256]{3,2,1,0:T(8,128)S(1)}, f32[2,4,64,256]{3,2,1,0:T(8,128)S(1)}, u32[]{:S(2)}, u32[]{:S(2)}) collective-permute-start(f32[2,4,64,256]{3,2,1,0:T(8,128)S(1)} %get-tuple-element.67), channel_id=1, source_target_pairs={{1,2},{2,1},{3,4},{4,3},{5,6},{6,5},{7,8},{8,7},{9,10},{10,9},{11,... | collective-permute-start | bytes 1572872 | tf_op jit(solution)/shard_map/ppermute | solution.py:441
  42.8 19.8 %collective-permute-start.14 = (f32[2,4,64,256]{3,2,1,0:T(8,128)S(1)}, f32[2,4,64,256]{3,2,1,0:T(8,128)S(1)}, u32[]{:S(2)}, u32[]{:S(2)}) collective-permute-start(f32[2,4,64,256]{3,2,1,0:T(8,128)S(1)} %get-tuple-element.67), channel_id=1, source_target_pairs={{0,1},{1,0},{2,3},{3,2},{4,5},{5,4},{6,7},{7,6},{8,9},{9,8},{10,11... | collective-permute-start | bytes 1572872 | tf_op jit(solution)/shard_map/ppermute | solution.py:441
  47.3 20.9 %collective-permute-start.12 = (f32[2,4,64,256]{3,2,1,0:T(8,128)S(1)}, f32[2,4,64,256]{3,2,1,0:T(8,128)S(1)}, u32[]{:S(2)}, u32[]{:S(2)}) collective-permute-start(f32[2,4,64,256]{3,2,1,0:T(8,128)S(1)} %get-tuple-element.62), channel_id=1, source_target_pairs={{1,2},{2,1},{3,4},{4,3},{5,6},{6,5},{7,8},{8,7},{9,10},{10,9},{11,... | collective-permute-start | bytes 1572872 | tf_op jit(solution)/shard_map/ppermute | solution.py:441
  49.3 18.9 %collective-permute-start.11 = (f32[2,4,64,256]{3,2,1,0:T(8,128)S(1)}, f32[2,4,64,256]{3,2,1,0:T(8,128)S(1)}, u32[]{:S(2)}, u32[]{:S(2)}) collective-permute-start(f32[2,4,64,256]{3,2,1,0:T(8,128)S(1)} %get-tuple-element.62), channel_id=1, source_target_pairs={{0,1},{1,0},{2,3},{3,2},{4,5},{5,4},{6,7},{7,6},{8,9},{9,8},{10,11... | collective-permute-start | bytes 1572872 | tf_op jit(solution)/shard_map/ppermute | solution.py:441
  63.6 6.9 %collective-permute-start.16 = (f32[4,64,256]{2,1,0:T(8,128)S(1)}, f32[4,64,256]{2,1,0:T(8,128)S(1)}, u32[]{:S(2)}, u32[]{:S(2)}) collective-permute-start(f32[4,64,256]{2,1,0:T(8,128)S(1)} %bitcast.31), channel_id=1, source_target_pairs={{0,16},{16,0},{1,17},{17,1},{2,18},{18,2},{3,19},{19,3},{4,20},{20... | collective-permute-start | bytes 786440 | tf_op jit(solution)/shard_map/ppermute | solution.py:450
  69.2 6.4 %collective-permute-start.13 = (f32[4,64,256]{2,1,0:T(8,128)S(1)}, f32[4,64,256]{2,1,0:T(8,128)S(1)}, u32[]{:S(2)}, u32[]{:S(2)}) collective-permute-start(f32[4,64,256]{2,1,0:T(8,128)S(1)} %bitcast.32), channel_id=1, source_target_pairs={{0,16},{16,0},{1,17},{17,1},{2,18},{18,2},{3,19},{19,3},{4,20},{20... | collective-permute-start | bytes 786440 | tf_op jit(solution)/shard_map/ppermute | solution.py:450

commit v5 on v4

--- a/solution.py
+++ b/solution.py
@@ -148,7 +148,7 @@
             s3[:, aligned(SUB * i), cols] = three
         return 0
 
-    lax.fori_loop(0, width // SUB, body, 0)
+    lax.fori_loop(0, width // SUB, body, 0, unroll=1 if width % (2 * SUB) else 2)
 
 
 def local_loop(width, start, depth, buoy, s2, s3, image, along, scr):
@@ -163,7 +163,7 @@
             along[:, rows, cols] = one
         return 0
 
-    lax.fori_loop(0, width // SUB, body, 0)
+    lax.fori_loop(0, width // SUB, body, 0, unroll=1 if width % (2 * SUB) else 2)
 
 
 def own_kernel(width, info, now, buoy, s2, s3, image, along, scr):
@@ -268,13 +268,13 @@
         return 0
 
     if again:
-        lax.fori_loop(0, first_row // SUB, keep, 0)
+        lax.fori_loop(0, first_row // SUB, keep, 0, unroll=3)
 
     def send(i, _):
         faces[:, :, aligned(SUB * i), :] = following[:, :, aligned(offset + face_row + SUB * i), :]
         return 0
 
-    lax.fori_loop(0, faces.shape[2] // SUB, send, 0)
+    lax.fori_loop(0, faces.shape[2] // SUB, send, 0, unroll=2)
 
 
 def start_kernel(parts, width, core, info, *refs):

time: 76.6 us -> 76.6 us (level)
  no operation moved by 1% of the time
where the time goes in v5:
time: 76.6 us; the launch traced here: 76.3 us
  Pallas kernels  26.8 us (35%)
  waiting for transfers between devices  25.9 us (34%)
  starting transfers between devices  23.2 us (30%)
    pallas_call x10, Pallas kernels, call(): pl.pallas_call(kernel, name=kernel.func.__name__, out_shape=outs, in_spec...  24.6 us
    ppermute x11, starting transfers between devices, swap(): return lax.ppermute(stack, 'space', pairs)  16.6 us
    ppermute x11, waiting for transfers between devices, swap(): return lax.ppermute(stack, 'space', pairs)  15.8 us
    ppermute x6, waiting for transfers between devices, turn(): lax.ppermute(field, 'probe', [(i, (i + s) % parts) for i in range(parts)])  10.1 us
    ppermute x6, starting transfers between devices, turn(): lax.ppermute(field, 'probe', [(i, (i + s) % parts) for i in range(parts)])  6.65 us
    pallas_call x2, Pallas kernels, lay(): pl.pallas_call(functools.partial(lay_kernel, len(pieces)), name='lay_kern...  2.16 us
  transfers between devices with their start and end apart: 17, of which 8 were waited for; matrix products, arithmetic and copies ran while one was open for 0% of the time, Pallas kernels for 31%

profile of v5, /device:TPU:4, one launch (start us, length us, event | category | flops | bytes accessed | tf_op | source)
XLA Modules:
  0.0 76.3 jit_solution(8992370746572770628)
XLA Ops:
  0.0 0.1 stack.59.info
  0.1 2.4 %pack_kernel.2 = (f32[2,4,136,256]{3,2,1,0:T(8,128)S(1)}, f32[2,4,72,256]{3,2,1,0:T(8,128)S(1)}, f32[2,4,64,256]{3,2,1,0:T(8,128)S(1)}, f32[1,4,72,256]{3,2,1,0:T(8,128)S(1)}, f32[1,4,64,256]{3,2,1,0:T(8,128)S(1)}) custom-call(s32[7]{0:T(128)S(1)} %stack.59.info, f32[4,256,256]{2,1,0:T(8,128)} %refs_5_.3, f32[4,256,256]{2,1,0:T(8,128)} %bitcast.23), custom_call_target="tpu_custom_call" | custom-call | flops 1024 | bytes 1024 | tf_op jit(solution)/shard_map/pack_kernel/pallas_call | solution.py:365
  2.5 0.0 copy-start
  2.5 0.1 collective-permute-start
  2.6 1.7 %collective-permute-start.1 = (f32[1,4,72,256]{3,2,1,0:T(8,128)S(1)}, f32[1,4,72,256]{3,2,1,0:T(8,128)S(1)}, u32[]{:S(2)}, u32[]{:S(2)}) collective-permute-start(f32[1,4,72,256]{3,2,1,0:T(8,128)S(1)} %get-tuple-element.40), channel_id=1, source_target_pairs={{0,16},{16,0},{1,17},{17,1},{2,18},{18,2},{3,19},{19,3},{4,20},{20... | collective-permute-start | bytes 884744 | tf_op jit(solution)/shard_map/ppermute | solution.py:450
  4.3 2.2 %collective-permute-start.5 = (f32[2,4,72,256]{3,2,1,0:T(8,128)S(1)}, f32[2,4,72,256]{3,2,1,0:T(8,128)S(1)}, u32[]{:S(2)}, u32[]{:S(2)}) collective-permute-start(f32[2,4,72,256]{3,2,1,0:T(8,128)S(1)} %get-tuple-element.44), channel_id=1, source_target_pairs={{1,2},{2,1},{3,4},{4,3},{5,6},{6,5},{7,8},{8,7},{9,10},{10,9},{11,... | collective-permute-start | bytes 1769480 | tf_op jit(solution)/shard_map/ppermute | solution.py:441
  6.4 5.6 %collective-permute-done.1.now_a = f32[1,4,72,256]{3,2,1,0:T(8,128)S(1)} collective-permute-done((f32[1,4,72,256]{3,2,1,0:T(8,128)S(1)}, f32[1,4,72,256]{3,2,1,0:T(8,128)S(1)}, u32[]{:S(2)}, u32[]{:S(2)}) %collective-permute-start.1) | collective-permute-done | bytes 294944 | tf_op jit(solution)/shard_map/ppermute | solution.py:450
  12.0 0.0 collective-permute-start.3
  12.0 1.6 %collective-permute-done.3.refs_2_ = f32[1,4,72,256]{3,2,1,0:T(8,128)S(1)} collective-permute-done((f32[1,4,72,256]{3,2,1,0:T(8,128)S(1)}, f32[1,4,72,256]{3,2,1,0:T(8,128)S(1)}, u32[]{:S(2)}, u32[]{:S(2)}) %collective-permute-start.3) | collective-permute-done | bytes 294944 | tf_op jit(solution)/shard_map/ppermute | solution.py:441
  13.6 1.6 %collective-permute-start.4 = (f32[1,4,64,256]{3,2,1,0:T(8,128)S(1)}, f32[1,4,64,256]{3,2,1,0:T(8,128)S(1)}, u32[]{:S(2)}, u32[]{:S(2)}) collective-permute-start(f32[1,4,64,256]{3,2,1,0:T(8,128)S(1)} %get-tuple-element.43), channel_id=1, source_target_pairs={{0,16},{16,0},{1,17},{17,1},{2,18},{18,2},{3,19},{19,3},{4,20},{20... | collective-permute-start | bytes 786440 | tf_op jit(solution)/shard_map/ppermute | solution.py:450
  15.2 0.7 pack_kernel.3
  15.9 0.5 collective-permute-start.10
  16.4 1.9 %collective-permute-start.9 = (f32[1,4,72,256]{3,2,1,0:T(8,128)S(1)}, f32[1,4,72,256]{3,2,1,0:T(8,128)S(1)}, u32[]{:S(2)}, u32[]{:S(2)}) collective-permute-start(f32[1,4,72,256]{3,2,1,0:T(8,128)S(1)} %collective-permute-done.1.now_a), channel_id=1, source_target_pairs={{1,2},{2,1},{3,4},{4,3},{5,6},{6,5},{7,8},{8,7},{9,10},{10,9},{11,... | collective-permute-start | bytes 884744 | tf_op jit(solution)/shard_map/ppermute | solution.py:441
  18.3 3.5 %collective-permute-done.5.refs_1_ = f32[2,4,72,256]{3,2,1,0:T(8,128)S(1)} collective-permute-done((f32[2,4,72,256]{3,2,1,0:T(8,128)S(1)}, f32[2,4,72,256]{3,2,1,0:T(8,128)S(1)}, u32[]{:S(2)}, u32[]{:S(2)}) %collective-permute-start.5) | collective-permute-done | bytes 589856 | tf_op jit(solution)/shard_map/ppermute | solution.py:441
  21.8 1.9 %collective-permute-start.2 = (f32[2,4,64,256]{3,2,1,0:T(8,128)S(1)}, f32[2,4,64,256]{3,2,1,0:T(8,128)S(1)}, u32[]{:S(2)}, u32[]{:S(2)}) collective-permute-start(f32[2,4,64,256]{3,2,1,0:T(8,128)S(1)} %get-tuple-element.41), channel_id=1, source_target_pairs={{1,2},{2,1},{3,4},{4,3},{5,6},{6,5},{7,8},{8,7},{9,10},{10,9},{11,... | collective-permute-start | bytes 1572872 | tf_op jit(solution)/shard_map/ppermute | solution.py:441
  23.7 0.0 collective-permute-done.refs_0_
  23.7 3.6 %slope_kernel.1 = (f32[4,136,256]{2,1,0:T(8,128)S(1)}, f32[4,136,256]{2,1,0:T(8,128)S(1)}, f32[4,136,256]{2,1,0:T(8,128)S(1)}) custom-call(s32[7]{0:T(128)S(1)} %stack.59.info, f32[4,256,256]{2,1,0:T(8,128)S(1)} %copy-done), custom_call_target="tpu_custom_call" | custom-call | flops 1024 | bytes 1024 | tf_op jit(solution)/shard_map/slope_kernel/pallas_call | solution.py:365
  27.4 0.0 collective-permute-done.4.now_b
  27.4 0.0 copy-start.3
  27.4 3.8 %far_kernel.1 = (f32[4,136,256]{2,1,0:T(8,128)S(1)}, f32[4,136,256]{2,1,0:T(8,128)S(1)}, f32[4,136,256]{2,1,0:T(8,128)S(1)}) custom-call(s32[7]{0:T(128)S(1)} %stack.59.info, f32[1,4,72,256]{3,2,1,0:T(8,128)S(1)} %collective-permute-done.1.now_a, f32[1,4,64,256]{3,2,1,0:T(8,128)S(1)} %collective-permute-done.4.now_b, f32[4,256,256]{2,1,0:T(8,128)S(1)} %copy-done, ...), custom_call_target="tpu_custom_call" | custom-call | flops 1024 | bytes 1024 | tf_op jit(solution)/shard_map/far_kernel/pallas_call | solution.py:365
  31.1 0.0 copy-start.2
  31.2 0.5 collective-permute-start.8
  31.6 3.5 %collective-permute-start.7 = (f32[1,4,64,256]{3,2,1,0:T(8,128)S(1)}, f32[1,4,64,256]{3,2,1,0:T(8,128)S(1)}, u32[]{:S(2)}, u32[]{:S(2)}) collective-permute-start(f32[1,4,64,256]{3,2,1,0:T(8,128)S(1)} %collective-permute-done.4.now_b), channel_id=1, source_target_pairs={{1,2},{2,1},{3,4},{4,3},{5,6},{6,5},{7,8},{8,7},{9,10},{10,9},{11,... | collective-permute-start | bytes 786440 | tf_op jit(solution)/shard_map/ppermute | solution.py:441
  35.1 0.0 collective-permute-done.9.refs_3_
  35.1 0.5 collective-permute-start.6
  35.6 3.8 %own_kernel.1 = (f32[4,136,256]{2,1,0:T(8,128)S(1)}, f32[4,136,256]{2,1,0:T(8,128)S(1)}) custom-call(s32[7]{0:T(128)S(1)} %stack.59.info, f32[4,256,256]{2,1,0:T(8,128)S(1)} %bitcast.24, f32[4,256,256]{2,1,0:T(8,128)S(1)} %copy-done, f32[4,136,256]{2,1,0:T(8,128)S(1)} %get-tuple-element.46.s2.refs_6_, f32[4,136,256]{2,1,0:T(8,128)S(1)} %get-tuple-element.47.s3.refs_7_), custom_call_target="tpu_custom_call" | custom-call | flops 1024 | bytes 1024 | tf_op jit(solution)/shard_map/own_kernel/pallas_call | solution.py:365
  39.4 0.0 collective-permute-done.10.refs_11_
  39.4 1.4 %finish_kernel.2 = (f32[2,4,136,256]{3,2,1,0:T(8,128)S(1)}, f32[4,136,256]{2,1,0:T(8,128)S(1)}, f32[4,136,256]{2,1,0:T(8,128)S(1)}, f32[2,4,64,256]{3,2,1,0:T(8,128)S(1)}) custom-call(s32[7]{0:T(128)S(1)} %stack.59.info, f32[2,4,136,256]{3,2,1,0:T(8,128)S(1)} %collective-permute-done.refs_0_, f32[2,4,72,256]{3,2,1,0:T(8,128)S(1)} %collective-permute-done.5.refs_1_, ...), custom_call_target="tpu_custom_call" | custom-call | flops 1024 | bytes 1024 | tf_op jit(solution)/shard_map/finish_kernel/pallas_call | solution.py:365
  40.8 1.9 %collective-permute-start.15 = (f32[2,4,64,256]{3,2,1,0:T(8,128)S(1)}, f32[2,4,64,256]{3,2,1,0:T(8,128)S(1)}, u32[]{:S(2)}, u32[]{:S(2)}) collective-permute-start(f32[2,4,64,256]{3,2,1,0:T(8,128)S(1)} %get-tuple-element.67), channel_id=1, source_target_pairs={{1,2},{2,1},{3,4},{4,3},{5,6},{6,5},{7,8},{8,7},{9,10},{10,9},{11,... | collective-permute-start | bytes 1572872 | tf_op jit(solution)/shard_map/ppermute | solution.py:441
  42.7 1.9 %collective-permute-start.14 = (f32[2,4,64,256]{3,2,1,0:T(8,128)S(1)}, f32[2,4,64,256]{3,2,1,0:T(8,128)S(1)}, u32[]{:S(2)}, u32[]{:S(2)}) collective-permute-start(f32[2,4,64,256]{3,2,1,0:T(8,128)S(1)} %get-tuple-element.67), channel_id=1, source_target_pairs={{0,1},{1,0},{2,3},{3,2},{4,5},{5,4},{6,7},{7,6},{8,9},{9,8},{10,11... | collective-permute-start | bytes 1572872 | tf_op jit(solution)/shard_map/ppermute | solution.py:441
  44.6 0.3 collective-permute-done.7.refs_3_
  45.0 0.9 %collective-permute-done.8.refs_11_ = f32[2,4,64,256]{3,2,1,0:T(8,128)S(1)} collective-permute-done((f32[2,4,64,256]{3,2,1,0:T(8,128)S(1)}, f32[2,4,64,256]{3,2,1,0:T(8,128)S(1)}, u32[]{:S(2)}, u32[]{:S(2)}) %collective-permute-start.8) | collective-permute-done | bytes 524320 | tf_op jit(solution)/shard_map/ppermute | solution.py:450
  45.8 1.5 %finish_kernel.3 = (f32[2,4,136,256]{3,2,1,0:T(8,128)S(1)}, f32[4,136,256]{2,1,0:T(8,128)S(1)}, f32[4,136,256]{2,1,0:T(8,128)S(1)}, f32[2,4,64,256]{3,2,1,0:T(8,128)S(1)}) custom-call(s32[7]{0:T(128)S(1)} %stack.59.info, f32[2,4,136,256]{3,2,1,0:T(8,128)S(1)} %collective-permute-done.refs_0_, f32[2,4,64,256]{3,2,1,0:T(8,128)S(1)} %collective-permute-done.2.refs_1_, ...), custom_call_target="tpu_custom_call" | custom-call | flops 1024 | bytes 1024 | tf_op jit(solution)/shard_map/finish_kernel/pallas_call | solution.py:365
  47.3 1.9 %collective-permute-start.12 = (f32[2,4,64,256]{3,2,1,0:T(8,128)S(1)}, f32[2,4,64,256]{3,2,1,0:T(8,128)S(1)}, u32[]{:S(2)}, u32[]{:S(2)}) collective-permute-start(f32[2,4,64,256]{3,2,1,0:T(8,128)S(1)} %get-tuple-element.62), channel_id=1, source_target_pairs={{1,2},{2,1},{3,4},{4,3},{5,6},{6,5},{7,8},{8,7},{9,10},{10,9},{11,... | collective-permute-start | bytes 1572872 | tf_op jit(solution)/shard_map/ppermute | solution.py:441
  49.2 0.8 %collective-permute-start.11 = (f32[2,4,64,256]{3,2,1,0:T(8,128)S(1)}, f32[2,4,64,256]{3,2,1,0:T(8,128)S(1)}, u32[]{:S(2)}, u32[]{:S(2)}) collective-permute-start(f32[2,4,64,256]{3,2,1,0:T(8,128)S(1)} %get-tuple-element.62), channel_id=1, source_target_pairs={{0,1},{1,0},{2,3},{3,2},{4,5},{5,4},{6,7},{7,6},{8,9},{9,8},{10,11... | collective-permute-start | bytes 1572872 | tf_op jit(solution)/shard_map/ppermute | solution.py:441
  50.0 5.5 %start_kernel.1.refs_2_ = f32[2,4,128,256]{3,2,1,0:T(8,128)S(1)} custom-call(s32[7]{0:T(128)S(1)} %stack.59.info, f32[2,4,136,256]{3,2,1,0:T(8,128)S(1)} %get-tuple-element.63.refs_0_, f32[4,256,256]{2,1,0:T(8,128)S(1)} %bitcast.27, f32[4,256,256]{2,1,0:T(8,128)S(1)} %bitcast.20, f32[4,256,256]{2,1,0:T(8,128)S(1)} %copy-done.2, f32[4,256,256]{2,1,0:T(8,128)S(1)} %copy-done, ...), custom_call_target="tpu_custom_call" | custom-call | flops 1024 | bytes 1024 | tf_op jit(solution)/shard_map/start_kernel/pallas_call | solution.py:365
  55.6 7.0 %collective-permute-done.15.refs_1_ = f32[2,4,64,256]{3,2,1,0:T(8,128)S(1)} collective-permute-done((f32[2,4,64,256]{3,2,1,0:T(8,128)S(1)}, f32[2,4,64,256]{3,2,1,0:T(8,128)S(1)}, u32[]{:S(2)}, u32[]{:S(2)}) %collective-permute-start.15) | collective-permute-done | bytes 524320 | tf_op jit(solution)/shard_map/ppermute | solution.py:441
  62.5 0.0 collective-permute-done.14.refs_0_
  62.5 1.0 %end_kernel.3 = (f32[4,64,256]{2,1,0:T(8,128)S(1)}, f32[1,4,64,256]{3,2,1,0:T(8,128)S(1)}) custom-call(s32[7]{0:T(128)S(1)} %stack.59.info, f32[2,4,64,256]{3,2,1,0:T(8,128)S(1)} %collective-permute-done.14.refs_0_, f32[2,4,64,256]{3,2,1,0:T(8,128)S(1)} %collective-permute-done.15.refs_1_, f32[2,4,128,256]{3,2,1,0:T(8,128)S(1)} %start_kernel.1.refs_2_, ...), custom_call_target="tpu_custom_call" | custom-call | flops 1024 | bytes 1024 | tf_op jit(solution)/shard_map/end_kernel/pallas_call | solution.py:365
  63.6 1.2 %collective-permute-start.16 = (f32[4,64,256]{2,1,0:T(8,128)S(1)}, f32[4,64,256]{2,1,0:T(8,128)S(1)}, u32[]{:S(2)}, u32[]{:S(2)}) collective-permute-start(f32[4,64,256]{2,1,0:T(8,128)S(1)} %bitcast.31), channel_id=1, source_target_pairs={{0,16},{16,0},{1,17},{17,1},{2,18},{18,2},{3,19},{19,3},{4,20},{20... | collective-permute-start | bytes 786440 | tf_op jit(solution)/shard_map/ppermute | solution.py:450
  64.8 3.4 %collective-permute-done.12.refs_1_ = f32[2,4,64,256]{3,2,1,0:T(8,128)S(1)} collective-permute-done((f32[2,4,64,256]{3,2,1,0:T(8,128)S(1)}, f32[2,4,64,256]{3,2,1,0:T(8,128)S(1)}, u32[]{:S(2)}, u32[]{:S(2)}) %collective-permute-start.12) | collective-permute-done | bytes 524320 | tf_op jit(solution)/shard_map/ppermute | solution.py:441
  68.2 1.0 %end_kernel.2 = (f32[4,64,256]{2,1,0:T(8,128)S(1)}, f32[1,4,64,256]{3,2,1,0:T(8,128)S(1)}) custom-call(s32[7]{0:T(128)S(1)} %stack.59.info, f32[2,4,64,256]{3,2,1,0:T(8,128)S(1)} %collective-permute-done.11.refs_0_, f32[2,4,64,256]{3,2,1,0:T(8,128)S(1)} %collective-permute-done.12.refs_1_, f32[2,4,128,256]{3,2,1,0:T(8,128)S(1)} %start_kernel.1.refs_2_, ...), custom_call_target="tpu_custom_call" | custom-call | flops 1024 | bytes 1024 | tf_op jit(solution)/shard_map/end_kernel/pallas_call | solution.py:365
  69.2 1.2 %collective-permute-start.13 = (f32[4,64,256]{2,1,0:T(8,128)S(1)}, f32[4,64,256]{2,1,0:T(8,128)S(1)}, u32[]{:S(2)}, u32[]{:S(2)}) collective-permute-start(f32[4,64,256]{2,1,0:T(8,128)S(1)} %bitcast.32), channel_id=1, source_target_pairs={{0,16},{16,0},{1,17},{17,1},{2,18},{18,2},{3,19},{19,3},{4,20},{20... | collective-permute-start | bytes 786440 | tf_op jit(solution)/shard_map/ppermute | solution.py:450
  70.4 0.1 pad_add_fusion.rows
  70.5 0.0 collective-permute-done.16.refs_1_
  70.5 1.4 %lay_kernel.2.refs_1_ = f32[4,256,256]{2,1,0:T(8,128)} custom-call(s32[3]{0:T(128)S(1)} %pad_add_fusion.rows, f32[4,64,256]{2,1,0:T(8,128)S(1)} %get-tuple-element.68.refs_0_, f32[4,64,256]{2,1,0:T(8,128)S(1)} %collective-permute-done.16.refs_1_, f32[4,64,256]{2,1,0:T(8,128)S(1)} %get-tuple-element.70.refs_2_), custom_call_target="tpu_custom_call" | custom-call | tf_op jit(solution)/shard_map/lay_kernel/pallas_call | solution.py:394
  71.9 3.7 %collective-permute-done.13.refs_0_ = f32[4,64,256]{2,1,0:T(8,128)S(1)} collective-permute-done((f32[4,64,256]{2,1,0:T(8,128)S(1)}, f32[4,64,256]{2,1,0:T(8,128)S(1)}, u32[]{:S(2)}, u32[]{:S(2)}) %collective-permute-start.13) | collective-permute-done | bytes 262176 | tf_op jit(solution)/shard_map/ppermute | solution.py:450
  75.6 0.7 lay_kernel.3
  (10 shorter events, 0.0 us)
Async XLA Ops:
  0.0 15.2 %copy-start.4 = (f32[1,4,256,256]{3,2,1,0:T(8,128)S(1)}, f32[1,4,256,256]{3,2,1,0:T(8,128)}, u32[]{:S(2)}) copy-start(f32[1,4,256,256]{3,2,1,0:T(8,128)} %param.5) | copy-start | bytes 3145732
  0.0 15.2 %copy-start.1 = (f32[1,4,256,256]{3,2,1,0:T(8,128)S(1)}, f32[1,4,256,256]{3,2,1,0:T(8,128)}, u32[]{:S(2)}) copy-start(f32[1,4,256,256]{3,2,1,0:T(8,128)} %param.9) | copy-start | bytes 3145732
  2.5 21.2 %copy-start = (f32[4,256,256]{2,1,0:T(8,128)S(1)}, f32[4,256,256]{2,1,0:T(8,128)}, u32[]{:S(2)}) copy-start(f32[4,256,256]{2,1,0:T(8,128)} %refs_5_.3) | copy-start | bytes 3145732
  2.5 21.2 %collective-permute-start = (f32[2,4,136,256]{3,2,1,0:T(8,128)S(1)}, f32[2,4,136,256]{3,2,1,0:T(8,128)S(1)}, u32[]{:S(2)}, u32[]{:S(2)}) collective-permute-start(f32[2,4,136,256]{3,2,1,0:T(8,128)S(1)} %get-tuple-element.38), channel_id=1, source_target_pairs={{0,1},{1,0},{2,3},{3,2},{4,5},{5,4},{6,7},{7,6},{8,9},{9,8},{10,11... | collective-permute-start | bytes 3342344 | tf_op jit(solution)/shard_map/ppermute | solution.py:441
  2.6 9.4 %collective-permute-start.1 = (f32[1,4,72,256]{3,2,1,0:T(8,128)S(1)}, f32[1,4,72,256]{3,2,1,0:T(8,128)S(1)}, u32[]{:S(2)}, u32[]{:S(2)}) collective-permute-start(f32[1,4,72,256]{3,2,1,0:T(8,128)S(1)} %get-tuple-element.40), channel_id=1, source_target_pairs={{0,16},{16,0},{1,17},{17,1},{2,18},{18,2},{3,19},{19,3},{4,20},{20... | collective-permute-start | bytes 884744 | tf_op jit(solution)/shard_map/ppermute | solution.py:450
  4.3 17.5 %collective-permute-start.5 = (f32[2,4,72,256]{3,2,1,0:T(8,128)S(1)}, f32[2,4,72,256]{3,2,1,0:T(8,128)S(1)}, u32[]{:S(2)}, u32[]{:S(2)}) collective-permute-start(f32[2,4,72,256]{3,2,1,0:T(8,128)S(1)} %get-tuple-element.44), channel_id=1, source_target_pairs={{1,2},{2,1},{3,4},{4,3},{5,6},{6,5},{7,8},{8,7},{9,10},{10,9},{11,... | collective-permute-start | bytes 1769480 | tf_op jit(solution)/shard_map/ppermute | solution.py:441
  12.0 1.6 %collective-permute-start.3 = (f32[1,4,72,256]{3,2,1,0:T(8,128)S(1)}, f32[1,4,72,256]{3,2,1,0:T(8,128)S(1)}, u32[]{:S(2)}, u32[]{:S(2)}) collective-permute-start(f32[1,4,72,256]{3,2,1,0:T(8,128)S(1)} %collective-permute-done.1.now_a), channel_id=1, source_target_pairs={{0,1},{1,0},{2,3},{3,2},{4,5},{5,4},{6,7},{7,6},{8,9},{9,8},{10,11... | collective-permute-start | bytes 884744 | tf_op jit(solution)/shard_map/ppermute | solution.py:441
  13.6 13.8 %collective-permute-start.4 = (f32[1,4,64,256]{3,2,1,0:T(8,128)S(1)}, f32[1,4,64,256]{3,2,1,0:T(8,128)S(1)}, u32[]{:S(2)}, u32[]{:S(2)}) collective-permute-start(f32[1,4,64,256]{3,2,1,0:T(8,128)S(1)} %get-tuple-element.43), channel_id=1, source_target_pairs={{0,16},{16,0},{1,17},{17,1},{2,18},{18,2},{3,19},{19,3},{4,20},{20... | collective-permute-start | bytes 786440 | tf_op jit(solution)/shard_map/ppermute | solution.py:450
  15.9 23.5 %collective-permute-start.10 = (f32[2,4,72,256]{3,2,1,0:T(8,128)S(1)}, f32[2,4,72,256]{3,2,1,0:T(8,128)S(1)}, u32[]{:S(2)}, u32[]{:S(2)}) collective-permute-start(f32[2,4,72,256]{3,2,1,0:T(8,128)S(1)} %get-tuple-element.58), channel_id=1, source_target_pairs={{0,16},{16,0},{1,17},{17,1},{2,18},{18,2},{3,19},{19,3},{4,20},{20... | collective-permute-start | bytes 1769480 | tf_op jit(solution)/shard_map/ppermute | solution.py:450
  16.4 18.7 %collective-permute-start.9 = (f32[1,4,72,256]{3,2,1,0:T(8,128)S(1)}, f32[1,4,72,256]{3,2,1,0:T(8,128)S(1)}, u32[]{:S(2)}, u32[]{:S(2)}) collective-permute-start(f32[1,4,72,256]{3,2,1,0:T(8,128)S(1)} %collective-permute-done.1.now_a), channel_id=1, source_target_pairs={{1,2},{2,1},{3,4},{4,3},{5,6},{6,5},{7,8},{8,7},{9,10},{10,9},{11,... | collective-permute-start | bytes 884744 | tf_op jit(solution)/shard_map/ppermute | solution.py:441
  21.8 21.0 %collective-permute-start.2 = (f32[2,4,64,256]{3,2,1,0:T(8,128)S(1)}, f32[2,4,64,256]{3,2,1,0:T(8,128)S(1)}, u32[]{:S(2)}, u32[]{:S(2)}) collective-permute-start(f32[2,4,64,256]{3,2,1,0:T(8,128)S(1)} %get-tuple-element.41), channel_id=1, source_target_pairs={{1,2},{2,1},{3,4},{4,3},{5,6},{6,5},{7,8},{8,7},{9,10},{10,9},{11,... | collective-permute-start | bytes 1572872 | tf_op jit(solution)/shard_map/ppermute | solution.py:441
  27.4 8.3 %copy-start.3 = (f32[1,4,256,256]{3,2,1,0:T(8,128)S(1)}, f32[1,4,256,256]{3,2,1,0:T(8,128)}, u32[]{:S(2)}) copy-start(f32[1,4,256,256]{3,2,1,0:T(8,128)} %param.6) | copy-start | bytes 3145732
  31.1 8.3 %copy-start.2 = (f32[4,256,256]{2,1,0:T(8,128)S(1)}, f32[4,256,256]{2,1,0:T(8,128)}, u32[]{:S(2)}) copy-start(f32[4,256,256]{2,1,0:T(8,128)} %refs_4_.5) | copy-start | bytes 3145732
  31.2 14.7 %collective-permute-start.8 = (f32[2,4,64,256]{3,2,1,0:T(8,128)S(1)}, f32[2,4,64,256]{3,2,1,0:T(8,128)S(1)}, u32[]{:S(2)}, u32[]{:S(2)}) collective-permute-start(f32[2,4,64,256]{3,2,1,0:T(8,128)S(1)} %get-tuple-element.54), channel_id=1, source_target_pairs={{0,16},{16,0},{1,17},{17,1},{2,18},{18,2},{3,19},{19,3},{4,20},{20... | collective-permute-start | bytes 1572872 | tf_op jit(solution)/shard_map/ppermute | solution.py:450
  31.6 13.3 %collective-permute-start.7 = (f32[1,4,64,256]{3,2,1,0:T(8,128)S(1)}, f32[1,4,64,256]{3,2,1,0:T(8,128)S(1)}, u32[]{:S(2)}, u32[]{:S(2)}) collective-permute-start(f32[1,4,64,256]{3,2,1,0:T(8,128)S(1)} %collective-permute-done.4.now_b), channel_id=1, source_target_pairs={{1,2},{2,1},{3,4},{4,3},{5,6},{6,5},{7,8},{8,7},{9,10},{10,9},{11,... | collective-permute-start | bytes 786440 | tf_op jit(solution)/shard_map/ppermute | solution.py:441
  35.1 9.8 %collective-permute-start.6 = (f32[1,4,64,256]{3,2,1,0:T(8,128)S(1)}, f32[1,4,64,256]{3,2,1,0:T(8,128)S(1)}, u32[]{:S(2)}, u32[]{:S(2)}) collective-permute-start(f32[1,4,64,256]{3,2,1,0:T(8,128)S(1)} %collective-permute-done.4.now_b), channel_id=1, source_target_pairs={{0,1},{1,0},{2,3},{3,2},{4,5},{5,4},{6,7},{7,6},{8,9},{9,8},{10,11... | collective-permute-start | bytes 786440 | tf_op jit(solution)/shard_map/ppermute | solution.py:441
  40.8 21.7 %collective-permute-start.15 = (f32[2,4,64,256]{3,2,1,0:T(8,128)S(1)}, f32[2,4,64,256]{3,2,1,0:T(8,128)S(1)}, u32[]{:S(2)}, u32[]{:S(2)}) collective-permute-start(f32[2,4,64,256]{3,2,1,0:T(8,128)S(1)} %get-tuple-element.67), channel_id=1, source_target_pairs={{1,2},{2,1},{3,4},{4,3},{5,6},{6,5},{7,8},{8,7},{9,10},{10,9},{11,... | collective-permute-start | bytes 1572872 | tf_op jit(solution)/shard_map/ppermute | solution.py:441
  42.7 19.8 %collective-permute-start.14 = (f32[2,4,64,256]{3,2,1,0:T(8,128)S(1)}, f32[2,4,64,256]{3,2,1,0:T(8,128)S(1)}, u32[]{:S(2)}, u32[]{:S(2)}) collective-permute-start(f32[2,4,64,256]{3,2,1,0:T(8,128)S(1)} %get-tuple-element.67), channel_id=1, source_target_pairs={{0,1},{1,0},{2,3},{3,2},{4,5},{5,4},{6,7},{7,6},{8,9},{9,8},{10,11... | collective-permute-start | bytes 1572872 | tf_op jit(solution)/shard_map/ppermute | solution.py:441
  47.3 20.9 %collective-permute-start.12 = (f32[2,4,64,256]{3,2,1,0:T(8,128)S(1)}, f32[2,4,64,256]{3,2,1,0:T(8,128)S(1)}, u32[]{:S(2)}, u32[]{:S(2)}) collective-permute-start(f32[2,4,64,256]{3,2,1,0:T(8,128)S(1)} %get-tuple-element.62), channel_id=1, source_target_pairs={{1,2},{2,1},{3,4},{4,3},{5,6},{6,5},{7,8},{8,7},{9,10},{10,9},{11,... | collective-permute-start | bytes 1572872 | tf_op jit(solution)/shard_map/ppermute | solution.py:441
  49.2 18.9 %collective-permute-start.11 = (f32[2,4,64,256]{3,2,1,0:T(8,128)S(1)}, f32[2,4,64,256]{3,2,1,0:T(8,128)S(1)}, u32[]{:S(2)}, u32[]{:S(2)}) collective-permute-start(f32[2,4,64,256]{3,2,1,0:T(8,128)S(1)} %get-tuple-element.62), channel_id=1, source_target_pairs={{0,1},{1,0},{2,3},{3,2},{4,5},{5,4},{6,7},{7,6},{8,9},{9,8},{10,11... | collective-permute-start | bytes 1572872 | tf_op jit(solution)/shard_map/ppermute | solution.py:441
  63.6 6.9 %collective-permute-start.16 = (f32[4,64,256]{2,1,0:T(8,128)S(1)}, f32[4,64,256]{2,1,0:T(8,128)S(1)}, u32[]{:S(2)}, u32[]{:S(2)}) collective-permute-start(f32[4,64,256]{2,1,0:T(8,128)S(1)} %bitcast.31), channel_id=1, source_target_pairs={{0,16},{16,0},{1,17},{17,1},{2,18},{18,2},{3,19},{19,3},{4,20},{20... | collective-permute-start | bytes 786440 | tf_op jit(solution)/shard_map/ppermute | solution.py:450
  69.2 6.4 %collective-permute-start.13 = (f32[4,64,256]{2,1,0:T(8,128)S(1)}, f32[4,64,256]{2,1,0:T(8,128)S(1)}, u32[]{:S(2)}, u32[]{:S(2)}) collective-permute-start(f32[4,64,256]{2,1,0:T(8,128)S(1)} %bitcast.32), channel_id=1, source_target_pairs={{0,16},{16,0},{1,17},{17,1},{2,18},{18,2},{3,19},{19,3},{4,20},{20... | collective-permute-start | bytes 786440 | tf_op jit(solution)/shard_map/ppermute | solution.py:450
